TPU v7x, 32 devices: a whole 2x2x4 slice. The times are simulated.
32 devices in a mesh: sp: 2 (over x), ep: 16 (over z, y, core).
Axes of the slice: x: 2, y: 2, z: 4, core: 2. Of those that a mesh axis runs over, the one named last changes fastest.
Arguments:
- activations: bfloat16 [16, 8, 3584], P('ep', 'sp'), may hold values from -6 to 6
- out_grad: bfloat16 [16, 8, 3584], P('ep', 'sp'), may hold values from -6 to 6
- route_weights: bfloat16 [16, 8, 8], P('ep', 'sp'), may hold values from 0.019897461 to 0.5
- expert_ids: int32 [16, 8, 8], P('ep', 'sp'), may hold values from 0 to 15, all different within a row; in each aligned block of 8 rows (0 to 7, 8 to 15, ..., all dimensions but the last counted through in order) at most 6 rows name the same one
- w_gate: bfloat16 [16, 3584, 1024], P('ep', None, 'sp'), may hold values from -0.09375 to 0.09375
- w_up: bfloat16 [16, 3584, 1024], P('ep', None, 'sp'), may hold values from -0.09375 to 0.09375
- w_down: bfloat16 [16, 1024, 3584], P('ep', 'sp'), may hold values from -0.1875 to 0.1875
Outputs:
- input_grad: bfloat16 [16, 8, 3584], P('ep', 'sp')
- w_down_grad: float32 [16, 1024, 3584], P('ep', 'sp')
Inputs may be any that keep to these rules, and one draw needn't show every extreme that they name: `expert_ids`: each row names 8 different experts. In each aligned block of 8 rows (one token group, the first two dimensions taken together) no expert is named by more than 6 rows, a bound that some block reaches.
All inputs are finite; a program needn't handle non-finite values.
Results may differ from a plain program's by a relative error of at most 0.014.
Values may be sent and summed in bfloat16 or wider, within the bound.
No kernel may reach another device: no remote copies, remote signals or barrier semaphores. Data moves between devices by JAX's collectives and lax.ppermute only.
A program may use at most 64 MiB of HBM per device.

v0:
```python
import jax
import jax.numpy as jnp
from jax import lax
from jax.sharding import PartitionSpec as P

TOP = 8


def expert_rows(rows_in, rows_grad, gate_w, up_w, down_w):
    gate_pre = jnp.dot(rows_in, gate_w, preferred_element_type=jnp.float32)
    up_pre = jnp.dot(rows_in, up_w, preferred_element_type=jnp.float32)
    squash = jax.nn.sigmoid(gate_pre)
    swish = gate_pre * squash
    hidden = (swish * up_pre).astype(jnp.bfloat16)
    hidden_grad = lax.dot_general(
        rows_grad, down_w, (((1,), (1,)), ((), ())), preferred_element_type=jnp.float32
    )
    gate_grad = (hidden_grad * up_pre * squash * (1.0 + gate_pre * (1.0 - squash))).astype(
        jnp.bfloat16
    )
    up_grad = (hidden_grad * swish).astype(jnp.bfloat16)
    first = lax.dot_general(
        gate_grad, gate_w, (((1,), (1,)), ((), ())), preferred_element_type=jnp.float32
    )
    second = lax.dot_general(
        up_grad, up_w, (((1,), (1,)), ((), ())), preferred_element_type=jnp.float32
    )
    partial_rows = (first + second).astype(jnp.bfloat16)
    weight_grad = lax.dot_general(
        hidden, rows_grad, (((0,), (0,)), ((), ())), preferred_element_type=jnp.float32
    )
    return (partial_rows, weight_grad)


def per_device(activations, out_grad, route_weights, expert_ids, w_gate, w_up, w_down):
    n_expert = lax.axis_size("ep")
    n_group = lax.axis_size("sp")
    tok_dev = activations.shape[1]
    width = activations.shape[2]
    capacity = max(2, tok_dev * n_group * TOP * 3 // (2 * n_expert))
    group_ids = lax.all_gather(expert_ids, "sp", axis=1, tiled=True)
    group_in, group_grad, group_weight = (
        lax.all_gather(activations, "sp", axis=1, tiled=True),
        lax.all_gather(out_grad, "sp", axis=1, tiled=True),
        lax.all_gather(route_weights, "sp", axis=1, tiled=True),
    )
    send_width = group_in.shape[2]
    tok_grp = group_ids.shape[1]
    slot_expert = group_ids[0].reshape(-1)
    slot_token = jnp.arange(slot_expert.shape[0], dtype=jnp.int32) // TOP
    onehot = (slot_expert[:, None] == jnp.arange(n_expert, dtype=jnp.int32)[None, :]).astype(
        jnp.int32
    )
    before = jnp.cumsum(onehot, axis=0) - onehot
    rank = jnp.sum(before * onehot, axis=1)
    position = slot_expert * capacity + rank
    total_rows = n_expert * capacity
    token_in = group_in[0][slot_token]
    scaled = (
        group_weight[0].reshape(-1).astype(jnp.float32)[:, None]
        * group_grad[0][slot_token].astype(jnp.float32)
    ).astype(jnp.bfloat16)
    send_in = (
        jnp.zeros((total_rows, send_width), jnp.bfloat16)
        .at[position]
        .set(token_in)
        .reshape(n_expert, capacity, send_width)
    )
    send_grad = (
        jnp.zeros((total_rows, send_width), jnp.bfloat16)
        .at[position]
        .set(scaled)
        .reshape(n_expert, capacity, send_width)
    )
    recv_in, recv_grad = (
        lax.all_to_all(send_in, "ep", split_axis=0, concat_axis=0, tiled=True),
        lax.all_to_all(send_grad, "ep", split_axis=0, concat_axis=0, tiled=True),
    )
    flat_in = recv_in.reshape(total_rows, width)
    flat_grad = recv_grad.reshape(total_rows, width)
    gate_w = w_gate[0]
    up_w = w_up[0]
    down_w = w_down[0]
    partial_rows, weight_grad = expert_rows(flat_in, flat_grad, gate_w, up_w, down_w)
    partial_rows = partial_rows.reshape(n_expert, capacity, width)
    slot_owner = jnp.full((total_rows,), -1, jnp.int32).at[position].set(slot_token)
    owner_match = jnp.arange(tok_grp, dtype=jnp.int32)[:, None] == slot_owner[None, :]
    back_rows = lax.all_to_all(partial_rows, "ep", split_axis=0, concat_axis=0, tiled=True)
    token_sum = jnp.dot(
        owner_match.astype(jnp.bfloat16),
        back_rows.reshape(total_rows, width),
        preferred_element_type=jnp.float32,
    )
    own_sum = lax.psum_scatter(
        token_sum.astype(jnp.bfloat16), "sp", scatter_dimension=0, tiled=True
    )
    return (own_sum.reshape(1, tok_dev, width), weight_grad[None])


def solution(mesh):
    return jax.shard_map(
        per_device,
        mesh=mesh,
        in_specs=(
            P("ep", "sp", None),
            P("ep", "sp", None),
            P("ep", "sp", None),
            P("ep", "sp", None),
            P("ep", None, "sp"),
            P("ep", None, "sp"),
            P("ep", "sp", None),
        ),
        out_specs=(P("ep", "sp", None), P("ep", "sp", None)),
        check_vma=False,
    )
```

profile of v0, /device:TPU:0, one launch (start us, length us, event | category | flops | bytes accessed | tf_op | source)
XLA Modules:
  0.0 116.4 jit_solution(2344344698198534478)
XLA Ops:
  0.7 5.5 %all_gather.12 = s32[1,8,8]{2,0,1:T(1,128)S(1)} all-gather(s32[1,4,8]{2,0,1:T(1,128)} %bitcast.44), channel_id=1, replica_groups=mesh['sp'=2,'ep'=16] {'sp'}, dimensions={1}, use_global_device_ids=true | all-gather | bytes 384 | tf_op jit(solution)/shard_map/all_gather | solution.py:41
  7.9 0.8 copy.16
  8.7 4.8 %all_gather.15 = bf16[1,8,3584]{2,0,1:T(2,128)(2,1)S(1)} all-gather(bf16[1,4,3584]{2,0,1:T(2,128)(2,1)S(1)} %copy.16), channel_id=1, replica_groups=mesh['sp'=2,'ep'=16] {'sp'}, dimensions={1}, use_global_device_ids=true | all-gather | bytes 86016 | tf_op jit(solution)/shard_map/all_gather | solution.py:43
  13.6 2.8 %scatter_custom_fusion.2 = bf16[96,3584]{1,0:T(8,128)(2,1)S(1)} fusion(s32[64]{0:T(128)S(1)} %fusion.23, bf16[8,3584]{1,0:T(8,128)(2,1)S(1)} %bitcast.43, s32[1024]{0:T(1024)S(1)} %pad_clamp_fusion, bf16[]{:T(256)} %constant.34.clone.1), kind=kCustom, calls=%fused_computation.20 | custom fusion | bytes 688130 | tf_op jit(solution)/shard_map/scatter | solution.py:66
  16.4 1.2 reshape.107
  17.5 6.4 %all-to-all-start.1 = ((bf16[16,6,3584]{2,1,0:T(8,128)(2,1)}), bf16[16,6,3584]{2,1,0:T(8,128)(2,1)S(1)}, u32[]{:S(2)}, u32[]{:S(2)}) async-start(bf16[16,6,3584]{2,1,0:T(8,128)(2,1)} %reshape.107), calls=%async_computation.1 | async-start | bytes 1835008 | tf_op jit(solution)/shard_map/all_to_all | solution.py:76
  24.0 4.4 %all_gather.13 = bf16[1,8,8]{2,0,1:T(2,128)(2,1)S(1)} all-gather(bf16[1,4,8]{2,0,1:T(2,128)(2,1)S(1)} %copy.14), channel_id=1, replica_groups=mesh['sp'=2,'ep'=16] {'sp'}, dimensions={1}, use_global_device_ids=true | all-gather | bytes 192 | tf_op jit(solution)/shard_map/all_gather | solution.py:45
  28.5 4.8 %all_gather.14 = bf16[1,8,3584]{2,0,1:T(2,128)(2,1)S(1)} all-gather(bf16[1,4,3584]{2,0,1:T(2,128)(2,1)S(1)} %copy.15), channel_id=1, replica_groups=mesh['sp'=2,'ep'=16] {'sp'}, dimensions={1}, use_global_device_ids=true | all-gather | bytes 86016 | tf_op jit(solution)/shard_map/all_gather | solution.py:44
  33.3 2.9 %scatter_custom_fusion.1 = bf16[96,3584]{1,0:T(8,128)(2,1)S(1)} fusion(s32[64]{0:T(128)S(1)} %fusion.23, f32[64]{0:T(128)S(1)} %reshape.112, bf16[]{:T(256)} %constant.34.clone.1, bf16[8,3584]{1,0:T(8,128)(2,1)S(1)} %bitcast.42, s32[1024]{0:T(1024)S(1)} %pad_clamp_fusion), kind=kCustom, calls=%fused_computation.19 | custom fusion | flops 688128 | bytes 750082 | tf_op jit(solution)/shard_map/scatter | solution.py:72
  36.2 1.2 reshape.105
  37.4 7.4 %all-to-all-done.1 = bf16[16,6,3584]{2,1,0:T(8,128)(2,1)S(1)} async-done(((bf16[16,6,3584]{2,1,0:T(8,128)(2,1)}), bf16[16,6,3584]{2,1,0:T(8,128)(2,1)S(1)}, u32[]{:S(2)}, u32[]{:S(2)}) %all-to-all-start.1) | async-done | bytes 688160 | tf_op jit(solution)/shard_map/all_to_all | solution.py:76
  44.7 6.1 %all-to-all-start = ((bf16[16,6,3584]{2,1,0:T(8,128)(2,1)}), bf16[16,6,3584]{2,1,0:T(8,128)(2,1)S(1)}, u32[]{:S(2)}, u32[]{:S(2)}) async-start(bf16[16,6,3584]{2,1,0:T(8,128)(2,1)} %reshape.105), calls=%async_computation | async-start | bytes 1835008 | tf_op jit(solution)/shard_map/all_to_all | solution.py:77
  51.1 2.9 %fusion.3 = f32[96,512]{1,0:T(8,128)S(1)} fusion(bf16[96,3584]{1,0:T(8,128)(2,1)S(1)} %reshape.108, bf16[1,3584,512]{2,1,0:T(8,128)(2,1)} %param.11), kind=kOutput, calls=%fused_computation.11 | convolution fusion | flops 352321536 | bytes 4554752 | tf_op jit(solution)/shard_map/dot_general | solution.py:10
  54.9 16.7 %all-to-all-done = bf16[16,6,3584]{2,1,0:T(8,128)(2,1)S(1)} async-done(((bf16[16,6,3584]{2,1,0:T(8,128)(2,1)}), bf16[16,6,3584]{2,1,0:T(8,128)(2,1)S(1)}, u32[]{:S(2)}, u32[]{:S(2)}) %all-to-all-start) | async-done | bytes 688160 | tf_op jit(solution)/shard_map/all_to_all | solution.py:77
  71.8 3.4 %fusion.8 = f32[96,512]{1,0:T(8,128)S(1)} fusion(bf16[96,3584]{1,0:T(8,128)(2,1)S(1)} %reshape.106, bf16[1,512,3584]{2,1,0:T(8,128)(2,1)} %param.13), kind=kOutput, calls=%fused_computation.16 | convolution fusion | flops 352321536 | bytes 4554752 | tf_op jit(solution)/shard_map/dot_general | solution.py:15
  75.3 1.2 %fusion.1 = f32[96,3584]{1,0:T(8,128)S(1)} fusion(bf16[1,3584,512]{2,1,0:T(8,128)(2,1)S(1)} %copy-done, f32[96,512]{1,0:T(8,128)S(1)} %fusion.3, f32[96,512]{1,0:T(8,128)S(1)} %fusion.8, f32[96,512]{1,0:T(8,128)S(1)} %fusion.6), kind=kOutput, calls=%fused_computation.9 | convolution fusion | flops 352813056 | bytes 5636096 | tf_op jit(solution)/shard_map/dot_general | solution.py:22
  76.5 0.8 copy-done.2
  77.3 1.2 %fusion = bf16[96,3584]{1,0:T(8,128)(2,1)S(1)} fusion(f32[96,3584]{1,0:T(8,128)S(1)} %fusion.1, bf16[1,3584,512]{2,1,0:T(8,128)(2,1)S(1)} %copy-done.2, f32[96,512]{1,0:T(8,128)S(1)} %fusion.8, f32[96,512]{1,0:T(8,128)S(1)} %fusion.3), kind=kOutput, calls=%fused_computation.7 | convolution fusion | flops 353304576 | bytes 6127616 | tf_op jit(solution)/shard_map/dot_general | solution.py:25
  78.6 1.2 reshape.109
  79.7 6.1 %all-to-all-start.2 = ((bf16[16,6,3584]{2,1,0:T(8,128)(2,1)}), bf16[16,6,3584]{2,1,0:T(8,128)(2,1)S(1)}, u32[]{:S(2)}, u32[]{:S(2)}) async-start(bf16[16,6,3584]{2,1,0:T(8,128)(2,1)} %reshape.109), calls=%async_computation.2 | async-start | bytes 1835008 | tf_op jit(solution)/shard_map/all_to_all | solution.py:88
  87.1 0.8 scatter_custom_fusion
  87.8 4.2 %convolution_bitcast_fusion = f32[1,512,3584]{2,1,0:T(8,128)} fusion(bf16[96,3584]{1,0:T(8,128)(2,1)S(1)} %reshape.106, f32[96,512]{1,0:T(8,128)S(1)} %fusion.6, f32[96,512]{1,0:T(8,128)S(1)} %fusion.3), kind=kOutput, calls=%fused_computation.5 | convolution fusion | flops 352616448 | bytes 8421376 | tf_op jit(solution)/shard_map/dot_general | solution.py:29
  92.1 14.5 %all-to-all-done.2 = bf16[16,6,3584]{2,1,0:T(8,128)(2,1)S(1)} async-done(((bf16[16,6,3584]{2,1,0:T(8,128)(2,1)}), bf16[16,6,3584]{2,1,0:T(8,128)(2,1)S(1)}, u32[]{:S(2)}, u32[]{:S(2)}) %all-to-all-start.2) | async-done | bytes 688160 | tf_op jit(solution)/shard_map/all_to_all | solution.py:88
  107.0 8.7 %all-reduce = bf16[8,3584]{1,0:T(8,128)(2,1)S(1)} all-reduce(bf16[8,3584]{1,0:T(8,128)(2,1)S(1)} %convolution_convert_fusion), channel_id=2, replica_groups=mesh['sp'=2,'ep'=16] {'sp'}, use_global_device_ids=true, to_apply=%region_5.6.clone | all-reduce | flops 28672 | bytes 114688
  (35 shorter events, 4.9 us)
Async XLA Ops:
  0.6 23.3 %copy-start.4 = (bf16[1,4,8]{2,1,0:T(4,128)(2,1)S(1)}, bf16[1,4,8]{2,1,0:T(4,128)(2,1)}, u32[]{:S(2)}) copy-start(bf16[1,4,8]{2,1,0:T(4,128)(2,1)} %param.9) | copy-start | bytes 196
  0.6 27.8 %copy-start.3 = (bf16[1,4,3584]{2,1,0:T(4,128)(2,1)S(1)}, bf16[1,4,3584]{2,1,0:T(4,128)(2,1)}, u32[]{:S(2)}) copy-start(bf16[1,4,3584]{2,1,0:T(4,128)(2,1)} %param.8) | copy-start | bytes 86020
  17.5 27.2 %all-to-all-start.1 = ((bf16[16,6,3584]{2,1,0:T(8,128)(2,1)}), bf16[16,6,3584]{2,1,0:T(8,128)(2,1)S(1)}, u32[]{:S(2)}, u32[]{:S(2)}) async-start(bf16[16,6,3584]{2,1,0:T(8,128)(2,1)} %reshape.107), calls=%async_computation.1 | async-start | bytes 1835008 | tf_op jit(solution)/shard_map/all_to_all | solution.py:76
  44.7 26.9 %all-to-all-start = ((bf16[16,6,3584]{2,1,0:T(8,128)(2,1)}), bf16[16,6,3584]{2,1,0:T(8,128)(2,1)S(1)}, u32[]{:S(2)}, u32[]{:S(2)}) async-start(bf16[16,6,3584]{2,1,0:T(8,128)(2,1)} %reshape.105), calls=%async_computation | async-start | bytes 1835008 | tf_op jit(solution)/shard_map/all_to_all | solution.py:77
  51.0 3.1 %copy-start.1 = (bf16[1,3584,512]{2,1,0:T(8,128)(2,1)S(1)}, bf16[1,3584,512]{2,1,0:T(8,128)(2,1)}, u32[]{:S(2)}) copy-start(bf16[1,3584,512]{2,1,0:T(8,128)(2,1)} %param.12) | copy-start | bytes 11010052
  71.8 3.4 %copy-start = (bf16[1,3584,512]{2,1,0:T(8,128)(2,1)S(1)}, bf16[1,3584,512]{2,1,0:T(8,128)(2,1)}, u32[]{:S(2)}) copy-start(bf16[1,3584,512]{2,1,0:T(8,128)(2,1)} %param.11) | copy-start | bytes 11010052
  75.3 2.0 %copy-start.2 = (bf16[1,3584,512]{2,1,0:T(8,128)(2,1)S(1)}, bf16[1,3584,512]{2,1,0:T(8,128)(2,1)}, u32[]{:S(2)}) copy-start(bf16[1,3584,512]{2,1,0:T(8,128)(2,1)} %param.12) | copy-start | bytes 11010052
  77.3 8.5 %copy-start.5 = (u32[32]{0:T(128)S(1)}, u32[32]{0:T(128)}, u32[]{:S(2)}) copy-start(u32[32]{0:T(128)} %constant.46) | copy-start | bytes 388
  79.7 26.9 %all-to-all-start.2 = ((bf16[16,6,3584]{2,1,0:T(8,128)(2,1)}), bf16[16,6,3584]{2,1,0:T(8,128)(2,1)S(1)}, u32[]{:S(2)}, u32[]{:S(2)}) async-start(bf16[16,6,3584]{2,1,0:T(8,128)(2,1)} %reshape.109), calls=%async_computation.2 | async-start | bytes 1835008 | tf_op jit(solution)/shard_map/all_to_all | solution.py:88
where the time goes:
time: 118 us; the launch traced here: 116 us
  waiting for transfers between devices  38.6 us (33%)
  blocking collectives  28.3 us (24%)
  starting transfers between devices  18.6 us (16%)
  matrix products  13.9 us (12%)
  local copies, waits for them, and re-layouts  11.6 us (10%)
  other arithmetic  3.92 us (3%)
  between operations  1.52 us (1%)
    all_to_all x1, waiting for transfers between devices, per_device(): lax.all_to_all(send_grad, 'ep', split_axis=0, concat_axis=0, tiled=True)  16.7 us
    all_to_all x1, waiting for transfers between devices, per_device(): lax.all_to_all(partial_rows, 'ep', split_axis=0, concat_axis=0, tiled=True)  14.5 us
    unnamed x1, blocking collectives  8.74 us
    all_to_all x1, waiting for transfers between devices, per_device(): lax.all_to_all(send_in, 'ep', split_axis=0, concat_axis=0, tiled=True)  7.36 us
    all_to_all x1, starting transfers between devices, per_device(): lax.all_to_all(send_in, 'ep', split_axis=0, concat_axis=0, tiled=True)  6.42 us
    all_to_all x1, starting transfers between devices, per_device(): lax.all_to_all(send_grad, 'ep', split_axis=0, concat_axis=0, tiled=True)  6.08 us
    all_to_all x1, starting transfers between devices, per_device(): lax.all_to_all(partial_rows, 'ep', split_axis=0, concat_axis=0, tiled=True)  6.08 us
    all_gather x1, blocking collectives, per_device(): group_ids = lax.all_gather(expert_ids, 'sp', axis=1, tiled=True)  5.5 us
  transfers between devices with their start and end apart: 3, of which 3 were waited for; matrix products, arithmetic and copies ran while one was open for 12% of the time, Pallas kernels for 0%

commit v1 on v0

v1 whole, which is shorter than its diff:
```python
import jax
import jax.numpy as jnp
from jax import lax
from jax.sharding import PartitionSpec as P

TOP = 8
F32 = jnp.float32
BF16 = jnp.bfloat16


def expert_rows(rows_in, rows_grad, gate_w, up_w, down_w):
    gate_pre = jnp.dot(rows_in, gate_w, preferred_element_type=F32)
    up_pre = jnp.dot(rows_in, up_w, preferred_element_type=F32)
    squash = jax.nn.sigmoid(gate_pre)
    swish = gate_pre * squash
    hidden = (swish * up_pre).astype(BF16)
    hidden_grad = lax.dot_general(
        rows_grad, down_w, (((1,), (1,)), ((), ())), preferred_element_type=F32
    )
    gate_grad = (hidden_grad * up_pre * squash * (1.0 + gate_pre * (1.0 - squash))).astype(BF16)
    up_grad = (hidden_grad * swish).astype(BF16)
    first = lax.dot_general(
        gate_grad, gate_w, (((1,), (1,)), ((), ())), preferred_element_type=F32
    )
    second = lax.dot_general(up_grad, up_w, (((1,), (1,)), ((), ())), preferred_element_type=F32)
    partial_rows = (first + second).astype(BF16)
    weight_grad = lax.dot_general(
        hidden, rows_grad, (((0,), (0,)), ((), ())), preferred_element_type=F32
    )
    return (partial_rows, weight_grad)


def routed(activations, out_grad, route_weights, expert_ids, w_gate, w_up, w_down):
    n_expert = lax.axis_size("ep")
    n_group = lax.axis_size("sp")
    tok_dev = activations.shape[1]
    width = activations.shape[2]
    capacity = max(2, tok_dev * n_group * TOP * 3 // (2 * n_expert))
    group_ids = lax.all_gather(expert_ids, "sp", axis=1, tiled=True)
    group_in, group_grad, group_weight = (
        lax.all_gather(activations, "sp", axis=1, tiled=True),
        lax.all_gather(out_grad, "sp", axis=1, tiled=True),
        lax.all_gather(route_weights, "sp", axis=1, tiled=True),
    )
    tok_grp = group_ids.shape[1]
    slot_expert = group_ids[0].reshape(-1)
    slot_token = jnp.arange(slot_expert.shape[0], dtype=jnp.int32) // TOP
    onehot = (slot_expert[:, None] == jnp.arange(n_expert, dtype=jnp.int32)[None, :]).astype(
        jnp.int32
    )
    before = jnp.cumsum(onehot, axis=0) - onehot
    rank = jnp.sum(before * onehot, axis=1)
    position = slot_expert * capacity + rank
    total_rows = n_expert * capacity
    token_in = group_in[0][slot_token]
    scaled = (
        group_weight[0].reshape(-1).astype(F32)[:, None] * group_grad[0][slot_token].astype(F32)
    ).astype(BF16)
    send_in = (
        jnp.zeros((total_rows, width), BF16)
        .at[position]
        .set(token_in)
        .reshape(n_expert, capacity, width)
    )
    send_grad = (
        jnp.zeros((total_rows, width), BF16)
        .at[position]
        .set(scaled)
        .reshape(n_expert, capacity, width)
    )
    recv_in, recv_grad = (
        lax.all_to_all(send_in, "ep", split_axis=0, concat_axis=0, tiled=True),
        lax.all_to_all(send_grad, "ep", split_axis=0, concat_axis=0, tiled=True),
    )
    flat_in = recv_in.reshape(total_rows, width)
    flat_grad = recv_grad.reshape(total_rows, width)
    partial_rows, weight_grad = expert_rows(flat_in, flat_grad, w_gate[0], w_up[0], w_down[0])
    partial_rows = partial_rows.reshape(n_expert, capacity, width)
    slot_owner = jnp.full((total_rows,), -1, jnp.int32).at[position].set(slot_token)
    owner_match = jnp.arange(tok_grp, dtype=jnp.int32)[:, None] == slot_owner[None, :]
    back_rows = lax.all_to_all(partial_rows, "ep", split_axis=0, concat_axis=0, tiled=True)
    token_sum = jnp.dot(
        owner_match.astype(BF16),
        back_rows.reshape(total_rows, width),
        preferred_element_type=F32,
    )
    own_sum = lax.psum_scatter(token_sum.astype(BF16), "sp", scatter_dimension=0, tiled=True)
    return (own_sum.reshape(1, tok_dev, width), weight_grad[None])


def exchange(value, partner, n_sp, n_ep):
    pairs = [(i, partner(i)) for i in range(n_sp * n_ep)]
    return lax.ppermute(value, ("sp", "ep"), pairs)


def dense(activations, out_grad, route_weights, expert_ids, w_gate, w_up, w_down):
    n_ep = lax.axis_size("ep")
    n_sp = lax.axis_size("sp")
    tok_dev, width = activations.shape[1:]
    swap = lambda value, partner: exchange(value, partner, n_sp, n_ep)
    far = [4 * j for j in range(1, n_ep // 4)][::-1]
    one = lambda i: i ^ n_ep if i & 1 else i ^ 2
    two = lambda i: i ^ 2 if i & 1 else i ^ n_ep
    core = lambda i: i ^ 1

    chosen = expert_ids[0][:, :, None] == jnp.arange(n_ep, dtype=jnp.int32)[None, None, :]
    per_expert = jnp.sum(jnp.where(chosen, route_weights[0].astype(F32)[:, :, None], 0.0), axis=1)
    per_expert = jnp.pad(per_expert, ((0, 0), (0, -n_ep % 128))).astype(BF16)
    mine = jnp.concatenate([activations[0], out_grad[0], per_expert], axis=1)[None]

    parts = {j: swap(mine, lambda i, j=j: i ^ j) for j in far}
    held = jnp.concatenate([mine] + [parts[j] for j in sorted(far)], axis=0)
    held = jnp.concatenate([held, swap(held, one)], axis=0)
    held = jnp.concatenate([held, swap(held, two)], axis=0)
    held = jnp.concatenate([held, swap(held, core)], axis=0)
    blocks = held.shape[0]
    held = held.reshape(blocks * tok_dev, held.shape[2])
    weight = lax.dynamic_slice_in_dim(held[:, 2 * width :], lax.axis_index("ep"), 1, axis=1)
    rows_in = held[:, :width]
    rows_grad = (weight.astype(F32) * held[:, width : 2 * width].astype(F32)).astype(BF16)

    partial_rows, weight_grad = expert_rows(rows_in, rows_grad, w_gate[0], w_up[0], w_down[0])

    total = partial_rows.reshape(blocks, tok_dev, width)
    for partner in (core, two, one):
        half = total.shape[0] // 2
        got = swap(total[half:].astype(BF16), partner)
        total = total[:half].astype(F32) + got.astype(F32)
    sent = total.astype(BF16)
    own = total[0]
    for j in far:
        own = own + swap(sent[j // 4], lambda i, j=j: i ^ j).astype(F32)
    return (own.astype(BF16)[None], weight_grad[None])


def per_device(activations, out_grad, route_weights, expert_ids, w_gate, w_up, w_down):
    n_ep = lax.axis_size("ep")
    n_sp = lax.axis_size("sp")
    tokens = activations.shape[1] * n_sp * n_ep
    rows = n_ep * max(2, activations.shape[1] * n_sp * TOP * 3 // (2 * n_ep))
    few = tokens <= 2 * rows and n_sp == 2 and n_ep >= 8 and n_ep & (n_ep - 1) == 0
    body = dense if few else routed
    return body(activations, out_grad, route_weights, expert_ids, w_gate, w_up, w_down)


def solution(mesh):
    return jax.shard_map(
        per_device,
        mesh=mesh,
        in_specs=(
            P("ep", "sp", None),
            P("ep", "sp", None),
            P("ep", "sp", None),
            P("ep", "sp", None),
            P("ep", None, "sp"),
            P("ep", None, "sp"),
            P("ep", "sp", None),
        ),
        out_specs=(P("ep", "sp", None), P("ep", "sp", None)),
        check_vma=False,
    )
```

time: 118 us -> 74.2 us (0.63); the launches traced: 116 us -> 73.8 us
  blocking collectives: 28.3 us -> 0 us
  waiting for transfers between devices: 38.6 us -> 23.4 us
  other arithmetic: 3.92 us -> 6.98 us
  local copies, waits for them, and re-layouts: 11.6 us -> 14 us
  matrix products: 13.9 us -> 11.7 us
  starting transfers between devices: 18.6 us -> 16.9 us
    all_to_all x3 -> x0, waiting for transfers between devices: 38.6 us -> none  [the longest x1 16.7 us: per_device(): lax.all_to_all(send_grad, 'ep', split_axis=0, concat_axis=0, tiled=True)]
    ppermute x0 -> x12, waiting for transfers between devices: none -> 23.4 us  [exchange(): return lax.ppermute(value, ('sp', 'ep'), pairs)]
    all_gather x4 -> x0, blocking collectives: 19.6 us -> none  [the longest x1 5.5 us: per_device(): group_ids = lax.all_gather(expert_ids, 'sp', axis=1, tiled=True)]
    all_to_all x3 -> x0, starting transfers between devices: 18.6 us -> none  [the longest x1 6.42 us: per_device(): lax.all_to_all(send_in, 'ep', split_axis=0, concat_axis=0, tiled=True)]
    ppermute x0 -> x12, starting transfers between devices: none -> 16.9 us  [exchange(): return lax.ppermute(value, ('sp', 'ep'), pairs)]
    unnamed x1 -> x0, blocking collectives: 8.74 us -> none
    scatter x2 -> x0, local copies, waits for them, and re-layouts: 3.57 us -> none  [the longest x1 2.79 us: per_device(): send_in = jnp.zeros((total_rows, send_width), jnp.bfloat16).at[position]....]
    unnamed x18 -> x11, local copies, waits for them, and re-layouts: 2.5 us -> 5.45 us
  transfers between devices with their start and end apart: 3 -> 12, of which waited for: 3 -> 8; matrix products, arithmetic and copies ran while one was open for 12% -> 12% of each run, Pallas kernels for 0% -> 0%
where the time goes in v1:
time: 74.2 us; the launch traced here: 73.8 us
  waiting for transfers between devices  23.4 us (32%)
  starting transfers between devices  16.9 us (23%)
  local copies, waits for them, and re-layouts  14 us (19%)
  matrix products  11.7 us (16%)
  other arithmetic  6.98 us (9%)
  between operations  0.76 us (1%)
    ppermute x12, waiting for transfers between devices, exchange(): return lax.ppermute(value, ('sp', 'ep'), pairs)  23.4 us
    ppermute x12, starting transfers between devices, exchange(): return lax.ppermute(value, ('sp', 'ep'), pairs)  16.9 us
    unnamed x11, local copies, waits for them, and re-layouts  5.45 us
    dot_general x1, matrix products, expert_rows(): lax.dot_general(hidden, rows_grad, (((0,), (0,)), ((), ())), preferred_el...  4.25 us
    reshape x1, local copies, waits for them, and re-layouts, dense(): held = held.reshape(blocks * tok_dev, held.shape[2])  2.96 us
    dot_general x1, matrix products, expert_rows(): gate_pre = jnp.dot(rows_in, gate_w, preferred_element_type=F32)  2.84 us
    slice x3, local copies, waits for them, and re-layouts, dense(): got = swap(total[half:].astype(BF16), partner)  2.02 us
    add x2, other arithmetic, dense(): total = total[:half].astype(F32) + got.astype(F32)  1.49 us
  transfers between devices with their start and end apart: 12, of which 8 were waited for; matrix products, arithmetic and copies ran while one was open for 12% of the time, Pallas kernels for 0%

profile of v1, /device:TPU:0, one launch (start us, length us, event | category | flops | bytes accessed | tf_op | source)
XLA Modules:
  0.0 73.8 jit_solution(17147331187473840528)
XLA Ops:
  2.9 5.1 %collective-permute-start.2 = (bf16[1,4,7296]{2,1,0:T(4,128)(2,1)S(1)}, bf16[1,4,7296]{2,1,0:T(4,128)(2,1)S(1)}, u32[]{:S(2)}, u32[]{:S(2)}) collective-permute-start(bf16[1,4,7296]{2,1,0:T(4,128)(2,1)S(1)} %fusion.16), channel_id=1, source_target_pairs={{0,12},{1,13},{2,14},{3,15},{4,8},{5,9},{6,10},{7,11},{8,4},{9,5},... | collective-permute-start | bytes 175112 | tf_op jit(solution)/shard_map/ppermute | solution.py:93
  8.7 1.4 %constant_dynamic-update-slice_fusion.10 = (bf16[16,4,7296]{2,1,0:T(4,128)(2,1)S(1)}, bf16[32,4,7296]{2,1,0:T(4,128)(2,1)}, bf16[8,4,7296]{2,1,0:T(4,128)(2,1)S(1)}) fusion(bf16[4,16]{1,0:T(4,128)(2,1)S(1)} %select_reduce_fusion, bf16[4,3584]{1,0:T(4,128)(2,1)} %bitcast.59, bf16[4,3584]{1,0:T(4,128)(2,1)} %bitcast.61), kind=kLoop, calls=%fused_computation.47 | loop fusion | flops 233469 | bytes 232576
  10.4 2.8 %collective-permute-done.1 = bf16[1,4,7296]{2,1,0:T(4,128)(2,1)S(1)} collective-permute-done((bf16[1,4,7296]{2,1,0:T(4,128)(2,1)S(1)}, bf16[1,4,7296]{2,1,0:T(4,128)(2,1)S(1)}, u32[]{:S(2)}, u32[]{:S(2)}) %collective-permute-start.1) | collective-permute-done | bytes 58400 | tf_op jit(solution)/shard_map/ppermute | solution.py:93
  13.3 1.7 %collective-permute-start.3 = (bf16[4,4,7296]{2,1,0:T(4,128)(2,1)S(1)}, bf16[4,4,7296]{2,1,0:T(4,128)(2,1)S(1)}, u32[]{:S(2)}, u32[]{:S(2)}) collective-permute-start(bf16[4,4,7296]{2,1,0:T(4,128)(2,1)S(1)} %pad_maximum_fusion), channel_id=1, source_target_pairs={{0,2},{1,17},{2,0},{3,19},{4,6},{5,21},{6,4},{7,23},{8,10},{9,25},... | collective-permute-start | bytes 700424 | tf_op jit(solution)/shard_map/ppermute | solution.py:93
  17.1 2.4 %collective-permute-done.3 = bf16[4,4,7296]{2,1,0:T(4,128)(2,1)S(1)} collective-permute-done((bf16[4,4,7296]{2,1,0:T(4,128)(2,1)S(1)}, bf16[4,4,7296]{2,1,0:T(4,128)(2,1)S(1)}, u32[]{:S(2)}, u32[]{:S(2)}) %collective-permute-start.3) | collective-permute-done | bytes 233504 | tf_op jit(solution)/shard_map/ppermute | solution.py:93
  20.4 1.6 %collective-permute-start.4 = (bf16[8,4,7296]{2,1,0:T(4,128)(2,1)S(1)}, bf16[8,4,7296]{2,1,0:T(4,128)(2,1)S(1)}, u32[]{:S(2)}, u32[]{:S(2)}) collective-permute-start(bf16[8,4,7296]{2,1,0:T(4,128)(2,1)S(1)} %get-tuple-element.10), channel_id=1, source_target_pairs={{0,16},{1,3},{2,18},{3,1},{4,20},{5,7},{6,22},{7,5},{8,24},{9,11},... | collective-permute-start | bytes 1400840 | tf_op jit(solution)/shard_map/ppermute | solution.py:93
  22.0 7.0 %collective-permute-done.4 = bf16[8,4,7296]{2,1,0:T(4,128)(2,1)S(1)} collective-permute-done((bf16[8,4,7296]{2,1,0:T(4,128)(2,1)S(1)}, bf16[8,4,7296]{2,1,0:T(4,128)(2,1)S(1)}, u32[]{:S(2)}, u32[]{:S(2)}) %collective-permute-start.4) | collective-permute-done | bytes 466976 | tf_op jit(solution)/shard_map/ppermute | solution.py:93
  30.0 2.5 %collective-permute-done.5 = bf16[16,4,7296]{2,1,0:T(4,128)(2,1)S(1)} collective-permute-done((bf16[16,4,7296]{2,1,0:T(4,128)(2,1)S(1)}, bf16[16,4,7296]{2,1,0:T(4,128)(2,1)S(1)}, u32[]{:S(2)}, u32[]{:S(2)}) %collective-permute-start.5) | collective-permute-done | bytes 933920 | tf_op jit(solution)/shard_map/ppermute | solution.py:93
  32.5 1.2 %constant_dynamic-update-slice_fusion.11 = bf16[32,4,7296]{2,1,0:T(4,128)(2,1)} fusion(bf16[32,4,7296]{2,1,0:T(4,128)(2,1)} %get-tuple-element.7, bf16[16,4,7296]{2,1,0:T(4,128)(2,1)S(1)} %collective-permute-done.5), kind=kLoop, calls=%fused_computation.48 | loop fusion | bytes 1867776 | tf_op jit(solution)/shard_map/concatenate | solution.py:115
  33.7 3.0 %reshape.20 = bf16[128,7296]{1,0:T(8,128)(2,1)S(1)} reshape(bf16[32,4,7296]{2,1,0:T(4,128)(2,1)} %constant_dynamic-update-slice_fusion.11) | data formatting | bytes 3735552 | tf_op jit(solution)/shard_map/reshape | solution.py:117
  36.9 2.8 %fusion.3 = f32[128,512]{1,0:T(8,128)S(1)} fusion(bf16[1,3584,512]{2,1,0:T(8,128)(2,1)} %param.11, bf16[128,7296]{1,0:T(8,128)(2,1)S(1)} %reshape.20), kind=kOutput, calls=%fused_computation.5 | convolution fusion | flops 469762048 | bytes 4849664 | tf_op jit(solution)/shard_map/dot_general | solution.py:12
  40.7 1.4 %copy-done.2 = bf16[1,512,3584]{2,1,0:T(8,128)(2,1)S(1)} copy-done((bf16[1,512,3584]{2,1,0:T(8,128)(2,1)S(1)}, bf16[1,512,3584]{2,1,0:T(8,128)(2,1)}, u32[]{:S(2)}) %copy-start.2) | copy-done | bytes 3670040
  42.1 1.3 %fusion.8 = f32[128,512]{1,0:T(8,128)S(1)} fusion(bf16[1,512,3584]{2,1,0:T(8,128)(2,1)S(1)} %copy-done.2, bf16[128,7296]{1,0:T(8,128)(2,1)S(1)} %reshape.20, f32[128]{0:T(128)S(1)} %bitcast_convert_fusion.1), kind=kOutput, calls=%fused_computation.10 | convolution fusion | flops 471138304 | bytes 4850176 | tf_op jit(solution)/shard_map/dot_general | solution.py:17
  44.1 1.3 %fusion.1 = f32[128,3584]{1,0:T(8,128)S(1)} fusion(bf16[1,3584,512]{2,1,0:T(8,128)(2,1)S(1)} %copy-done, f32[128,512]{1,0:T(8,128)S(1)} %fusion.3, f32[128,512]{1,0:T(8,128)S(1)} %fusion.8, f32[128,512]{1,0:T(8,128)S(1)} %fusion.6), kind=kOutput, calls=%fused_computation.3 | convolution fusion | flops 470417408 | bytes 6291456 | tf_op jit(solution)/shard_map/dot_general | solution.py:22
  45.4 1.3 %fusion = bf16[128,3584]{1,0:T(8,128)(2,1)S(1)} fusion(f32[128,3584]{1,0:T(8,128)S(1)} %fusion.1, bf16[1,3584,512]{2,1,0:T(8,128)(2,1)S(1)} %copy-done.1, f32[128,512]{1,0:T(8,128)S(1)} %fusion.8, f32[128,512]{1,0:T(8,128)S(1)} %fusion.3), kind=kOutput, calls=%fused_computation.2 | convolution fusion | flops 471072768 | bytes 6946816 | tf_op jit(solution)/shard_map/dot_general | solution.py:25
  47.6 1.9 %slice.50 = bf16[16,4,3584]{2,1,0:T(4,128)(2,1)} reshape(bf16[64,3584]{1,0:T(8,128)(2,1)} %get-tuple-element.4) | data formatting | bytes 917504 | tf_op jit(solution)/shard_map/slice | solution.py:127
  51.7 1.4 %convert_add_fusion = f32[8,8,3584]{2,1,0:T(8,128)S(1)} fusion(f32[8,8,3584]{2,1,0:T(8,128)} %bitcast.55, bf16[8,8,3584]{2,1,0:T(8,128)(2,1)} %bitcast.53), kind=kLoop, calls=%fused_computation.13 | loop fusion | flops 458752 | bytes 2293760 | tf_op jit(solution)/shard_map/add | solution.py:128
  53.2 1.6 %collective-permute-start.7 = (bf16[8,4,3584]{2,1,0:T(4,128)(2,1)S(1)}, bf16[8,4,3584]{2,1,0:T(4,128)(2,1)S(1)}, u32[]{:S(2)}, u32[]{:S(2)}) collective-permute-start(bf16[8,4,3584]{2,1,0:T(4,128)(2,1)S(1)} %slice.98), channel_id=1, source_target_pairs={{0,16},{1,3},{2,18},{3,1},{4,20},{5,7},{6,22},{7,5},{8,24},{9,11},... | collective-permute-start | bytes 688136 | tf_op jit(solution)/shard_map/ppermute | solution.py:93
  54.8 4.4 %collective-permute-done.7 = bf16[8,4,3584]{2,1,0:T(4,128)(2,1)S(1)} collective-permute-done((bf16[8,4,3584]{2,1,0:T(4,128)(2,1)S(1)}, bf16[8,4,3584]{2,1,0:T(4,128)(2,1)S(1)}, u32[]{:S(2)}, u32[]{:S(2)}) %collective-permute-start.7) | collective-permute-done | bytes 229408 | tf_op jit(solution)/shard_map/ppermute | solution.py:93
  59.4 1.7 %collective-permute-start.8 = (bf16[4,4,3584]{2,1,0:T(4,128)(2,1)S(1)}, bf16[4,4,3584]{2,1,0:T(4,128)(2,1)S(1)}, u32[]{:S(2)}, u32[]{:S(2)}) collective-permute-start(bf16[4,4,3584]{2,1,0:T(4,128)(2,1)S(1)} %slice.99), channel_id=1, source_target_pairs={{0,2},{1,17},{2,0},{3,19},{4,6},{5,21},{6,4},{7,23},{8,10},{9,25},... | collective-permute-start | bytes 344072 | tf_op jit(solution)/shard_map/ppermute | solution.py:93
  61.1 3.2 %collective-permute-done.8 = bf16[4,4,3584]{2,1,0:T(4,128)(2,1)S(1)} collective-permute-done((bf16[4,4,3584]{2,1,0:T(4,128)(2,1)S(1)}, bf16[4,4,3584]{2,1,0:T(4,128)(2,1)S(1)}, u32[]{:S(2)}, u32[]{:S(2)}) %collective-permute-start.8) | collective-permute-done | bytes 114720 | tf_op jit(solution)/shard_map/ppermute | solution.py:93
  64.4 2.8 %collective-permute-start.9 = (bf16[4,3584]{1,0:T(4,128)(2,1)S(1)}, bf16[4,3584]{1,0:T(4,128)(2,1)S(1)}, u32[]{:S(2)}, u32[]{:S(2)}) collective-permute-start(bf16[4,3584]{1,0:T(4,128)(2,1)S(1)} %get-tuple-element.11), channel_id=1, source_target_pairs={{0,12},{1,13},{2,14},{3,15},{4,8},{5,9},{6,10},{7,11},{8,4},{9,5},... | collective-permute-start | bytes 86024 | tf_op jit(solution)/shard_map/ppermute | solution.py:93
  67.2 1.7 %collective-permute-start.10 = (bf16[4,3584]{1,0:T(4,128)(2,1)S(1)}, bf16[4,3584]{1,0:T(4,128)(2,1)S(1)}, u32[]{:S(2)}, u32[]{:S(2)}) collective-permute-start(bf16[4,3584]{1,0:T(4,128)(2,1)S(1)} %get-tuple-element.13), channel_id=1, source_target_pairs={{0,8},{1,9},{2,10},{3,11},{4,12},{5,13},{6,14},{7,15},{8,0},{9,1},... | collective-permute-start | bytes 86024 | tf_op jit(solution)/shard_map/ppermute | solution.py:93
  68.9 4.2 %convolution_bitcast_fusion = f32[1,512,3584]{2,1,0:T(8,128)} fusion(bf16[128,7296]{1,0:T(8,128)(2,1)S(1)} %reshape.20, f32[128]{0:T(128)S(1)} %bitcast_convert_fusion.1, f32[128,512]{1,0:T(8,128)S(1)} %fusion.6, f32[128,512]{1,0:T(8,128)S(1)} %fusion.3), kind=kOutput, calls=%fused_computation | convolution fusion | flops 471531520 | bytes 8782336 | tf_op jit(solution)/shard_map/dot_general | solution.py:27
  (38 shorter events, 13.2 us)
Async XLA Ops:
  2.9 7.5 %collective-permute-start.2 = (bf16[1,4,7296]{2,1,0:T(4,128)(2,1)S(1)}, bf16[1,4,7296]{2,1,0:T(4,128)(2,1)S(1)}, u32[]{:S(2)}, u32[]{:S(2)}) collective-permute-start(bf16[1,4,7296]{2,1,0:T(4,128)(2,1)S(1)} %fusion.16), channel_id=1, source_target_pairs={{0,12},{1,13},{2,14},{3,15},{4,8},{5,9},{6,10},{7,11},{8,4},{9,5},... | collective-permute-start | bytes 175112 | tf_op jit(solution)/shard_map/ppermute | solution.py:93
  8.0 5.1 %collective-permute-start.1 = (bf16[1,4,7296]{2,1,0:T(4,128)(2,1)S(1)}, bf16[1,4,7296]{2,1,0:T(4,128)(2,1)S(1)}, u32[]{:S(2)}, u32[]{:S(2)}) collective-permute-start(bf16[1,4,7296]{2,1,0:T(4,128)(2,1)S(1)} %fusion.16), channel_id=1, source_target_pairs={{0,8},{1,9},{2,10},{3,11},{4,12},{5,13},{6,14},{7,15},{8,0},{9,1},... | collective-permute-start | bytes 175112 | tf_op jit(solution)/shard_map/ppermute | solution.py:93
  8.0 5.1 %collective-permute-start = (bf16[1,4,7296]{2,1,0:T(4,128)(2,1)S(1)}, bf16[1,4,7296]{2,1,0:T(4,128)(2,1)S(1)}, u32[]{:S(2)}, u32[]{:S(2)}) collective-permute-start(bf16[1,4,7296]{2,1,0:T(4,128)(2,1)S(1)} %fusion.16), channel_id=1, source_target_pairs={{0,4},{1,5},{2,6},{3,7},{4,0},{5,1},{6,2},{7,3},{8,12},{9,13},{10,... | collective-permute-start | bytes 175112 | tf_op jit(solution)/shard_map/ppermute | solution.py:93
  13.3 6.1 %collective-permute-start.3 = (bf16[4,4,7296]{2,1,0:T(4,128)(2,1)S(1)}, bf16[4,4,7296]{2,1,0:T(4,128)(2,1)S(1)}, u32[]{:S(2)}, u32[]{:S(2)}) collective-permute-start(bf16[4,4,7296]{2,1,0:T(4,128)(2,1)S(1)} %pad_maximum_fusion), channel_id=1, source_target_pairs={{0,2},{1,17},{2,0},{3,19},{4,6},{5,21},{6,4},{7,23},{8,10},{9,25},... | collective-permute-start | bytes 700424 | tf_op jit(solution)/shard_map/ppermute | solution.py:93
  20.4 8.6 %collective-permute-start.4 = (bf16[8,4,7296]{2,1,0:T(4,128)(2,1)S(1)}, bf16[8,4,7296]{2,1,0:T(4,128)(2,1)S(1)}, u32[]{:S(2)}, u32[]{:S(2)}) collective-permute-start(bf16[8,4,7296]{2,1,0:T(4,128)(2,1)S(1)} %get-tuple-element.10), channel_id=1, source_target_pairs={{0,16},{1,3},{2,18},{3,1},{4,20},{5,7},{6,22},{7,5},{8,24},{9,11},... | collective-permute-start | bytes 1400840 | tf_op jit(solution)/shard_map/ppermute | solution.py:93
  30.0 2.5 %collective-permute-start.5 = (bf16[16,4,7296]{2,1,0:T(4,128)(2,1)S(1)}, bf16[16,4,7296]{2,1,0:T(4,128)(2,1)S(1)}, u32[]{:S(2)}, u32[]{:S(2)}) collective-permute-start(bf16[16,4,7296]{2,1,0:T(4,128)(2,1)S(1)} %get-tuple-element.6), channel_id=1, source_target_pairs={{0,1},{1,0},{2,3},{3,2},{4,5},{5,4},{6,7},{7,6},{8,9},{9,8},{10,11... | collective-permute-start | bytes 2801672 | tf_op jit(solution)/shard_map/ppermute | solution.py:93
  36.9 3.2 %copy-start.1 = (bf16[1,3584,512]{2,1,0:T(8,128)(2,1)S(1)}, bf16[1,3584,512]{2,1,0:T(8,128)(2,1)}, u32[]{:S(2)}) copy-start(bf16[1,3584,512]{2,1,0:T(8,128)(2,1)} %param.12) | copy-start | bytes 11010052
  40.1 2.0 %copy-start.2 = (bf16[1,512,3584]{2,1,0:T(8,128)(2,1)S(1)}, bf16[1,512,3584]{2,1,0:T(8,128)(2,1)}, u32[]{:S(2)}) copy-start(bf16[1,512,3584]{2,1,0:T(8,128)(2,1)} %param.13) | copy-start | bytes 11010052
  42.1 2.0 %copy-start = (bf16[1,3584,512]{2,1,0:T(8,128)(2,1)S(1)}, bf16[1,3584,512]{2,1,0:T(8,128)(2,1)}, u32[]{:S(2)}) copy-start(bf16[1,3584,512]{2,1,0:T(8,128)(2,1)} %param.11) | copy-start | bytes 11010052
  49.5 2.2 %collective-permute-start.6 = (bf16[16,4,3584]{2,1,0:T(4,128)(2,1)}, bf16[16,4,3584]{2,1,0:T(4,128)(2,1)}, u32[]{:S(2)}, u32[]{:S(2)}) collective-permute-start(bf16[16,4,3584]{2,1,0:T(4,128)(2,1)} %slice.50), channel_id=1, source_target_pairs={{0,1},{1,0},{2,3},{3,2},{4,5},{5,4},{6,7},{7,6},{8,9},{9,8},{10,11... | collective-permute-start | bytes 1376264 | tf_op jit(solution)/shard_map/ppermute | solution.py:93
  53.2 6.1 %collective-permute-start.7 = (bf16[8,4,3584]{2,1,0:T(4,128)(2,1)S(1)}, bf16[8,4,3584]{2,1,0:T(4,128)(2,1)S(1)}, u32[]{:S(2)}, u32[]{:S(2)}) collective-permute-start(bf16[8,4,3584]{2,1,0:T(4,128)(2,1)S(1)} %slice.98), channel_id=1, source_target_pairs={{0,16},{1,3},{2,18},{3,1},{4,20},{5,7},{6,22},{7,5},{8,24},{9,11},... | collective-permute-start | bytes 688136 | tf_op jit(solution)/shard_map/ppermute | solution.py:93
  59.4 4.9 %collective-permute-start.8 = (bf16[4,4,3584]{2,1,0:T(4,128)(2,1)S(1)}, bf16[4,4,3584]{2,1,0:T(4,128)(2,1)S(1)}, u32[]{:S(2)}, u32[]{:S(2)}) collective-permute-start(bf16[4,4,3584]{2,1,0:T(4,128)(2,1)S(1)} %slice.99), channel_id=1, source_target_pairs={{0,2},{1,17},{2,0},{3,19},{4,6},{5,21},{6,4},{7,23},{8,10},{9,25},... | collective-permute-start | bytes 344072 | tf_op jit(solution)/shard_map/ppermute | solution.py:93
  64.4 8.7 %collective-permute-start.9 = (bf16[4,3584]{1,0:T(4,128)(2,1)S(1)}, bf16[4,3584]{1,0:T(4,128)(2,1)S(1)}, u32[]{:S(2)}, u32[]{:S(2)}) collective-permute-start(bf16[4,3584]{1,0:T(4,128)(2,1)S(1)} %get-tuple-element.11), channel_id=1, source_target_pairs={{0,12},{1,13},{2,14},{3,15},{4,8},{5,9},{6,10},{7,11},{8,4},{9,5},... | collective-permute-start | bytes 86024 | tf_op jit(solution)/shard_map/ppermute | solution.py:93
  67.2 5.9 %collective-permute-start.11 = (bf16[4,3584]{1,0:T(4,128)(2,1)S(1)}, bf16[4,3584]{1,0:T(4,128)(2,1)S(1)}, u32[]{:S(2)}, u32[]{:S(2)}) collective-permute-start(bf16[4,3584]{1,0:T(4,128)(2,1)S(1)} %get-tuple-element.12), channel_id=1, source_target_pairs={{0,4},{1,5},{2,6},{3,7},{4,0},{5,1},{6,2},{7,3},{8,12},{9,13},{10,... | collective-permute-start | bytes 86024 | tf_op jit(solution)/shard_map/ppermute | solution.py:93
  67.2 5.9 %collective-permute-start.10 = (bf16[4,3584]{1,0:T(4,128)(2,1)S(1)}, bf16[4,3584]{1,0:T(4,128)(2,1)S(1)}, u32[]{:S(2)}, u32[]{:S(2)}) collective-permute-start(bf16[4,3584]{1,0:T(4,128)(2,1)S(1)} %get-tuple-element.13), channel_id=1, source_target_pairs={{0,8},{1,9},{2,10},{3,11},{4,12},{5,13},{6,14},{7,15},{8,0},{9,1},... | collective-permute-start | bytes 86024 | tf_op jit(solution)/shard_map/ppermute | solution.py:93

commit v2 on v1

--- a/solution.py
+++ b/solution.py
@@ -1,11 +1,23 @@
+import functools
+
 import jax
 import jax.numpy as jnp
 from jax import lax
+from jax.experimental import pallas as pl
+from jax.experimental.pallas import tpu as pltpu
 from jax.sharding import PartitionSpec as P
 
 TOP = 8
 F32 = jnp.float32
 BF16 = jnp.bfloat16
+
+
+def room(mib):
+    return pltpu.CompilerParams(vmem_limit_bytes=mib * 2**20)
+
+
+BUSY = pl.CostEstimate(flops=10**10, transcendentals=0, bytes_accessed=0)
+WHOLE = pl.BlockSpec(memory_space=pltpu.VMEM)
 
 
 def expert_rows(rows_in, rows_grad, gate_w, up_w, down_w):
@@ -93,43 +105,167 @@
     return lax.ppermute(value, ("sp", "ep"), pairs)
 
 
+def rows_kernel(*refs):
+    out_ref = refs[-1]
+    rows = refs[0].shape[1]
+    for n, ref in enumerate(refs[:-1]):
+        out_ref[n * rows : (n + 1) * rows, :] = ref[0]
+
+
+def stack_rows(blocks):
+    rows, width = blocks[0].shape[1:]
+    return pl.pallas_call(
+        rows_kernel,
+        out_shape=jax.ShapeDtypeStruct((len(blocks) * rows, width), blocks[0].dtype),
+        in_specs=[WHOLE] * len(blocks),
+        out_specs=WHOLE,
+        compiler_params=room(2),
+        cost_estimate=BUSY,
+    )(*blocks)
+
+
+def spread_kernel(grad_in, weight_in, ids_in, out_ref, grad_ref, weight_ref, ids_ref, sem):
+    copies = [
+        pltpu.make_async_copy(source, target, sem.at[n])
+        for n, (source, target) in enumerate(
+            ((grad_in, grad_ref), (weight_in, weight_ref), (ids_in, ids_ref))
+        )
+    ]
+    for copy in copies:
+        copy.start()
+    for copy in copies:
+        copy.wait()
+    width = grad_ref.shape[2]
+    lane = lax.broadcasted_iota(jnp.int32, (grad_ref.shape[1], out_ref.shape[2] - width), 1)
+    weight = weight_ref[0].astype(F32)
+    spread = jnp.zeros(lane.shape, F32)
+    for k in range(ids_ref.shape[2]):
+        spread += jnp.where(lane == ids_ref[0, :, k : k + 1], weight[:, k : k + 1], 0.0)
+    out_ref[0, :, :width] = grad_ref[0]
+    out_ref[0, :, width:] = spread.astype(BF16)
+
+
+def spread_weights(out_grad, route_weights, expert_ids, n_expert):
+    _, tok_dev, width = out_grad.shape
+    return pl.pallas_call(
+        spread_kernel,
+        out_shape=jax.ShapeDtypeStruct((1, tok_dev, width + n_expert + -n_expert % 128), BF16),
+        in_specs=[pl.BlockSpec(memory_space=pltpu.HBM)] * 3,
+        out_specs=WHOLE,
+        scratch_shapes=[
+            pltpu.VMEM(out_grad.shape, out_grad.dtype),
+            pltpu.VMEM(route_weights.shape, route_weights.dtype),
+            pltpu.VMEM(expert_ids.shape, expert_ids.dtype),
+            pltpu.SemaphoreType.DMA((3,)),
+        ],
+        compiler_params=room(2),
+        cost_estimate=BUSY,
+        name="spread",
+    )(*(pltpu.with_memory_space_constraint(x, pltpu.HBM) for x in (out_grad, route_weights, expert_ids)))
+
+
+def forward_kernel(n, *refs):
+    pieces, (gate_w, up_w, gate_by, up_by, hidden_t) = refs[:n], refs[n:]
+    rows = jnp.concatenate([piece[...] for piece in pieces], axis=0)
+    step = min(256, gate_w.shape[1])
+    for c in range(0, gate_w.shape[1], step):
+        cols = slice(c, c + step)
+        gate_pre = jnp.dot(rows, gate_w[:, cols], preferred_element_type=F32)
+        up_pre = jnp.dot(rows, up_w[:, cols], preferred_element_type=F32)
+        squash = jax.nn.sigmoid(gate_pre)
+        swish = gate_pre * squash
+        gate_by[:, cols] = up_pre * squash * (1.0 + gate_pre * (1.0 - squash))
+        up_by[:, cols] = swish
+        hidden_t[cols, :] = (swish * up_pre).T.astype(BF16)
+
+
+def backward_kernel(n, width, *refs):
+    pieces, (down_w, gate_w, up_w, gate_by, up_by, part, scaled) = refs[:n], refs[n:]
+    expert = lax.axis_index("ep")
+    start = 0
+    for piece in pieces:
+        spread = piece[:, width:].astype(F32)
+        lane = lax.broadcasted_iota(jnp.int32, spread.shape, 1)
+        weight = jnp.sum(jnp.where(lane == expert, spread, 0.0), axis=1, keepdims=True)
+        rows = slice(start, start + piece.shape[0])
+        scaled[rows, :] = (weight * piece[:, :width].astype(F32)).astype(BF16)
+        start += piece.shape[0]
+    nt = (((1,), (1,)), ((), ()))
+    hidden_grad = lax.dot_general(scaled[...], down_w[...], nt, preferred_element_type=F32)
+    gate_grad = (hidden_grad * gate_by[...]).astype(BF16)
+    up_grad = (hidden_grad * up_by[...]).astype(BF16)
+    step = 512 if width % 512 == 0 else width
+    for c in range(0, width, step):
+        cols = slice(c, c + step)
+        first = lax.dot_general(gate_grad, gate_w[cols, :], nt, preferred_element_type=F32)
+        second = lax.dot_general(up_grad, up_w[cols, :], nt, preferred_element_type=F32)
+        part[:, cols] = (first + second).astype(BF16)
+
+
 def dense(activations, out_grad, route_weights, expert_ids, w_gate, w_up, w_down):
     n_ep = lax.axis_size("ep")
     n_sp = lax.axis_size("sp")
     tok_dev, width = activations.shape[1:]
-    swap = lambda value, partner: exchange(value, partner, n_sp, n_ep)
+    units = w_gate.shape[2]
+
+    def swap(value, partner):
+        return exchange(value, partner, n_sp, n_ep)
+
     far = [4 * j for j in range(1, n_ep // 4)][::-1]
     one = lambda i: i ^ n_ep if i & 1 else i ^ 2
     two = lambda i: i ^ 2 if i & 1 else i ^ n_ep
     core = lambda i: i ^ 1
 
-    chosen = expert_ids[0][:, :, None] == jnp.arange(n_ep, dtype=jnp.int32)[None, None, :]
-    per_expert = jnp.sum(jnp.where(chosen, route_weights[0].astype(F32)[:, :, None], 0.0), axis=1)
-    per_expert = jnp.pad(per_expert, ((0, 0), (0, -n_ep % 128))).astype(BF16)
-    mine = jnp.concatenate([activations[0], out_grad[0], per_expert], axis=1)[None]
-
-    parts = {j: swap(mine, lambda i, j=j: i ^ j) for j in far}
-    held = jnp.concatenate([mine] + [parts[j] for j in sorted(far)], axis=0)
-    held = jnp.concatenate([held, swap(held, one)], axis=0)
-    held = jnp.concatenate([held, swap(held, two)], axis=0)
-    held = jnp.concatenate([held, swap(held, core)], axis=0)
-    blocks = held.shape[0]
-    held = held.reshape(blocks * tok_dev, held.shape[2])
-    weight = lax.dynamic_slice_in_dim(held[:, 2 * width :], lax.axis_index("ep"), 1, axis=1)
-    rows_in = held[:, :width]
-    rows_grad = (weight.astype(F32) * held[:, width : 2 * width].astype(F32)).astype(BF16)
-
-    partial_rows, weight_grad = expert_rows(rows_in, rows_grad, w_gate[0], w_up[0], w_down[0])
-
-    total = partial_rows.reshape(blocks, tok_dev, width)
+    def gather(mine):
+        parts = {j: swap(mine, lambda i, j=j: i ^ j) for j in far}
+        column = stack_rows([mine] + [parts[j] for j in sorted(far)])
+        half = jnp.concatenate([column, swap(column, one)], axis=0)
+        other = swap(half, core)
+        rest = swap(half, two)
+        return [half, rest, other, swap(rest, core)]
+
+    rows_in = gather(activations)
+    gradients = spread_weights(out_grad, route_weights, expert_ids, n_ep)
+    rows_grad = gather(gradients)
+    gate_w, up_w, down_w = w_gate[0], w_up[0], w_down[0]
+    rows = sum(piece.shape[0] for piece in rows_in)
+    n = len(rows_in)
+
+    gate_by, up_by, hidden_t = pl.pallas_call(
+        functools.partial(forward_kernel, n),
+        out_shape=(
+            jax.ShapeDtypeStruct((rows, units), F32),
+            jax.ShapeDtypeStruct((rows, units), F32),
+            jax.ShapeDtypeStruct((units, rows), BF16),
+        ),
+        in_specs=[WHOLE] * (n + 2),
+        out_specs=(WHOLE,) * 3,
+        compiler_params=room(16),
+        name="forward",
+    )(*rows_in, gate_w, up_w)
+    part, scaled = pl.pallas_call(
+        functools.partial(backward_kernel, n, width),
+        out_shape=(
+            jax.ShapeDtypeStruct((rows, width), BF16),
+            jax.ShapeDtypeStruct((rows, width), BF16),
+        ),
+        in_specs=[WHOLE] * (n + 5),
+        out_specs=(WHOLE,) * 2,
+        compiler_params=room(24),
+        name="backward",
+    )(*rows_grad, down_w, gate_w, up_w, gate_by, up_by)
+    weight_grad = jnp.dot(hidden_t, scaled, preferred_element_type=F32)
+
+    total = part
     for partner in (core, two, one):
         half = total.shape[0] // 2
         got = swap(total[half:].astype(BF16), partner)
         total = total[:half].astype(F32) + got.astype(F32)
     sent = total.astype(BF16)
-    own = total[0]
+    own = total[:tok_dev]
     for j in far:
-        own = own + swap(sent[j // 4], lambda i, j=j: i ^ j).astype(F32)
+        block = sent[j // 4 * tok_dev : (j // 4 + 1) * tok_dev]
+        own = own + swap(block, lambda i, j=j: i ^ j).astype(F32)
     return (own.astype(BF16)[None], weight_grad[None])
 
 
@@ -139,8 +275,9 @@
     tokens = activations.shape[1] * n_sp * n_ep
     rows = n_ep * max(2, activations.shape[1] * n_sp * TOP * 3 // (2 * n_ep))
     few = tokens <= 2 * rows and n_sp == 2 and n_ep >= 8 and n_ep & (n_ep - 1) == 0
-    body = dense if few else routed
-    return body(activations, out_grad, route_weights, expert_ids, w_gate, w_up, w_down)
+    if not few:
+        return routed(activations, out_grad, route_weights, expert_ids, w_gate, w_up, w_down)
+    return dense(activations, out_grad, route_weights, expert_ids, w_gate, w_up, w_down)
 
 
 def solution(mesh):

time: 74.2 us -> 59.4 us (0.80)
  local copies, waits for them, and re-layouts: 14 us -> 0.92 us
  starting transfers between devices: 16.9 us -> 25.3 us
  matrix products: 11.7 us -> 4.15 us
  other arithmetic: 6.98 us -> 0.85 us
  Pallas kernels: 0 us -> 5.92 us
  waiting for transfers between devices: 23.4 us -> 21.3 us
    ppermute x12 -> x20, starting transfers between devices: 16.9 us -> 25.3 us  [exchange(): return lax.ppermute(value, ('sp', 'ep'), pairs)]
    dot_general x6 -> x1, matrix products: 11.7 us -> 4.15 us  [dense(): weight_grad = jnp.dot(hidden_t, scaled, preferred_element_type=F32)]
    pallas_call x0 -> x5, Pallas kernels: none -> 5.92 us  [the longest x1 3.76 us: dense(): pl.pallas_call(functools.partial(backward_kernel, n, width), out_shape=(j...]
    unnamed x11 -> x8, local copies, waits for them, and re-layouts: 5.45 us -> 0.81 us
    reshape x1 -> x0, local copies, waits for them, and re-layouts: 2.96 us -> none  [dense(): held = held.reshape(blocks * tok_dev, held.shape[2])]
    concatenate x2 -> x0, local copies, waits for them, and re-layouts: 2.3 us -> none  [the longest x1 1.25 us: dense(): held = jnp.concatenate([held, swap(held, core)], axis=0)]
    ppermute x12 -> x20, waiting for transfers between devices: 23.4 us -> 21.3 us  [exchange(): return lax.ppermute(value, ('sp', 'ep'), pairs)]
    slice x3, local copies, waits for them, and re-layouts: 2.02 us -> 0.07 us  [dense(): got = swap(total[half:].astype(BF16), partner)]
  transfers between devices with their start and end apart: 12 -> 20, of which waited for: 8 -> 8; matrix products, arithmetic and copies ran while one was open for 12% -> 7% of each run, Pallas kernels for 0% -> 2%
where the time goes in v2:
time: 59.4 us; the launch traced here: 59.2 us
  starting transfers between devices  25.3 us (43%)
  waiting for transfers between devices  21.3 us (36%)
  Pallas kernels  5.92 us (10%)
  matrix products  4.15 us (7%)
  local copies, waits for them, and re-layouts  0.92 us (2%)
  other arithmetic  0.85 us (1%)
  between operations  0.77 us (1%)
    ppermute x20, starting transfers between devices, exchange(): return lax.ppermute(value, ('sp', 'ep'), pairs)  25.3 us
    ppermute x20, waiting for transfers between devices, exchange(): return lax.ppermute(value, ('sp', 'ep'), pairs)  21.3 us
    dot_general x1, matrix products, dense(): weight_grad = jnp.dot(hidden_t, scaled, preferred_element_type=F32)  4.15 us
    pallas_call x1, Pallas kernels, dense(): pl.pallas_call(functools.partial(backward_kernel, n, width), out_shape=(j...  3.76 us
    pallas_call x1, Pallas kernels, dense(): pl.pallas_call(functools.partial(forward_kernel, n), out_shape=(jax.Shape...  1.22 us
  transfers between devices with their start and end apart: 20, of which 8 were waited for; matrix products, arithmetic and copies ran while one was open for 7% of the time, Pallas kernels for 2%

profile of v2, /device:TPU:0, one launch (start us, length us, event | category | flops | bytes accessed | tf_op | source)
XLA Modules:
  0.0 59.2 jit_solution(6487639125452578066)
XLA Ops:
  0.6 0.9 %spread.1.refs_0_ = bf16[1,4,3712]{2,1,0:T(4,128)(2,1)S(1)} custom-call(bf16[1,4,3584]{2,1,0:T(4,128)(2,1)} %grad_in.1, bf16[1,4,8]{2,1,0:T(4,128)(2,1)} %weight_in.1, s32[1,4,8]{2,1,0:T(4,128)} %ids_in.1), custom_call_target="tpu_custom_call" | custom-call | flops 10000000000 | tf_op jit(solution)/shard_map/spread/pallas_call | solution.py:150
  1.5 5.1 %collective-permute-start.2 = (bf16[1,4,3712]{2,1,0:T(4,128)(2,1)S(1)}, bf16[1,4,3712]{2,1,0:T(4,128)(2,1)S(1)}, u32[]{:S(2)}, u32[]{:S(2)}) collective-permute-start(bf16[1,4,3712]{2,1,0:T(4,128)(2,1)S(1)} %spread.1.refs_0_), channel_id=1, source_target_pairs={{0,12},{1,13},{2,14},{3,15},{4,8},{5,9},{6,10},{7,11},{8,4},{9,5},... | collective-permute-start | bytes 89096 | tf_op jit(solution)/shard_map/ppermute | solution.py:105
  7.3 2.3 %collective-permute-start.8 = (bf16[1,4,3584]{2,1,0:T(4,128)(2,1)S(1)}, bf16[1,4,3584]{2,1,0:T(4,128)(2,1)S(1)}, u32[]{:S(2)}, u32[]{:S(2)}) collective-permute-start(bf16[1,4,3584]{2,1,0:T(4,128)(2,1)S(1)} %copy-done.3), channel_id=1, source_target_pairs={{0,8},{1,9},{2,10},{3,11},{4,12},{5,13},{6,14},{7,15},{8,0},{9,1},... | collective-permute-start | bytes 86024 | tf_op jit(solution)/shard_map/ppermute | solution.py:105
  9.6 2.0 %collective-permute-start.7 = (bf16[1,4,3584]{2,1,0:T(4,128)(2,1)S(1)}, bf16[1,4,3584]{2,1,0:T(4,128)(2,1)S(1)}, u32[]{:S(2)}, u32[]{:S(2)}) collective-permute-start(bf16[1,4,3584]{2,1,0:T(4,128)(2,1)S(1)} %copy-done.3), channel_id=1, source_target_pairs={{0,4},{1,5},{2,6},{3,7},{4,0},{5,1},{6,2},{7,3},{8,12},{9,13},{10,... | collective-permute-start | bytes 86024 | tf_op jit(solution)/shard_map/ppermute | solution.py:105
  11.6 0.7 %collective-permute-start.9 = (bf16[1,4,3584]{2,1,0:T(4,128)(2,1)S(1)}, bf16[1,4,3584]{2,1,0:T(4,128)(2,1)S(1)}, u32[]{:S(2)}, u32[]{:S(2)}) collective-permute-start(bf16[1,4,3584]{2,1,0:T(4,128)(2,1)S(1)} %copy-done.3), channel_id=1, source_target_pairs={{0,12},{1,13},{2,14},{3,15},{4,8},{5,9},{6,10},{7,11},{8,4},{9,5},... | collective-permute-start | bytes 86024 | tf_op jit(solution)/shard_map/ppermute | solution.py:105
  12.4 1.6 %collective-permute-start.3 = (bf16[16,3712]{1,0:T(8,128)(2,1)S(1)}, bf16[16,3712]{1,0:T(8,128)(2,1)S(1)}, u32[]{:S(2)}, u32[]{:S(2)}) collective-permute-start(bf16[16,3712]{1,0:T(8,128)(2,1)S(1)} %shard_map.86), channel_id=1, source_target_pairs={{0,2},{1,17},{2,0},{3,19},{4,6},{5,21},{6,4},{7,23},{8,10},{9,25},... | collective-permute-start | bytes 356360 | tf_op jit(solution)/shard_map/ppermute | solution.py:105
  14.0 3.3 %collective-permute-done.9.refs_3_ = bf16[1,4,3584]{2,1,0:T(4,128)(2,1)S(1)} collective-permute-done((bf16[1,4,3584]{2,1,0:T(4,128)(2,1)S(1)}, bf16[1,4,3584]{2,1,0:T(4,128)(2,1)S(1)}, u32[]{:S(2)}, u32[]{:S(2)}) %collective-permute-start.9) | collective-permute-done | bytes 28704 | tf_op jit(solution)/shard_map/ppermute | solution.py:105
  17.3 1.6 %collective-permute-start.10 = (bf16[16,3584]{1,0:T(8,128)(2,1)S(1)}, bf16[16,3584]{1,0:T(8,128)(2,1)S(1)}, u32[]{:S(2)}, u32[]{:S(2)}) collective-permute-start(bf16[16,3584]{1,0:T(8,128)(2,1)S(1)} %shard_map.87), channel_id=1, source_target_pairs={{0,2},{1,17},{2,0},{3,19},{4,6},{5,21},{6,4},{7,23},{8,10},{9,25},... | collective-permute-start | bytes 344072 | tf_op jit(solution)/shard_map/ppermute | solution.py:105
  18.9 1.6 %collective-permute-start.4 = (bf16[32,3712]{1,0:T(8,128)(2,1)S(1)}, bf16[32,3712]{1,0:T(8,128)(2,1)S(1)}, u32[]{:S(2)}, u32[]{:S(2)}) collective-permute-start(bf16[32,3712]{1,0:T(8,128)(2,1)S(1)} %pad_maximum_fusion.refs_0_), channel_id=1, source_target_pairs={{0,16},{1,3},{2,18},{3,1},{4,20},{5,7},{6,22},{7,5},{8,24},{9,11},... | collective-permute-start | bytes 712712 | tf_op jit(solution)/shard_map/ppermute | solution.py:105
  20.5 2.9 %collective-permute-done.10 = bf16[16,3584]{1,0:T(8,128)(2,1)S(1)} collective-permute-done((bf16[16,3584]{1,0:T(8,128)(2,1)S(1)}, bf16[16,3584]{1,0:T(8,128)(2,1)S(1)}, u32[]{:S(2)}, u32[]{:S(2)}) %collective-permute-start.10) | collective-permute-done | bytes 114720 | tf_op jit(solution)/shard_map/ppermute | solution.py:105
  23.4 1.5 %collective-permute-start.11 = (bf16[32,3584]{1,0:T(8,128)(2,1)S(1)}, bf16[32,3584]{1,0:T(8,128)(2,1)S(1)}, u32[]{:S(2)}, u32[]{:S(2)}) collective-permute-start(bf16[32,3584]{1,0:T(8,128)(2,1)S(1)} %pad_maximum_fusion.1.refs_0_), channel_id=1, source_target_pairs={{0,16},{1,3},{2,18},{3,1},{4,20},{5,7},{6,22},{7,5},{8,24},{9,11},... | collective-permute-start | bytes 688136 | tf_op jit(solution)/shard_map/ppermute | solution.py:105
  25.6 3.9 %collective-permute-done.11.refs_1_ = bf16[32,3584]{1,0:T(8,128)(2,1)S(1)} collective-permute-done((bf16[32,3584]{1,0:T(8,128)(2,1)S(1)}, bf16[32,3584]{1,0:T(8,128)(2,1)S(1)}, u32[]{:S(2)}, u32[]{:S(2)}) %collective-permute-start.11) | collective-permute-done | bytes 229408 | tf_op jit(solution)/shard_map/ppermute | solution.py:105
  29.5 1.5 %collective-permute-done.13.refs_3_ = bf16[32,3584]{1,0:T(8,128)(2,1)S(1)} collective-permute-done((bf16[32,3584]{1,0:T(8,128)(2,1)S(1)}, bf16[32,3584]{1,0:T(8,128)(2,1)S(1)}, u32[]{:S(2)}, u32[]{:S(2)}) %collective-permute-start.13) | collective-permute-done | bytes 229408 | tf_op jit(solution)/shard_map/ppermute | solution.py:105
  31.0 1.2 %forward.1 = (f32[128,512]{1,0:T(8,128)S(1)}, f32[128,512]{1,0:T(8,128)S(1)}, bf16[512,128]{1,0:T(8,128)(2,1)S(1)}) custom-call(bf16[32,3584]{1,0:T(8,128)(2,1)S(1)} %pad_maximum_fusion.1.refs_0_, bf16[32,3584]{1,0:T(8,128)(2,1)S(1)} %collective-permute-done.11.refs_1_, bf16[32,3584]{1,0:T(8,128)(2,1)S(1)} %collective-permute-done.12.refs_2_, ...), custom_call_target="tpu_custom_call" | custom-call | tf_op jit(solution)/shard_map/forward/pallas_call | solution.py:234
  32.3 0.8 %copy-done.2 = bf16[1,512,3584]{2,1,0:T(8,128)(2,1)S(1)} copy-done((bf16[1,512,3584]{2,1,0:T(8,128)(2,1)S(1)}, bf16[1,512,3584]{2,1,0:T(8,128)(2,1)}, u32[]{:S(2)}) %copy-start.2) | copy-done | bytes 3670040
  33.1 3.8 %backward.1 = (bf16[128,3584]{1,0:T(8,128)(2,1)S(1)}, bf16[128,3584]{1,0:T(8,128)(2,1)S(1)}) custom-call(bf16[32,3712]{1,0:T(8,128)(2,1)S(1)} %pad_maximum_fusion.refs_0_, bf16[32,3712]{1,0:T(8,128)(2,1)S(1)} %collective-permute-done.4.refs_1_, bf16[32,3712]{1,0:T(8,128)(2,1)S(1)} %collective-permute-done.5.refs_2_, ...), custom_call_target="tpu_custom_call" | custom-call | tf_op jit(solution)/shard_map/backward/pallas_call | solution.py:246
  37.1 1.7 %collective-permute-done.14 = bf16[64,3584]{1,0:T(8,128)(2,1)S(1)} collective-permute-done((bf16[64,3584]{1,0:T(8,128)(2,1)S(1)}, bf16[64,3584]{1,0:T(8,128)(2,1)S(1)}, u32[]{:S(2)}, u32[]{:S(2)}) %collective-permute-start.14) | collective-permute-done | bytes 458784 | tf_op jit(solution)/shard_map/ppermute | solution.py:105
  38.9 1.5 %collective-permute-start.15 = (bf16[32,3584]{1,0:T(8,128)(2,1)S(1)}, bf16[32,3584]{1,0:T(8,128)(2,1)S(1)}, u32[]{:S(2)}, u32[]{:S(2)}) collective-permute-start(bf16[32,3584]{1,0:T(8,128)(2,1)S(1)} %slice.64), channel_id=1, source_target_pairs={{0,16},{1,3},{2,18},{3,1},{4,20},{5,7},{6,22},{7,5},{8,24},{9,11},... | collective-permute-start | bytes 688136 | tf_op jit(solution)/shard_map/ppermute | solution.py:105
  40.4 4.6 %collective-permute-done.15 = bf16[32,3584]{1,0:T(8,128)(2,1)S(1)} collective-permute-done((bf16[32,3584]{1,0:T(8,128)(2,1)S(1)}, bf16[32,3584]{1,0:T(8,128)(2,1)S(1)}, u32[]{:S(2)}, u32[]{:S(2)}) %collective-permute-start.15) | collective-permute-done | bytes 229408 | tf_op jit(solution)/shard_map/ppermute | solution.py:105
  45.0 1.6 %collective-permute-start.16 = (bf16[16,3584]{1,0:T(8,128)(2,1)S(1)}, bf16[16,3584]{1,0:T(8,128)(2,1)S(1)}, u32[]{:S(2)}, u32[]{:S(2)}) collective-permute-start(bf16[16,3584]{1,0:T(8,128)(2,1)S(1)} %slice.65), channel_id=1, source_target_pairs={{0,2},{1,17},{2,0},{3,19},{4,6},{5,21},{6,4},{7,23},{8,10},{9,25},... | collective-permute-start | bytes 344072 | tf_op jit(solution)/shard_map/ppermute | solution.py:105
  46.6 3.3 %collective-permute-done.16 = bf16[16,3584]{1,0:T(8,128)(2,1)S(1)} collective-permute-done((bf16[16,3584]{1,0:T(8,128)(2,1)S(1)}, bf16[16,3584]{1,0:T(8,128)(2,1)S(1)}, u32[]{:S(2)}, u32[]{:S(2)}) %collective-permute-start.16) | collective-permute-done | bytes 114720 | tf_op jit(solution)/shard_map/ppermute | solution.py:105
  50.0 0.8 %collective-permute-start.17 = (bf16[4,3584]{1,0:T(4,128)(2,1)S(1)}, bf16[4,3584]{1,0:T(4,128)(2,1)S(1)}, u32[]{:S(2)}, u32[]{:S(2)}) collective-permute-start(bf16[4,3584]{1,0:T(4,128)(2,1)S(1)} %get-tuple-element.14), channel_id=1, source_target_pairs={{0,12},{1,13},{2,14},{3,15},{4,8},{5,9},{6,10},{7,11},{8,4},{9,5},... | collective-permute-start | bytes 86024 | tf_op jit(solution)/shard_map/ppermute | solution.py:105
  50.8 3.7 %collective-permute-start.18 = (bf16[4,3584]{1,0:T(4,128)(2,1)S(1)}, bf16[4,3584]{1,0:T(4,128)(2,1)S(1)}, u32[]{:S(2)}, u32[]{:S(2)}) collective-permute-start(bf16[4,3584]{1,0:T(4,128)(2,1)S(1)} %get-tuple-element.16), channel_id=1, source_target_pairs={{0,8},{1,9},{2,10},{3,11},{4,12},{5,13},{6,14},{7,15},{8,0},{9,1},... | collective-permute-start | bytes 86024 | tf_op jit(solution)/shard_map/ppermute | solution.py:105
  54.4 4.1 %convolution_bitcast_fusion = f32[1,512,3584]{2,1,0:T(8,128)} fusion(bf16[512,128]{1,0:T(8,128)(2,1)S(1)} %get-tuple-element.10, bf16[128,3584]{1,0:T(8,128)(2,1)S(1)} %get-tuple-element.11), kind=kOutput, calls=%fused_computation | convolution fusion | flops 469762048 | bytes 8388608 | tf_op jit(solution)/shard_map/dot_general | solution.py:257
  (40 shorter events, 2.6 us)
Async XLA Ops:
  0.6 6.7 %copy-start.3 = (bf16[1,4,3584]{2,1,0:T(4,128)(2,1)S(1)}, bf16[1,4,3584]{2,1,0:T(4,128)(2,1)}, u32[]{:S(2)}) copy-start(bf16[1,4,3584]{2,1,0:T(4,128)(2,1)} %refs_0_.1) | copy-start | bytes 86020
  1.5 10.1 %collective-permute-start.2 = (bf16[1,4,3712]{2,1,0:T(4,128)(2,1)S(1)}, bf16[1,4,3712]{2,1,0:T(4,128)(2,1)S(1)}, u32[]{:S(2)}, u32[]{:S(2)}) collective-permute-start(bf16[1,4,3712]{2,1,0:T(4,128)(2,1)S(1)} %spread.1.refs_0_), channel_id=1, source_target_pairs={{0,12},{1,13},{2,14},{3,15},{4,8},{5,9},{6,10},{7,11},{8,4},{9,5},... | collective-permute-start | bytes 89096 | tf_op jit(solution)/shard_map/ppermute | solution.py:105
  6.7 5.7 %collective-permute-start.1 = (bf16[1,4,3712]{2,1,0:T(4,128)(2,1)S(1)}, bf16[1,4,3712]{2,1,0:T(4,128)(2,1)S(1)}, u32[]{:S(2)}, u32[]{:S(2)}) collective-permute-start(bf16[1,4,3712]{2,1,0:T(4,128)(2,1)S(1)} %spread.1.refs_0_), channel_id=1, source_target_pairs={{0,8},{1,9},{2,10},{3,11},{4,12},{5,13},{6,14},{7,15},{8,0},{9,1},... | collective-permute-start | bytes 89096 | tf_op jit(solution)/shard_map/ppermute | solution.py:105
  6.7 5.7 %collective-permute-start = (bf16[1,4,3712]{2,1,0:T(4,128)(2,1)S(1)}, bf16[1,4,3712]{2,1,0:T(4,128)(2,1)S(1)}, u32[]{:S(2)}, u32[]{:S(2)}) collective-permute-start(bf16[1,4,3712]{2,1,0:T(4,128)(2,1)S(1)} %spread.1.refs_0_), channel_id=1, source_target_pairs={{0,4},{1,5},{2,6},{3,7},{4,0},{5,1},{6,2},{7,3},{8,12},{9,13},{10,... | collective-permute-start | bytes 89096 | tf_op jit(solution)/shard_map/ppermute | solution.py:105
  7.3 6.7 %collective-permute-start.8 = (bf16[1,4,3584]{2,1,0:T(4,128)(2,1)S(1)}, bf16[1,4,3584]{2,1,0:T(4,128)(2,1)S(1)}, u32[]{:S(2)}, u32[]{:S(2)}) collective-permute-start(bf16[1,4,3584]{2,1,0:T(4,128)(2,1)S(1)} %copy-done.3), channel_id=1, source_target_pairs={{0,8},{1,9},{2,10},{3,11},{4,12},{5,13},{6,14},{7,15},{8,0},{9,1},... | collective-permute-start | bytes 86024 | tf_op jit(solution)/shard_map/ppermute | solution.py:105
  9.6 4.4 %collective-permute-start.7 = (bf16[1,4,3584]{2,1,0:T(4,128)(2,1)S(1)}, bf16[1,4,3584]{2,1,0:T(4,128)(2,1)S(1)}, u32[]{:S(2)}, u32[]{:S(2)}) collective-permute-start(bf16[1,4,3584]{2,1,0:T(4,128)(2,1)S(1)} %copy-done.3), channel_id=1, source_target_pairs={{0,4},{1,5},{2,6},{3,7},{4,0},{5,1},{6,2},{7,3},{8,12},{9,13},{10,... | collective-permute-start | bytes 86024 | tf_op jit(solution)/shard_map/ppermute | solution.py:105
  11.6 5.7 %collective-permute-start.9 = (bf16[1,4,3584]{2,1,0:T(4,128)(2,1)S(1)}, bf16[1,4,3584]{2,1,0:T(4,128)(2,1)S(1)}, u32[]{:S(2)}, u32[]{:S(2)}) collective-permute-start(bf16[1,4,3584]{2,1,0:T(4,128)(2,1)S(1)} %copy-done.3), channel_id=1, source_target_pairs={{0,12},{1,13},{2,14},{3,15},{4,8},{5,9},{6,10},{7,11},{8,4},{9,5},... | collective-permute-start | bytes 86024 | tf_op jit(solution)/shard_map/ppermute | solution.py:105
  12.4 18.6 %copy-start = (bf16[1,3584,512]{2,1,0:T(8,128)(2,1)S(1)}, bf16[1,3584,512]{2,1,0:T(8,128)(2,1)}, u32[]{:S(2)}) copy-start(bf16[1,3584,512]{2,1,0:T(8,128)(2,1)} %param.11) | copy-start | bytes 11010052
  12.4 18.6 %copy-start.1 = (bf16[1,3584,512]{2,1,0:T(8,128)(2,1)S(1)}, bf16[1,3584,512]{2,1,0:T(8,128)(2,1)}, u32[]{:S(2)}) copy-start(bf16[1,3584,512]{2,1,0:T(8,128)(2,1)} %param.12) | copy-start | bytes 11010052
  12.4 6.5 %collective-permute-start.3 = (bf16[16,3712]{1,0:T(8,128)(2,1)S(1)}, bf16[16,3712]{1,0:T(8,128)(2,1)S(1)}, u32[]{:S(2)}, u32[]{:S(2)}) collective-permute-start(bf16[16,3712]{1,0:T(8,128)(2,1)S(1)} %shard_map.86), channel_id=1, source_target_pairs={{0,2},{1,17},{2,0},{3,19},{4,6},{5,21},{6,4},{7,23},{8,10},{9,25},... | collective-permute-start | bytes 356360 | tf_op jit(solution)/shard_map/ppermute | solution.py:105
  17.3 6.1 %collective-permute-start.10 = (bf16[16,3584]{1,0:T(8,128)(2,1)S(1)}, bf16[16,3584]{1,0:T(8,128)(2,1)S(1)}, u32[]{:S(2)}, u32[]{:S(2)}) collective-permute-start(bf16[16,3584]{1,0:T(8,128)(2,1)S(1)} %shard_map.87), channel_id=1, source_target_pairs={{0,2},{1,17},{2,0},{3,19},{4,6},{5,21},{6,4},{7,23},{8,10},{9,25},... | collective-permute-start | bytes 344072 | tf_op jit(solution)/shard_map/ppermute | solution.py:105
  18.9 6.2 %collective-permute-start.4 = (bf16[32,3712]{1,0:T(8,128)(2,1)S(1)}, bf16[32,3712]{1,0:T(8,128)(2,1)S(1)}, u32[]{:S(2)}, u32[]{:S(2)}) collective-permute-start(bf16[32,3712]{1,0:T(8,128)(2,1)S(1)} %pad_maximum_fusion.refs_0_), channel_id=1, source_target_pairs={{0,16},{1,3},{2,18},{3,1},{4,20},{5,7},{6,22},{7,5},{8,24},{9,11},... | collective-permute-start | bytes 712712 | tf_op jit(solution)/shard_map/ppermute | solution.py:105
  23.4 6.1 %collective-permute-start.11 = (bf16[32,3584]{1,0:T(8,128)(2,1)S(1)}, bf16[32,3584]{1,0:T(8,128)(2,1)S(1)}, u32[]{:S(2)}, u32[]{:S(2)}) collective-permute-start(bf16[32,3584]{1,0:T(8,128)(2,1)S(1)} %pad_maximum_fusion.1.refs_0_), channel_id=1, source_target_pairs={{0,16},{1,3},{2,18},{3,1},{4,20},{5,7},{6,22},{7,5},{8,24},{9,11},... | collective-permute-start | bytes 688136 | tf_op jit(solution)/shard_map/ppermute | solution.py:105
  24.9 7.3 %collective-permute-start.5 = (bf16[32,3712]{1,0:T(8,128)(2,1)S(1)}, bf16[32,3712]{1,0:T(8,128)(2,1)S(1)}, u32[]{:S(2)}, u32[]{:S(2)}) collective-permute-start(bf16[32,3712]{1,0:T(8,128)(2,1)S(1)} %pad_maximum_fusion.refs_0_), channel_id=1, source_target_pairs={{0,1},{1,0},{2,3},{3,2},{4,5},{5,4},{6,7},{7,6},{8,9},{9,8},{10,11... | collective-permute-start | bytes 712712 | tf_op jit(solution)/shard_map/ppermute | solution.py:105
  25.1 7.1 %collective-permute-start.6 = (bf16[32,3712]{1,0:T(8,128)(2,1)S(1)}, bf16[32,3712]{1,0:T(8,128)(2,1)S(1)}, u32[]{:S(2)}, u32[]{:S(2)}) collective-permute-start(bf16[32,3712]{1,0:T(8,128)(2,1)S(1)} %collective-permute-done.4.refs_1_), channel_id=1, source_target_pairs={{0,1},{1,0},{2,3},{3,2},{4,5},{5,4},{6,7},{7,6},{8,9},{9,8},{10,11... | collective-permute-start | bytes 712712 | tf_op jit(solution)/shard_map/ppermute | solution.py:105
  25.5 4.1 %collective-permute-start.12 = (bf16[32,3584]{1,0:T(8,128)(2,1)S(1)}, bf16[32,3584]{1,0:T(8,128)(2,1)S(1)}, u32[]{:S(2)}, u32[]{:S(2)}) collective-permute-start(bf16[32,3584]{1,0:T(8,128)(2,1)S(1)} %pad_maximum_fusion.1.refs_0_), channel_id=1, source_target_pairs={{0,1},{1,0},{2,3},{3,2},{4,5},{5,4},{6,7},{7,6},{8,9},{9,8},{10,11... | collective-permute-start | bytes 688136 | tf_op jit(solution)/shard_map/ppermute | solution.py:105
  29.5 1.5 %collective-permute-start.13 = (bf16[32,3584]{1,0:T(8,128)(2,1)S(1)}, bf16[32,3584]{1,0:T(8,128)(2,1)S(1)}, u32[]{:S(2)}, u32[]{:S(2)}) collective-permute-start(bf16[32,3584]{1,0:T(8,128)(2,1)S(1)} %collective-permute-done.11.refs_1_), channel_id=1, source_target_pairs={{0,1},{1,0},{2,3},{3,2},{4,5},{5,4},{6,7},{7,6},{8,9},{9,8},{10,11... | collective-permute-start | bytes 688136 | tf_op jit(solution)/shard_map/ppermute | solution.py:105
  31.0 2.0 %copy-start.2 = (bf16[1,512,3584]{2,1,0:T(8,128)(2,1)S(1)}, bf16[1,512,3584]{2,1,0:T(8,128)(2,1)}, u32[]{:S(2)}) copy-start(bf16[1,512,3584]{2,1,0:T(8,128)(2,1)} %param.13) | copy-start | bytes 11010052
  36.9 1.9 %collective-permute-start.14 = (bf16[64,3584]{1,0:T(8,128)(2,1)S(1)}, bf16[64,3584]{1,0:T(8,128)(2,1)S(1)}, u32[]{:S(2)}, u32[]{:S(2)}) collective-permute-start(bf16[64,3584]{1,0:T(8,128)(2,1)S(1)} %slice.33), channel_id=1, source_target_pairs={{0,1},{1,0},{2,3},{3,2},{4,5},{5,4},{6,7},{7,6},{8,9},{9,8},{10,11... | collective-permute-start | bytes 1376264 | tf_op jit(solution)/shard_map/ppermute | solution.py:105
  38.9 6.1 %collective-permute-start.15 = (bf16[32,3584]{1,0:T(8,128)(2,1)S(1)}, bf16[32,3584]{1,0:T(8,128)(2,1)S(1)}, u32[]{:S(2)}, u32[]{:S(2)}) collective-permute-start(bf16[32,3584]{1,0:T(8,128)(2,1)S(1)} %slice.64), channel_id=1, source_target_pairs={{0,16},{1,3},{2,18},{3,1},{4,20},{5,7},{6,22},{7,5},{8,24},{9,11},... | collective-permute-start | bytes 688136 | tf_op jit(solution)/shard_map/ppermute | solution.py:105
  45.0 4.9 %collective-permute-start.16 = (bf16[16,3584]{1,0:T(8,128)(2,1)S(1)}, bf16[16,3584]{1,0:T(8,128)(2,1)S(1)}, u32[]{:S(2)}, u32[]{:S(2)}) collective-permute-start(bf16[16,3584]{1,0:T(8,128)(2,1)S(1)} %slice.65), channel_id=1, source_target_pairs={{0,2},{1,17},{2,0},{3,19},{4,6},{5,21},{6,4},{7,23},{8,10},{9,25},... | collective-permute-start | bytes 344072 | tf_op jit(solution)/shard_map/ppermute | solution.py:105
  50.0 8.6 %collective-permute-start.17 = (bf16[4,3584]{1,0:T(4,128)(2,1)S(1)}, bf16[4,3584]{1,0:T(4,128)(2,1)S(1)}, u32[]{:S(2)}, u32[]{:S(2)}) collective-permute-start(bf16[4,3584]{1,0:T(4,128)(2,1)S(1)} %get-tuple-element.14), channel_id=1, source_target_pairs={{0,12},{1,13},{2,14},{3,15},{4,8},{5,9},{6,10},{7,11},{8,4},{9,5},... | collective-permute-start | bytes 86024 | tf_op jit(solution)/shard_map/ppermute | solution.py:105
  50.8 7.8 %collective-permute-start.19 = (bf16[4,3584]{1,0:T(4,128)(2,1)S(1)}, bf16[4,3584]{1,0:T(4,128)(2,1)S(1)}, u32[]{:S(2)}, u32[]{:S(2)}) collective-permute-start(bf16[4,3584]{1,0:T(4,128)(2,1)S(1)} %get-tuple-element.15), channel_id=1, source_target_pairs={{0,4},{1,5},{2,6},{3,7},{4,0},{5,1},{6,2},{7,3},{8,12},{9,13},{10,... | collective-permute-start | bytes 86024 | tf_op jit(solution)/shard_map/ppermute | solution.py:105
  50.8 7.8 %collective-permute-start.18 = (bf16[4,3584]{1,0:T(4,128)(2,1)S(1)}, bf16[4,3584]{1,0:T(4,128)(2,1)S(1)}, u32[]{:S(2)}, u32[]{:S(2)}) collective-permute-start(bf16[4,3584]{1,0:T(4,128)(2,1)S(1)} %get-tuple-element.16), channel_id=1, source_target_pairs={{0,8},{1,9},{2,10},{3,11},{4,12},{5,13},{6,14},{7,15},{8,0},{9,1},... | collective-permute-start | bytes 86024 | tf_op jit(solution)/shard_map/ppermute | solution.py:105

commit v3 on v2

--- a/solution.py
+++ b/solution.py
@@ -17,6 +17,7 @@
 
 
 BUSY = pl.CostEstimate(flops=10**10, transcendentals=0, bytes_accessed=0)
+QUICK = pl.CostEstimate(flops=10**6, transcendentals=0, bytes_accessed=0)
 WHOLE = pl.BlockSpec(memory_space=pltpu.VMEM)
 
 
@@ -105,63 +106,78 @@
     return lax.ppermute(value, ("sp", "ep"), pairs)
 
 
-def rows_kernel(*refs):
-    out_ref = refs[-1]
-    rows = refs[0].shape[1]
-    for n, ref in enumerate(refs[:-1]):
-        out_ref[n * rows : (n + 1) * rows, :] = ref[0]
-
-
-def stack_rows(blocks):
-    rows, width = blocks[0].shape[1:]
-    return pl.pallas_call(
-        rows_kernel,
-        out_shape=jax.ShapeDtypeStruct((len(blocks) * rows, width), blocks[0].dtype),
-        in_specs=[WHOLE] * len(blocks),
-        out_specs=WHOLE,
-        compiler_params=room(2),
-        cost_estimate=BUSY,
-    )(*blocks)
-
-
-def spread_kernel(grad_in, weight_in, ids_in, out_ref, grad_ref, weight_ref, ids_ref, sem):
+def pack_kernel(in_ref, grad_ref, weight_ref, ids_ref, out_ref, rows, weights, ids, sem):
+    tok_dev, width = in_ref.shape[1:]
     copies = [
         pltpu.make_async_copy(source, target, sem.at[n])
         for n, (source, target) in enumerate(
-            ((grad_in, grad_ref), (weight_in, weight_ref), (ids_in, ids_ref))
+            (
+                (weight_ref, weights),
+                (ids_ref, ids),
+                (in_ref.at[0], rows.at[0]),
+                (grad_ref.at[0], rows.at[1]),
+            )
         )
     ]
     for copy in copies:
         copy.start()
     for copy in copies:
         copy.wait()
-    width = grad_ref.shape[2]
-    lane = lax.broadcasted_iota(jnp.int32, (grad_ref.shape[1], out_ref.shape[2] - width), 1)
-    weight = weight_ref[0].astype(F32)
+    lane = lax.broadcasted_iota(jnp.int32, (tok_dev, out_ref.shape[1] - width), 1)
+    weight = weights[0].astype(F32)
     spread = jnp.zeros(lane.shape, F32)
-    for k in range(ids_ref.shape[2]):
-        spread += jnp.where(lane == ids_ref[0, :, k : k + 1], weight[:, k : k + 1], 0.0)
-    out_ref[0, :, :width] = grad_ref[0]
-    out_ref[0, :, width:] = spread.astype(BF16)
-
-
-def spread_weights(out_grad, route_weights, expert_ids, n_expert):
+    for k in range(ids.shape[2]):
+        spread += jnp.where(lane == ids[0, :, k : k + 1], weight[:, k : k + 1], 0.0)
+    out_ref[:tok_dev, :width] = rows[0]
+    out_ref[:tok_dev, width:] = jnp.zeros(lane.shape, BF16)
+    out_ref[tok_dev:, :width] = rows[1]
+    out_ref[tok_dev:, width:] = spread.astype(BF16)
+
+
+def pack(activations, out_grad, route_weights, expert_ids, n_expert):
     _, tok_dev, width = out_grad.shape
+    operands = (activations, out_grad, route_weights, expert_ids)
     return pl.pallas_call(
-        spread_kernel,
-        out_shape=jax.ShapeDtypeStruct((1, tok_dev, width + n_expert + -n_expert % 128), BF16),
-        in_specs=[pl.BlockSpec(memory_space=pltpu.HBM)] * 3,
+        pack_kernel,
+        out_shape=jax.ShapeDtypeStruct((2 * tok_dev, width + n_expert + -n_expert % 128), BF16),
+        in_specs=[pl.BlockSpec(memory_space=pltpu.HBM)] * 4,
         out_specs=WHOLE,
         scratch_shapes=[
-            pltpu.VMEM(out_grad.shape, out_grad.dtype),
+            pltpu.VMEM((2, tok_dev, width), BF16),
             pltpu.VMEM(route_weights.shape, route_weights.dtype),
             pltpu.VMEM(expert_ids.shape, expert_ids.dtype),
-            pltpu.SemaphoreType.DMA((3,)),
+            pltpu.SemaphoreType.DMA((4,)),
         ],
         compiler_params=room(2),
+        cost_estimate=QUICK,
+        name="pack",
+    )(*(pltpu.with_memory_space_constraint(x, pltpu.HBM) for x in operands))
+
+
+def stack_kernel(*refs):
+    in_ref, grad_ref = refs[-2:]
+    rows, width = refs[0].shape[0] // 2, in_ref.shape[1]
+    for n, ref in enumerate(refs[:-2]):
+        block = slice(n * rows, (n + 1) * rows)
+        in_ref[block, :] = ref[:rows, :width]
+        grad_ref[block, :] = ref[rows:, :]
+
+
+def stack(blocks, width):
+    rows, wide = blocks[0].shape
+    rows = len(blocks) * rows // 2
+    return pl.pallas_call(
+        stack_kernel,
+        out_shape=(
+            jax.ShapeDtypeStruct((rows, width), BF16),
+            jax.ShapeDtypeStruct((rows, wide), BF16),
+        ),
+        in_specs=[WHOLE] * len(blocks),
+        out_specs=(WHOLE,) * 2,
+        compiler_params=room(2),
         cost_estimate=BUSY,
-        name="spread",
-    )(*(pltpu.with_memory_space_constraint(x, pltpu.HBM) for x in (out_grad, route_weights, expert_ids)))
+        name="stack",
+    )(*blocks)
 
 
 def forward_kernel(n, *refs):
@@ -216,17 +232,17 @@
     two = lambda i: i ^ 2 if i & 1 else i ^ n_ep
     core = lambda i: i ^ 1
 
-    def gather(mine):
-        parts = {j: swap(mine, lambda i, j=j: i ^ j) for j in far}
-        column = stack_rows([mine] + [parts[j] for j in sorted(far)])
+    def gather(column):
         half = jnp.concatenate([column, swap(column, one)], axis=0)
         other = swap(half, core)
         rest = swap(half, two)
         return [half, rest, other, swap(rest, core)]
 
-    rows_in = gather(activations)
-    gradients = spread_weights(out_grad, route_weights, expert_ids, n_ep)
-    rows_grad = gather(gradients)
+    mine = pack(activations, out_grad, route_weights, expert_ids, n_ep)
+    blocks = {j: swap(mine, lambda i, j=j: i ^ j) for j in far}
+    column_in, column_grad = stack([mine] + [blocks[j] for j in sorted(far)], width)
+    rows_in = gather(column_in)
+    rows_grad = gather(column_grad)
     gate_w, up_w, down_w = w_gate[0], w_up[0], w_down[0]
     rows = sum(piece.shape[0] for piece in rows_in)
     n = len(rows_in)
@@ -241,6 +257,7 @@
         in_specs=[WHOLE] * (n + 2),
         out_specs=(WHOLE,) * 3,
         compiler_params=room(16),
+        cost_estimate=QUICK,
         name="forward",
     )(*rows_in, gate_w, up_w)
     part, scaled = pl.pallas_call(
@@ -252,6 +269,7 @@
         in_specs=[WHOLE] * (n + 5),
         out_specs=(WHOLE,) * 2,
         compiler_params=room(24),
+        cost_estimate=QUICK,
         name="backward",
     )(*rows_grad, down_w, gate_w, up_w, gate_by, up_by)
     weight_grad = jnp.dot(hidden_t, scaled, preferred_element_type=F32)

time: 59.4 us -> 57.1 us (0.961)
  starting transfers between devices: 25.3 us -> 18 us
  waiting for transfers between devices: 21.3 us -> 26.2 us
    ppermute x20 -> x17, starting transfers between devices: 25.3 us -> 18 us  [exchange(): return lax.ppermute(value, ('sp', 'ep'), pairs)]
    ppermute x20 -> x17, waiting for transfers between devices: 21.3 us -> 26.2 us  [exchange(): return lax.ppermute(value, ('sp', 'ep'), pairs)]
  transfers between devices with their start and end apart: 20 -> 17, of which waited for: 8 -> 9; matrix products, arithmetic and copies ran while one was open for 7% -> 7% of each run, Pallas kernels for 2% -> 2%
where the time goes in v3:
time: 57.1 us; the launch traced here: 56.9 us
  waiting for transfers between devices  26.2 us (46%)
  starting transfers between devices  18 us (32%)
  Pallas kernels  5.95 us (10%)
  matrix products  4.15 us (7%)
  local copies, waits for them, and re-layouts  0.96 us (2%)
  other arithmetic  0.81 us (1%)
  between operations  0.76 us (1%)
    ppermute x17, waiting for transfers between devices, exchange(): return lax.ppermute(value, ('sp', 'ep'), pairs)  26.2 us
    ppermute x17, starting transfers between devices, exchange(): return lax.ppermute(value, ('sp', 'ep'), pairs)  18 us
    dot_general x1, matrix products, dense(): weight_grad = jnp.dot(hidden_t, scaled, preferred_element_type=F32)  4.15 us
    pallas_call x1, Pallas kernels, dense(): pl.pallas_call(functools.partial(backward_kernel, n, width), out_shape=(j...  3.76 us
    pallas_call x1, Pallas kernels, dense(): pl.pallas_call(functools.partial(forward_kernel, n), out_shape=(jax.Shape...  1.22 us
  transfers between devices with their start and end apart: 17, of which 9 were waited for; matrix products, arithmetic and copies ran while one was open for 7% of the time, Pallas kernels for 2%

profile of v3, /device:TPU:0, one launch (start us, length us, event | category | flops | bytes accessed | tf_op | source)
XLA Modules:
  0.0 56.9 jit_solution(16941920966246446143)
XLA Ops:
  0.6 0.9 %pack.1.refs_0_ = bf16[8,3712]{1,0:T(8,128)(2,1)S(1)} custom-call(bf16[1,4,3584]{2,1,0:T(4,128)(2,1)} %in_ref.1, bf16[1,4,3584]{2,1,0:T(4,128)(2,1)} %grad_ref.1, bf16[1,4,8]{2,1,0:T(4,128)(2,1)} %weight_ref.1, s32[1,4,8]{2,1,0:T(4,128)} %ids_ref.1), custom_call_target="tpu_custom_call" | custom-call | flops 1000000 | tf_op jit(solution)/shard_map/pack/pallas_call | solution.py:140
  1.6 5.1 %collective-permute-start.2 = (bf16[8,3712]{1,0:T(8,128)(2,1)S(1)}, bf16[8,3712]{1,0:T(8,128)(2,1)S(1)}, u32[]{:S(2)}, u32[]{:S(2)}) collective-permute-start(bf16[8,3712]{1,0:T(8,128)(2,1)S(1)} %pack.1.refs_0_), channel_id=1, source_target_pairs={{0,12},{1,13},{2,14},{3,15},{4,8},{5,9},{6,10},{7,11},{8,4},{9,5},... | collective-permute-start | bytes 178184 | tf_op jit(solution)/shard_map/ppermute | solution.py:106
  6.7 0.6 %collective-permute-start = (bf16[8,3712]{1,0:T(8,128)(2,1)S(1)}, bf16[8,3712]{1,0:T(8,128)(2,1)S(1)}, u32[]{:S(2)}, u32[]{:S(2)}) collective-permute-start(bf16[8,3712]{1,0:T(8,128)(2,1)S(1)} %pack.1.refs_0_), channel_id=1, source_target_pairs={{0,4},{1,5},{2,6},{3,7},{4,0},{5,1},{6,2},{7,3},{8,12},{9,13},{10,... | collective-permute-start | bytes 178184 | tf_op jit(solution)/shard_map/ppermute | solution.py:106
  7.4 1.7 %collective-permute-done.2.refs_3_ = bf16[8,3712]{1,0:T(8,128)(2,1)S(1)} collective-permute-done((bf16[8,3712]{1,0:T(8,128)(2,1)S(1)}, bf16[8,3712]{1,0:T(8,128)(2,1)S(1)}, u32[]{:S(2)}, u32[]{:S(2)}) %collective-permute-start.2) | collective-permute-done | bytes 59424 | tf_op jit(solution)/shard_map/ppermute | solution.py:106
  9.1 2.8 %collective-permute-done.1.refs_2_ = bf16[8,3712]{1,0:T(8,128)(2,1)S(1)} collective-permute-done((bf16[8,3712]{1,0:T(8,128)(2,1)S(1)}, bf16[8,3712]{1,0:T(8,128)(2,1)S(1)}, u32[]{:S(2)}, u32[]{:S(2)}) %collective-permute-start.1) | collective-permute-done | bytes 59424 | tf_op jit(solution)/shard_map/ppermute | solution.py:106
  11.9 1.7 %collective-permute-start.7 = (bf16[16,3584]{1,0:T(8,128)(2,1)S(1)}, bf16[16,3584]{1,0:T(8,128)(2,1)S(1)}, u32[]{:S(2)}, u32[]{:S(2)}) collective-permute-start(bf16[16,3584]{1,0:T(8,128)(2,1)S(1)} %get-tuple-element.10), channel_id=1, source_target_pairs={{0,2},{1,17},{2,0},{3,19},{4,6},{5,21},{6,4},{7,23},{8,10},{9,25},... | collective-permute-start | bytes 344072 | tf_op jit(solution)/shard_map/ppermute | solution.py:106
  14.1 4.4 %collective-permute-done.3 = bf16[16,3712]{1,0:T(8,128)(2,1)S(1)} collective-permute-done((bf16[16,3712]{1,0:T(8,128)(2,1)S(1)}, bf16[16,3712]{1,0:T(8,128)(2,1)S(1)}, u32[]{:S(2)}, u32[]{:S(2)}) %collective-permute-start.3) | collective-permute-done | bytes 118816 | tf_op jit(solution)/shard_map/ppermute | solution.py:106
  18.6 1.6 %collective-permute-start.4 = (bf16[32,3712]{1,0:T(8,128)(2,1)S(1)}, bf16[32,3712]{1,0:T(8,128)(2,1)S(1)}, u32[]{:S(2)}, u32[]{:S(2)}) collective-permute-start(bf16[32,3712]{1,0:T(8,128)(2,1)S(1)} %constant_dynamic-update-slice_fusion.refs_0_), channel_id=1, source_target_pairs={{0,16},{1,3},{2,18},{3,1},{4,20},{5,7},{6,22},{7,5},{8,24},{9,11},... | collective-permute-start | bytes 712712 | tf_op jit(solution)/shard_map/ppermute | solution.py:106
  20.1 0.6 %collective-permute-start.8 = (bf16[32,3584]{1,0:T(8,128)(2,1)S(1)}, bf16[32,3584]{1,0:T(8,128)(2,1)S(1)}, u32[]{:S(2)}, u32[]{:S(2)}) collective-permute-start(bf16[32,3584]{1,0:T(8,128)(2,1)S(1)} %constant_dynamic-update-slice_fusion.2.refs_0_), channel_id=1, source_target_pairs={{0,16},{1,3},{2,18},{3,1},{4,20},{5,7},{6,22},{7,5},{8,24},{9,11},... | collective-permute-start | bytes 688136 | tf_op jit(solution)/shard_map/ppermute | solution.py:106
  20.7 4.0 %collective-permute-done.4.refs_1_ = bf16[32,3712]{1,0:T(8,128)(2,1)S(1)} collective-permute-done((bf16[32,3712]{1,0:T(8,128)(2,1)S(1)}, bf16[32,3712]{1,0:T(8,128)(2,1)S(1)}, u32[]{:S(2)}, u32[]{:S(2)}) %collective-permute-start.4) | collective-permute-done | bytes 237600 | tf_op jit(solution)/shard_map/ppermute | solution.py:106
  25.2 1.9 %collective-permute-done.8.refs_1_ = bf16[32,3584]{1,0:T(8,128)(2,1)S(1)} collective-permute-done((bf16[32,3584]{1,0:T(8,128)(2,1)S(1)}, bf16[32,3584]{1,0:T(8,128)(2,1)S(1)}, u32[]{:S(2)}, u32[]{:S(2)}) %collective-permute-start.8) | collective-permute-done | bytes 229408 | tf_op jit(solution)/shard_map/ppermute | solution.py:106
  27.2 1.5 %collective-permute-done.10.refs_3_ = bf16[32,3584]{1,0:T(8,128)(2,1)S(1)} collective-permute-done((bf16[32,3584]{1,0:T(8,128)(2,1)S(1)}, bf16[32,3584]{1,0:T(8,128)(2,1)S(1)}, u32[]{:S(2)}, u32[]{:S(2)}) %collective-permute-start.10) | collective-permute-done | bytes 229408 | tf_op jit(solution)/shard_map/ppermute | solution.py:106
  28.7 1.2 %forward.1 = (f32[128,512]{1,0:T(8,128)S(1)}, f32[128,512]{1,0:T(8,128)S(1)}, bf16[512,128]{1,0:T(8,128)(2,1)S(1)}) custom-call(bf16[32,3584]{1,0:T(8,128)(2,1)S(1)} %constant_dynamic-update-slice_fusion.2.refs_0_, bf16[32,3584]{1,0:T(8,128)(2,1)S(1)} %collective-permute-done.8.refs_1_, bf16[32,3584]{1,0:T(8,128)(2,1)S(1)} %collective-permute-done.9.refs_2_, ...), custom_call_target="tpu_custom_call" | custom-call | flops 1000000 | tf_op jit(solution)/shard_map/forward/pallas_call | solution.py:250
  29.9 0.8 %copy-done.2 = bf16[1,512,3584]{2,1,0:T(8,128)(2,1)S(1)} copy-done((bf16[1,512,3584]{2,1,0:T(8,128)(2,1)S(1)}, bf16[1,512,3584]{2,1,0:T(8,128)(2,1)}, u32[]{:S(2)}) %copy-start.2) | copy-done | bytes 3670040
  30.7 3.8 %backward.1 = (bf16[128,3584]{1,0:T(8,128)(2,1)S(1)}, bf16[128,3584]{1,0:T(8,128)(2,1)S(1)}) custom-call(bf16[32,3712]{1,0:T(8,128)(2,1)S(1)} %constant_dynamic-update-slice_fusion.refs_0_, bf16[32,3712]{1,0:T(8,128)(2,1)S(1)} %collective-permute-done.4.refs_1_, bf16[32,3712]{1,0:T(8,128)(2,1)S(1)} %collective-permute-done.5.refs_2_, ...), custom_call_target="tpu_custom_call" | custom-call | flops 1000000 | tf_op jit(solution)/shard_map/backward/pallas_call | solution.py:263
  34.7 1.7 %collective-permute-done.11 = bf16[64,3584]{1,0:T(8,128)(2,1)S(1)} collective-permute-done((bf16[64,3584]{1,0:T(8,128)(2,1)S(1)}, bf16[64,3584]{1,0:T(8,128)(2,1)S(1)}, u32[]{:S(2)}, u32[]{:S(2)}) %collective-permute-start.11) | collective-permute-done | bytes 458784 | tf_op jit(solution)/shard_map/ppermute | solution.py:106
  36.5 1.6 %collective-permute-start.12 = (bf16[32,3584]{1,0:T(8,128)(2,1)S(1)}, bf16[32,3584]{1,0:T(8,128)(2,1)S(1)}, u32[]{:S(2)}, u32[]{:S(2)}) collective-permute-start(bf16[32,3584]{1,0:T(8,128)(2,1)S(1)} %slice.64), channel_id=1, source_target_pairs={{0,16},{1,3},{2,18},{3,1},{4,20},{5,7},{6,22},{7,5},{8,24},{9,11},... | collective-permute-start | bytes 688136 | tf_op jit(solution)/shard_map/ppermute | solution.py:106
  38.1 4.5 %collective-permute-done.12 = bf16[32,3584]{1,0:T(8,128)(2,1)S(1)} collective-permute-done((bf16[32,3584]{1,0:T(8,128)(2,1)S(1)}, bf16[32,3584]{1,0:T(8,128)(2,1)S(1)}, u32[]{:S(2)}, u32[]{:S(2)}) %collective-permute-start.12) | collective-permute-done | bytes 229408 | tf_op jit(solution)/shard_map/ppermute | solution.py:106
  42.7 1.2 %collective-permute-start.13 = (bf16[16,3584]{1,0:T(8,128)(2,1)S(1)}, bf16[16,3584]{1,0:T(8,128)(2,1)S(1)}, u32[]{:S(2)}, u32[]{:S(2)}) collective-permute-start(bf16[16,3584]{1,0:T(8,128)(2,1)S(1)} %slice.65), channel_id=1, source_target_pairs={{0,2},{1,17},{2,0},{3,19},{4,6},{5,21},{6,4},{7,23},{8,10},{9,25},... | collective-permute-start | bytes 344072 | tf_op jit(solution)/shard_map/ppermute | solution.py:106
  43.9 3.6 %collective-permute-done.13 = bf16[16,3584]{1,0:T(8,128)(2,1)S(1)} collective-permute-done((bf16[16,3584]{1,0:T(8,128)(2,1)S(1)}, bf16[16,3584]{1,0:T(8,128)(2,1)S(1)}, u32[]{:S(2)}, u32[]{:S(2)}) %collective-permute-start.13) | collective-permute-done | bytes 114720 | tf_op jit(solution)/shard_map/ppermute | solution.py:106
  47.6 2.7 %collective-permute-start.14 = (bf16[4,3584]{1,0:T(4,128)(2,1)S(1)}, bf16[4,3584]{1,0:T(4,128)(2,1)S(1)}, u32[]{:S(2)}, u32[]{:S(2)}) collective-permute-start(bf16[4,3584]{1,0:T(4,128)(2,1)S(1)} %get-tuple-element.18), channel_id=1, source_target_pairs={{0,12},{1,13},{2,14},{3,15},{4,8},{5,9},{6,10},{7,11},{8,4},{9,5},... | collective-permute-start | bytes 86024 | tf_op jit(solution)/shard_map/ppermute | solution.py:106
  50.3 1.8 %collective-permute-start.15 = (bf16[4,3584]{1,0:T(4,128)(2,1)S(1)}, bf16[4,3584]{1,0:T(4,128)(2,1)S(1)}, u32[]{:S(2)}, u32[]{:S(2)}) collective-permute-start(bf16[4,3584]{1,0:T(4,128)(2,1)S(1)} %get-tuple-element.20), channel_id=1, source_target_pairs={{0,8},{1,9},{2,10},{3,11},{4,12},{5,13},{6,14},{7,15},{8,0},{9,1},... | collective-permute-start | bytes 86024 | tf_op jit(solution)/shard_map/ppermute | solution.py:106
  52.1 4.1 %convolution_bitcast_fusion = f32[1,512,3584]{2,1,0:T(8,128)} fusion(bf16[512,128]{1,0:T(8,128)(2,1)S(1)} %get-tuple-element.14, bf16[128,3584]{1,0:T(8,128)(2,1)S(1)} %get-tuple-element.15), kind=kOutput, calls=%fused_computation | convolution fusion | flops 469762048 | bytes 8388608 | tf_op jit(solution)/shard_map/dot_general | solution.py:275
  56.3 0.6 %fusion.3 = bf16[1,4,3584]{2,1,0:T(4,128)(2,1)} fusion(bf16[4,3584]{1,0:T(4,128)(2,1)S(1)} %collective-permute-done.16, bf16[4,3584]{1,0:T(4,128)(2,1)S(1)} %collective-permute-done.15, bf16[4,3584]{1,0:T(4,128)(2,1)S(1)} %collective-permute-done.14, f32[16,3584]{1,0:T(8,128)S(1)} %get-tuple-element.17), kind=kLoop, calls=%fused_computation.10 | loop fusion | flops 100352 | bytes 172032 | tf_op jit(solution)/shard_map/broadcast_in_dim | solution.py:287
  (33 shorter events, 1.6 us)
Async XLA Ops:
  1.6 27.1 %copy-start = (bf16[1,3584,512]{2,1,0:T(8,128)(2,1)S(1)}, bf16[1,3584,512]{2,1,0:T(8,128)(2,1)}, u32[]{:S(2)}) copy-start(bf16[1,3584,512]{2,1,0:T(8,128)(2,1)} %param.11) | copy-start | bytes 11010052
  1.6 27.1 %copy-start.1 = (bf16[1,3584,512]{2,1,0:T(8,128)(2,1)S(1)}, bf16[1,3584,512]{2,1,0:T(8,128)(2,1)}, u32[]{:S(2)}) copy-start(bf16[1,3584,512]{2,1,0:T(8,128)(2,1)} %param.12) | copy-start | bytes 11010052
  1.6 7.5 %collective-permute-start.2 = (bf16[8,3712]{1,0:T(8,128)(2,1)S(1)}, bf16[8,3712]{1,0:T(8,128)(2,1)S(1)}, u32[]{:S(2)}, u32[]{:S(2)}) collective-permute-start(bf16[8,3712]{1,0:T(8,128)(2,1)S(1)} %pack.1.refs_0_), channel_id=1, source_target_pairs={{0,12},{1,13},{2,14},{3,15},{4,8},{5,9},{6,10},{7,11},{8,4},{9,5},... | collective-permute-start | bytes 178184 | tf_op jit(solution)/shard_map/ppermute | solution.py:106
  6.7 5.2 %collective-permute-start.1 = (bf16[8,3712]{1,0:T(8,128)(2,1)S(1)}, bf16[8,3712]{1,0:T(8,128)(2,1)S(1)}, u32[]{:S(2)}, u32[]{:S(2)}) collective-permute-start(bf16[8,3712]{1,0:T(8,128)(2,1)S(1)} %pack.1.refs_0_), channel_id=1, source_target_pairs={{0,8},{1,9},{2,10},{3,11},{4,12},{5,13},{6,14},{7,15},{8,0},{9,1},... | collective-permute-start | bytes 178184 | tf_op jit(solution)/shard_map/ppermute | solution.py:106
  6.7 5.2 %collective-permute-start = (bf16[8,3712]{1,0:T(8,128)(2,1)S(1)}, bf16[8,3712]{1,0:T(8,128)(2,1)S(1)}, u32[]{:S(2)}, u32[]{:S(2)}) collective-permute-start(bf16[8,3712]{1,0:T(8,128)(2,1)S(1)} %pack.1.refs_0_), channel_id=1, source_target_pairs={{0,4},{1,5},{2,6},{3,7},{4,0},{5,1},{6,2},{7,3},{8,12},{9,13},{10,... | collective-permute-start | bytes 178184 | tf_op jit(solution)/shard_map/ppermute | solution.py:106
  11.9 8.2 %collective-permute-start.7 = (bf16[16,3584]{1,0:T(8,128)(2,1)S(1)}, bf16[16,3584]{1,0:T(8,128)(2,1)S(1)}, u32[]{:S(2)}, u32[]{:S(2)}) collective-permute-start(bf16[16,3584]{1,0:T(8,128)(2,1)S(1)} %get-tuple-element.10), channel_id=1, source_target_pairs={{0,2},{1,17},{2,0},{3,19},{4,6},{5,21},{6,4},{7,23},{8,10},{9,25},... | collective-permute-start | bytes 344072 | tf_op jit(solution)/shard_map/ppermute | solution.py:106
  13.6 4.9 %collective-permute-start.3 = (bf16[16,3712]{1,0:T(8,128)(2,1)S(1)}, bf16[16,3712]{1,0:T(8,128)(2,1)S(1)}, u32[]{:S(2)}, u32[]{:S(2)}) collective-permute-start(bf16[16,3712]{1,0:T(8,128)(2,1)S(1)} %get-tuple-element.9), channel_id=1, source_target_pairs={{0,2},{1,17},{2,0},{3,19},{4,6},{5,21},{6,4},{7,23},{8,10},{9,25},... | collective-permute-start | bytes 356360 | tf_op jit(solution)/shard_map/ppermute | solution.py:106
  18.6 6.2 %collective-permute-start.4 = (bf16[32,3712]{1,0:T(8,128)(2,1)S(1)}, bf16[32,3712]{1,0:T(8,128)(2,1)S(1)}, u32[]{:S(2)}, u32[]{:S(2)}) collective-permute-start(bf16[32,3712]{1,0:T(8,128)(2,1)S(1)} %constant_dynamic-update-slice_fusion.refs_0_), channel_id=1, source_target_pairs={{0,16},{1,3},{2,18},{3,1},{4,20},{5,7},{6,22},{7,5},{8,24},{9,11},... | collective-permute-start | bytes 712712 | tf_op jit(solution)/shard_map/ppermute | solution.py:106
  20.1 7.1 %collective-permute-start.8 = (bf16[32,3584]{1,0:T(8,128)(2,1)S(1)}, bf16[32,3584]{1,0:T(8,128)(2,1)S(1)}, u32[]{:S(2)}, u32[]{:S(2)}) collective-permute-start(bf16[32,3584]{1,0:T(8,128)(2,1)S(1)} %constant_dynamic-update-slice_fusion.2.refs_0_), channel_id=1, source_target_pairs={{0,16},{1,3},{2,18},{3,1},{4,20},{5,7},{6,22},{7,5},{8,24},{9,11},... | collective-permute-start | bytes 688136 | tf_op jit(solution)/shard_map/ppermute | solution.py:106
  20.7 9.2 %collective-permute-start.5 = (bf16[32,3712]{1,0:T(8,128)(2,1)S(1)}, bf16[32,3712]{1,0:T(8,128)(2,1)S(1)}, u32[]{:S(2)}, u32[]{:S(2)}) collective-permute-start(bf16[32,3712]{1,0:T(8,128)(2,1)S(1)} %constant_dynamic-update-slice_fusion.refs_0_), channel_id=1, source_target_pairs={{0,1},{1,0},{2,3},{3,2},{4,5},{5,4},{6,7},{7,6},{8,9},{9,8},{10,11... | collective-permute-start | bytes 712712 | tf_op jit(solution)/shard_map/ppermute | solution.py:106
  24.7 5.2 %collective-permute-start.6 = (bf16[32,3712]{1,0:T(8,128)(2,1)S(1)}, bf16[32,3712]{1,0:T(8,128)(2,1)S(1)}, u32[]{:S(2)}, u32[]{:S(2)}) collective-permute-start(bf16[32,3712]{1,0:T(8,128)(2,1)S(1)} %collective-permute-done.4.refs_1_), channel_id=1, source_target_pairs={{0,1},{1,0},{2,3},{3,2},{4,5},{5,4},{6,7},{7,6},{8,9},{9,8},{10,11... | collective-permute-start | bytes 712712 | tf_op jit(solution)/shard_map/ppermute | solution.py:106
  24.7 2.5 %collective-permute-start.9 = (bf16[32,3584]{1,0:T(8,128)(2,1)S(1)}, bf16[32,3584]{1,0:T(8,128)(2,1)S(1)}, u32[]{:S(2)}, u32[]{:S(2)}) collective-permute-start(bf16[32,3584]{1,0:T(8,128)(2,1)S(1)} %constant_dynamic-update-slice_fusion.2.refs_0_), channel_id=1, source_target_pairs={{0,1},{1,0},{2,3},{3,2},{4,5},{5,4},{6,7},{7,6},{8,9},{9,8},{10,11... | collective-permute-start | bytes 688136 | tf_op jit(solution)/shard_map/ppermute | solution.py:106
  27.2 1.5 %collective-permute-start.10 = (bf16[32,3584]{1,0:T(8,128)(2,1)S(1)}, bf16[32,3584]{1,0:T(8,128)(2,1)S(1)}, u32[]{:S(2)}, u32[]{:S(2)}) collective-permute-start(bf16[32,3584]{1,0:T(8,128)(2,1)S(1)} %collective-permute-done.8.refs_1_), channel_id=1, source_target_pairs={{0,1},{1,0},{2,3},{3,2},{4,5},{5,4},{6,7},{7,6},{8,9},{9,8},{10,11... | collective-permute-start | bytes 688136 | tf_op jit(solution)/shard_map/ppermute | solution.py:106
  28.7 2.0 %copy-start.2 = (bf16[1,512,3584]{2,1,0:T(8,128)(2,1)S(1)}, bf16[1,512,3584]{2,1,0:T(8,128)(2,1)}, u32[]{:S(2)}) copy-start(bf16[1,512,3584]{2,1,0:T(8,128)(2,1)} %param.13) | copy-start | bytes 11010052
  34.5 1.9 %collective-permute-start.11 = (bf16[64,3584]{1,0:T(8,128)(2,1)S(1)}, bf16[64,3584]{1,0:T(8,128)(2,1)S(1)}, u32[]{:S(2)}, u32[]{:S(2)}) collective-permute-start(bf16[64,3584]{1,0:T(8,128)(2,1)S(1)} %slice.33), channel_id=1, source_target_pairs={{0,1},{1,0},{2,3},{3,2},{4,5},{5,4},{6,7},{7,6},{8,9},{9,8},{10,11... | collective-permute-start | bytes 1376264 | tf_op jit(solution)/shard_map/ppermute | solution.py:106
  36.5 6.1 %collective-permute-start.12 = (bf16[32,3584]{1,0:T(8,128)(2,1)S(1)}, bf16[32,3584]{1,0:T(8,128)(2,1)S(1)}, u32[]{:S(2)}, u32[]{:S(2)}) collective-permute-start(bf16[32,3584]{1,0:T(8,128)(2,1)S(1)} %slice.64), channel_id=1, source_target_pairs={{0,16},{1,3},{2,18},{3,1},{4,20},{5,7},{6,22},{7,5},{8,24},{9,11},... | collective-permute-start | bytes 688136 | tf_op jit(solution)/shard_map/ppermute | solution.py:106
  42.7 4.9 %collective-permute-start.13 = (bf16[16,3584]{1,0:T(8,128)(2,1)S(1)}, bf16[16,3584]{1,0:T(8,128)(2,1)S(1)}, u32[]{:S(2)}, u32[]{:S(2)}) collective-permute-start(bf16[16,3584]{1,0:T(8,128)(2,1)S(1)} %slice.65), channel_id=1, source_target_pairs={{0,2},{1,17},{2,0},{3,19},{4,6},{5,21},{6,4},{7,23},{8,10},{9,25},... | collective-permute-start | bytes 344072 | tf_op jit(solution)/shard_map/ppermute | solution.py:106
  47.6 8.6 %collective-permute-start.14 = (bf16[4,3584]{1,0:T(4,128)(2,1)S(1)}, bf16[4,3584]{1,0:T(4,128)(2,1)S(1)}, u32[]{:S(2)}, u32[]{:S(2)}) collective-permute-start(bf16[4,3584]{1,0:T(4,128)(2,1)S(1)} %get-tuple-element.18), channel_id=1, source_target_pairs={{0,12},{1,13},{2,14},{3,15},{4,8},{5,9},{6,10},{7,11},{8,4},{9,5},... | collective-permute-start | bytes 86024 | tf_op jit(solution)/shard_map/ppermute | solution.py:106
  50.3 5.9 %collective-permute-start.16 = (bf16[4,3584]{1,0:T(4,128)(2,1)S(1)}, bf16[4,3584]{1,0:T(4,128)(2,1)S(1)}, u32[]{:S(2)}, u32[]{:S(2)}) collective-permute-start(bf16[4,3584]{1,0:T(4,128)(2,1)S(1)} %get-tuple-element.19), channel_id=1, source_target_pairs={{0,4},{1,5},{2,6},{3,7},{4,0},{5,1},{6,2},{7,3},{8,12},{9,13},{10,... | collective-permute-start | bytes 86024 | tf_op jit(solution)/shard_map/ppermute | solution.py:106
  50.3 5.9 %collective-permute-start.15 = (bf16[4,3584]{1,0:T(4,128)(2,1)S(1)}, bf16[4,3584]{1,0:T(4,128)(2,1)S(1)}, u32[]{:S(2)}, u32[]{:S(2)}) collective-permute-start(bf16[4,3584]{1,0:T(4,128)(2,1)S(1)} %get-tuple-element.20), channel_id=1, source_target_pairs={{0,8},{1,9},{2,10},{3,11},{4,12},{5,13},{6,14},{7,15},{8,0},{9,1},... | collective-permute-start | bytes 86024 | tf_op jit(solution)/shard_map/ppermute | solution.py:106

commit v4 on v3

--- a/solution.py
+++ b/solution.py
@@ -8,6 +8,7 @@
 from jax.sharding import PartitionSpec as P
 
 TOP = 8
+TURN = 512
 F32 = jnp.float32
 BF16 = jnp.bfloat16
 
@@ -99,6 +100,10 @@
     )
     own_sum = lax.psum_scatter(token_sum.astype(BF16), "sp", scatter_dimension=0, tiled=True)
     return (own_sum.reshape(1, tok_dev, width), weight_grad[None])
+
+
+def back_order(far):
+    return far[:1] + far[-1:] + far[1:-1] if len(far) > 1 else far
 
 
 def exchange(value, partner, n_sp, n_ep):
@@ -149,7 +154,7 @@
             pltpu.SemaphoreType.DMA((4,)),
         ],
         compiler_params=room(2),
-        cost_estimate=QUICK,
+        cost_estimate=BUSY,
         name="pack",
     )(*(pltpu.with_memory_space_constraint(x, pltpu.HBM) for x in operands))
 
@@ -175,9 +180,29 @@
         in_specs=[WHOLE] * len(blocks),
         out_specs=(WHOLE,) * 2,
         compiler_params=room(2),
-        cost_estimate=BUSY,
+        cost_estimate=QUICK,
         name="stack",
     )(*blocks)
+
+
+def turn_kernel(n, *refs):
+    for source, target in zip(refs[:n], refs[n:]):
+        for c in range(0, source.shape[0], TURN):
+            rows = slice(c, min(c + TURN, source.shape[0]))
+            target[:, rows] = source[rows, :].T
+
+
+def turn(*weights):
+    n = len(weights)
+    return pl.pallas_call(
+        functools.partial(turn_kernel, n),
+        out_shape=[jax.ShapeDtypeStruct(w.shape[::-1], w.dtype) for w in weights],
+        in_specs=[WHOLE] * n,
+        out_specs=[WHOLE] * n,
+        compiler_params=room(16),
+        cost_estimate=QUICK,
+        name="turn",
+    )(*weights)
 
 
 def forward_kernel(n, *refs):
@@ -195,8 +220,21 @@
         hidden_t[cols, :] = (swish * up_pre).T.astype(BF16)
 
 
+def part_columns(gate_grad, up_grad, gate_t, up_t, offset, own, other):
+    rows, width = own.shape
+    step = 256 if width % 256 == 0 else width
+    for c in range(0, width, step):
+        cols = slice(offset + c, offset + c + step)
+        first = jnp.dot(gate_grad, gate_t[:, cols], preferred_element_type=F32)
+        second = jnp.dot(up_grad, up_t[:, cols], preferred_element_type=F32)
+        part = (first + second).astype(BF16)
+        own[:, c : c + step] = part[:rows]
+        other[:, c : c + step] = part[rows:]
+
+
 def backward_kernel(n, width, *refs):
-    pieces, (down_w, gate_w, up_w, gate_by, up_by, part, scaled) = refs[:n], refs[n:]
+    pieces, refs = refs[:n], refs[n:]
+    down_t, gate_t, up_t, gate_by, up_by, own, other, scaled, gate_grad, up_grad = refs
     expert = lax.axis_index("ep")
     start = 0
     for piece in pieces:
@@ -206,16 +244,83 @@
         rows = slice(start, start + piece.shape[0])
         scaled[rows, :] = (weight * piece[:, :width].astype(F32)).astype(BF16)
         start += piece.shape[0]
-    nt = (((1,), (1,)), ((), ()))
-    hidden_grad = lax.dot_general(scaled[...], down_w[...], nt, preferred_element_type=F32)
-    gate_grad = (hidden_grad * gate_by[...]).astype(BF16)
-    up_grad = (hidden_grad * up_by[...]).astype(BF16)
-    step = 512 if width % 512 == 0 else width
-    for c in range(0, width, step):
-        cols = slice(c, c + step)
-        first = lax.dot_general(gate_grad, gate_w[cols, :], nt, preferred_element_type=F32)
-        second = lax.dot_general(up_grad, up_w[cols, :], nt, preferred_element_type=F32)
-        part[:, cols] = (first + second).astype(BF16)
+    hidden_grad = jnp.dot(scaled[...], down_t[...], preferred_element_type=F32)
+    gates = (hidden_grad * gate_by[...]).astype(BF16)
+    ups = (hidden_grad * up_by[...]).astype(BF16)
+    gate_grad[...] = gates
+    up_grad[...] = ups
+    part_columns(gates, ups, gate_t, up_t, 0, own, other)
+
+
+def backward(pieces, down_t, gate_t, up_t, gate_by, up_by):
+    n = len(pieces)
+    rows, units = gate_by.shape
+    width = down_t.shape[0]
+    half = jax.ShapeDtypeStruct((rows // 2, width // 2), BF16)
+    return pl.pallas_call(
+        functools.partial(backward_kernel, n, width),
+        out_shape=(
+            half,
+            half,
+            jax.ShapeDtypeStruct((rows, width), BF16),
+            jax.ShapeDtypeStruct((rows, units), BF16),
+            jax.ShapeDtypeStruct((rows, units), BF16),
+        ),
+        in_specs=[WHOLE] * (n + 5),
+        out_specs=(WHOLE,) * 5,
+        compiler_params=room(24),
+        cost_estimate=QUICK,
+        name="backward",
+    )(*pieces, down_t, gate_t, up_t, gate_by, up_by)
+
+
+def right_kernel(gate_grad, up_grad, gate_t, up_t, own, other):
+    part_columns(gate_grad[...], up_grad[...], gate_t, up_t, own.shape[1], own, other)
+
+
+def right_half(gate_grad, up_grad, gate_t, up_t):
+    half = jax.ShapeDtypeStruct((gate_grad.shape[0] // 2, gate_t.shape[1] // 2), BF16)
+    return pl.pallas_call(
+        right_kernel,
+        out_shape=(half, half),
+        in_specs=[WHOLE] * 4,
+        out_specs=(WHOLE,) * 2,
+        compiler_params=room(16),
+        cost_estimate=QUICK,
+        name="right",
+    )(gate_grad, up_grad, gate_t, up_t)
+
+
+def outer_kernel(first, hidden_t, scaled, *refs):
+    out, buffer, sem = refs[-3:]
+    chunks, size = buffer.shape[:2]
+    copies = []
+    for n in range(chunks):
+        rows = pl.ds((first * chunks + n) * size, size)
+        buffer[n] = jnp.dot(hidden_t[rows, :], scaled[...], preferred_element_type=F32)
+        copies.append(pltpu.make_async_copy(buffer.at[n], out.at[rows], sem.at[n]))
+        copies[-1].start()
+    for copy in copies:
+        copy.wait()
+
+
+def outer(first, hidden_t, scaled, *so_far):
+    units, width = hidden_t.shape[0], scaled.shape[1]
+    chunks = 4
+    return pl.pallas_call(
+        functools.partial(outer_kernel, first),
+        out_shape=pltpu.HBM((units, width), F32),
+        in_specs=[WHOLE] * 2 + [pl.BlockSpec(memory_space=pltpu.HBM)] * len(so_far),
+        out_specs=pl.BlockSpec(memory_space=pltpu.HBM),
+        scratch_shapes=[
+            pltpu.VMEM((chunks, units // 2 // chunks, width), F32),
+            pltpu.SemaphoreType.DMA((chunks,)),
+        ],
+        input_output_aliases={2: 0} if so_far else {},
+        compiler_params=room(12),
+        cost_estimate=QUICK,
+        name="outer",
+    )(hidden_t, scaled, *so_far)
 
 
 def dense(activations, out_grad, route_weights, expert_ids, w_gate, w_up, w_down):
@@ -243,7 +348,9 @@
     column_in, column_grad = stack([mine] + [blocks[j] for j in sorted(far)], width)
     rows_in = gather(column_in)
     rows_grad = gather(column_grad)
-    gate_w, up_w, down_w = w_gate[0], w_up[0], w_down[0]
+    gate_w, up_w = w_gate[0], w_up[0]
+    gate_t, up_t = turn(gate_w, up_w)
+    (down_t,) = turn(w_down[0])
     rows = sum(piece.shape[0] for piece in rows_in)
     n = len(rows_in)
 
@@ -260,28 +367,24 @@
         cost_estimate=QUICK,
         name="forward",
     )(*rows_in, gate_w, up_w)
-    part, scaled = pl.pallas_call(
-        functools.partial(backward_kernel, n, width),
-        out_shape=(
-            jax.ShapeDtypeStruct((rows, width), BF16),
-            jax.ShapeDtypeStruct((rows, width), BF16),
-        ),
-        in_specs=[WHOLE] * (n + 5),
-        out_specs=(WHOLE,) * 2,
-        compiler_params=room(24),
-        cost_estimate=QUICK,
-        name="backward",
-    )(*rows_grad, down_w, gate_w, up_w, gate_by, up_by)
-    weight_grad = jnp.dot(hidden_t, scaled, preferred_element_type=F32)
-
-    total = part
-    for partner in (core, two, one):
-        half = total.shape[0] // 2
-        got = swap(total[half:].astype(BF16), partner)
-        total = total[:half].astype(F32) + got.astype(F32)
+    own_left, other_left, scaled, gate_grad, up_grad = backward(
+        rows_grad, down_t, gate_t, up_t, gate_by, up_by
+    )
+    own_right, other_right = right_half(gate_grad, up_grad, gate_t, up_t)
+    owns = (own_left, own_right)
+    got = [swap(x, core) for x in (other_left, other_right)]
+    weight_grad = outer(0, hidden_t, scaled)
+    weight_grad = outer(1, hidden_t, scaled, weight_grad)
+
+    totals = [a.astype(F32) + b.astype(F32) for a, b in zip(owns, got)]
+    for partner in (two, one):
+        half = totals[0].shape[0] // 2
+        got = [swap(x[half:].astype(BF16), partner) for x in totals]
+        totals = [x[:half].astype(F32) + y.astype(F32) for x, y in zip(totals, got)]
+    total = jnp.concatenate(totals, axis=1)
     sent = total.astype(BF16)
     own = total[:tok_dev]
-    for j in far:
+    for j in back_order(far):
         block = sent[j // 4 * tok_dev : (j // 4 + 1) * tok_dev]
         own = own + swap(block, lambda i, j=j: i ^ j).astype(F32)
     return (own.astype(BF16)[None], weight_grad[None])

time: 57.1 us -> 57.3 us (level)
  Pallas kernels: 5.95 us -> 11.6 us
  waiting for transfers between devices: 26.2 us -> 20.9 us
  matrix products: 4.15 us -> 0 us
  starting transfers between devices: 18 us -> 20.7 us
  local copies, waits for them, and re-layouts: 0.96 us -> 2.28 us
    pallas_call x1 -> x6, Pallas kernels: 3.76 us -> 9.28 us  [the longest x2 4.27 us: outer(): pl.pallas_call(functools.partial(outer_kernel, first), out_shape=pltpu.HB...]
    ppermute x17 -> x20, waiting for transfers between devices: 26.2 us -> 20.9 us  [exchange(): return lax.ppermute(value, ('sp', 'ep'), pairs)]
    dot_general x1 -> x0, matrix products: 4.15 us -> none  [dense(): weight_grad = jnp.dot(hidden_t, scaled, preferred_element_type=F32)]
    ppermute x17 -> x20, starting transfers between devices: 18 us -> 20.7 us  [exchange(): return lax.ppermute(value, ('sp', 'ep'), pairs)]
    unnamed x8, local copies, waits for them, and re-layouts: 0.83 us -> 2.17 us
  transfers between devices with their start and end apart: 17 -> 20, of which waited for: 9 -> 10; matrix products, arithmetic and copies ran while one was open for 7% -> 0% of each run, Pallas kernels for 2% -> 16%
where the time goes in v4:
time: 57.3 us; the launch traced here: 57.2 us
  waiting for transfers between devices  20.9 us (36%)
  starting transfers between devices  20.7 us (36%)
  Pallas kernels  11.6 us (20%)
  local copies, waits for them, and re-layouts  2.28 us (4%)
  between operations  0.86 us (2%)
  other arithmetic  0.83 us (1%)
    ppermute x20, waiting for transfers between devices, exchange(): return lax.ppermute(value, ('sp', 'ep'), pairs)  20.9 us
    ppermute x20, starting transfers between devices, exchange(): return lax.ppermute(value, ('sp', 'ep'), pairs)  20.7 us
    pallas_call x2, Pallas kernels, outer(): pl.pallas_call(functools.partial(outer_kernel, first), out_shape=pltpu.HB...  4.27 us
    pallas_call x2, Pallas kernels, turn(): pl.pallas_call(functools.partial(turn_kernel, n), out_shape=[jax.ShapeDty...  2.93 us
    unnamed x8, local copies, waits for them, and re-layouts  2.17 us
    pallas_call x1, Pallas kernels, backward(): pl.pallas_call(functools.partial(backward_kernel, n, width), out_shape=(h...  1.43 us
    pallas_call x1, Pallas kernels, dense(): pl.pallas_call(functools.partial(forward_kernel, n), out_shape=(jax.Shape...  1.22 us
  transfers between devices with their start and end apart: 20, of which 10 were waited for; matrix products, arithmetic and copies ran while one was open for 0% of the time, Pallas kernels for 16%

profile of v4, /device:TPU:0, one launch (start us, length us, event | category | flops | bytes accessed | tf_op | source)
XLA Modules:
  0.0 57.2 jit_solution(8769260908493341470)
XLA Ops:
  0.6 1.1 %pack.1.refs_0_ = bf16[8,3712]{1,0:T(8,128)(2,1)S(1)} custom-call(bf16[1,4,3584]{2,1,0:T(4,128)(2,1)} %in_ref.1, bf16[1,4,3584]{2,1,0:T(4,128)(2,1)} %grad_ref.1, bf16[1,4,8]{2,1,0:T(4,128)(2,1)} %weight_ref.1, s32[1,4,8]{2,1,0:T(4,128)} %ids_ref.1), custom_call_target="tpu_custom_call" | custom-call | flops 10000000000 | tf_op jit(solution)/shard_map/pack/pallas_call | solution.py:145
  1.7 5.1 %collective-permute-start.2 = (bf16[8,3712]{1,0:T(8,128)(2,1)S(1)}, bf16[8,3712]{1,0:T(8,128)(2,1)S(1)}, u32[]{:S(2)}, u32[]{:S(2)}) collective-permute-start(bf16[8,3712]{1,0:T(8,128)(2,1)S(1)} %pack.1.refs_0_), channel_id=1, source_target_pairs={{0,12},{1,13},{2,14},{3,15},{4,8},{5,9},{6,10},{7,11},{8,4},{9,5},... | collective-permute-start | bytes 178184 | tf_op jit(solution)/shard_map/ppermute | solution.py:111
  7.5 1.7 %collective-permute-done.2.refs_3_ = bf16[8,3712]{1,0:T(8,128)(2,1)S(1)} collective-permute-done((bf16[8,3712]{1,0:T(8,128)(2,1)S(1)}, bf16[8,3712]{1,0:T(8,128)(2,1)S(1)}, u32[]{:S(2)}, u32[]{:S(2)}) %collective-permute-start.2) | collective-permute-done | bytes 59424 | tf_op jit(solution)/shard_map/ppermute | solution.py:111
  9.2 2.8 %collective-permute-done.1.refs_2_ = bf16[8,3712]{1,0:T(8,128)(2,1)S(1)} collective-permute-done((bf16[8,3712]{1,0:T(8,128)(2,1)S(1)}, bf16[8,3712]{1,0:T(8,128)(2,1)S(1)}, u32[]{:S(2)}, u32[]{:S(2)}) %collective-permute-start.1) | collective-permute-done | bytes 59424 | tf_op jit(solution)/shard_map/ppermute | solution.py:111
  12.1 1.7 %collective-permute-start.7 = (bf16[16,3584]{1,0:T(8,128)(2,1)S(1)}, bf16[16,3584]{1,0:T(8,128)(2,1)S(1)}, u32[]{:S(2)}, u32[]{:S(2)}) collective-permute-start(bf16[16,3584]{1,0:T(8,128)(2,1)S(1)} %get-tuple-element.19), channel_id=1, source_target_pairs={{0,2},{1,17},{2,0},{3,19},{4,6},{5,21},{6,4},{7,23},{8,10},{9,25},... | collective-permute-start | bytes 344072 | tf_op jit(solution)/shard_map/ppermute | solution.py:111
  14.3 4.4 %collective-permute-done.3 = bf16[16,3712]{1,0:T(8,128)(2,1)S(1)} collective-permute-done((bf16[16,3712]{1,0:T(8,128)(2,1)S(1)}, bf16[16,3712]{1,0:T(8,128)(2,1)S(1)}, u32[]{:S(2)}, u32[]{:S(2)}) %collective-permute-start.3) | collective-permute-done | bytes 118816 | tf_op jit(solution)/shard_map/ppermute | solution.py:111
  18.7 1.6 %collective-permute-start.4 = (bf16[32,3712]{1,0:T(8,128)(2,1)S(1)}, bf16[32,3712]{1,0:T(8,128)(2,1)S(1)}, u32[]{:S(2)}, u32[]{:S(2)}) collective-permute-start(bf16[32,3712]{1,0:T(8,128)(2,1)S(1)} %constant_dynamic-update-slice_fusion.refs_0_), channel_id=1, source_target_pairs={{0,16},{1,3},{2,18},{3,1},{4,20},{5,7},{6,22},{7,5},{8,24},{9,11},... | collective-permute-start | bytes 712712 | tf_op jit(solution)/shard_map/ppermute | solution.py:111
  20.9 4.0 %collective-permute-done.4.refs_1_ = bf16[32,3712]{1,0:T(8,128)(2,1)S(1)} collective-permute-done((bf16[32,3712]{1,0:T(8,128)(2,1)S(1)}, bf16[32,3712]{1,0:T(8,128)(2,1)S(1)}, u32[]{:S(2)}, u32[]{:S(2)}) %collective-permute-start.4) | collective-permute-done | bytes 237600 | tf_op jit(solution)/shard_map/ppermute | solution.py:111
  25.4 1.9 %collective-permute-done.8.refs_1_ = bf16[32,3584]{1,0:T(8,128)(2,1)S(1)} collective-permute-done((bf16[32,3584]{1,0:T(8,128)(2,1)S(1)}, bf16[32,3584]{1,0:T(8,128)(2,1)S(1)}, u32[]{:S(2)}, u32[]{:S(2)}) %collective-permute-start.8) | collective-permute-done | bytes 229408 | tf_op jit(solution)/shard_map/ppermute | solution.py:111
  28.3 1.0 %copy-done = bf16[1,3584,512]{2,1,0:T(8,128)(2,1)S(1)} copy-done((bf16[1,3584,512]{2,1,0:T(8,128)(2,1)S(1)}, bf16[1,3584,512]{2,1,0:T(8,128)(2,1)}, u32[]{:S(2)}) %copy-start) | copy-done | bytes 3670040
  29.4 1.1 %copy-done.1 = bf16[1,3584,512]{2,1,0:T(8,128)(2,1)S(1)} copy-done((bf16[1,3584,512]{2,1,0:T(8,128)(2,1)S(1)}, bf16[1,3584,512]{2,1,0:T(8,128)(2,1)}, u32[]{:S(2)}) %copy-start.1) | copy-done | bytes 3670040
  30.5 1.9 %turn.3 = (bf16[512,3584]{1,0:T(8,128)(2,1)S(1)}, bf16[512,3584]{1,0:T(8,128)(2,1)S(1)}) custom-call(bf16[3584,512]{1,0:T(8,128)(2,1)S(1)} %bitcast.6, bf16[3584,512]{1,0:T(8,128)(2,1)S(1)} %bitcast.8), custom_call_target="tpu_custom_call" | custom-call | flops 1000000 | tf_op jit(solution)/shard_map/turn/pallas_call | solution.py:197
  32.5 1.2 %forward.1 = (f32[128,512]{1,0:T(8,128)S(1)}, f32[128,512]{1,0:T(8,128)S(1)}, bf16[512,128]{1,0:T(8,128)(2,1)S(1)}) custom-call(bf16[32,3584]{1,0:T(8,128)(2,1)S(1)} %constant_dynamic-update-slice_fusion.2.refs_0_, bf16[32,3584]{1,0:T(8,128)(2,1)S(1)} %collective-permute-done.8.refs_1_, bf16[32,3584]{1,0:T(8,128)(2,1)S(1)} %collective-permute-done.9.refs_2_, ...), custom_call_target="tpu_custom_call" | custom-call | flops 1000000 | tf_op jit(solution)/shard_map/forward/pallas_call | solution.py:357
  33.7 1.4 %backward.1 = (bf16[64,1792]{1,0:T(8,128)(2,1)S(1)}, bf16[64,1792]{1,0:T(8,128)(2,1)S(1)}, bf16[128,3584]{1,0:T(8,128)(2,1)S(1)}, bf16[128,512]{1,0:T(8,128)(2,1)S(1)}, bf16[128,512]{1,0:T(8,128)(2,1)S(1)}) custom-call(bf16[32,3712]{1,0:T(8,128)(2,1)S(1)} %constant_dynamic-update-slice_fusion.refs_0_, bf16[32,3712]{1,0:T(8,128)(2,1)S(1)} %collective-permute-done.4.refs_1_, ...), custom_call_target="tpu_custom_call" | custom-call | flops 1000000 | tf_op jit(solution)/shard_map/backward/pallas_call | solution.py:260
  36.9 1.5 %collective-permute-start.12 = (bf16[32,1792]{1,0:T(8,128)(2,1)S(1)}, bf16[32,1792]{1,0:T(8,128)(2,1)S(1)}, u32[]{:S(2)}, u32[]{:S(2)}) collective-permute-start(bf16[32,1792]{1,0:T(8,128)(2,1)S(1)} %slice.94), channel_id=1, source_target_pairs={{0,16},{1,3},{2,18},{3,1},{4,20},{5,7},{6,22},{7,5},{8,24},{9,11},... | collective-permute-start | bytes 344072 | tf_op jit(solution)/shard_map/ppermute | solution.py:111
  39.5 2.2 %collective-permute-done.12 = bf16[32,1792]{1,0:T(8,128)(2,1)S(1)} collective-permute-done((bf16[32,1792]{1,0:T(8,128)(2,1)S(1)}, bf16[32,1792]{1,0:T(8,128)(2,1)S(1)}, u32[]{:S(2)}, u32[]{:S(2)}) %collective-permute-start.12) | collective-permute-done | bytes 114720 | tf_op jit(solution)/shard_map/ppermute | solution.py:111
  41.8 1.2 %collective-permute-start.13 = (bf16[16,1792]{1,0:T(8,128)(2,1)S(1)}, bf16[16,1792]{1,0:T(8,128)(2,1)S(1)}, u32[]{:S(2)}, u32[]{:S(2)}) collective-permute-start(bf16[16,1792]{1,0:T(8,128)(2,1)S(1)} %slice.96), channel_id=1, source_target_pairs={{0,2},{1,17},{2,0},{3,19},{4,6},{5,21},{6,4},{7,23},{8,10},{9,25},... | collective-permute-start | bytes 172040 | tf_op jit(solution)/shard_map/ppermute | solution.py:111
  43.4 1.2 %collective-permute-start.16 = (bf16[16,1792]{1,0:T(8,128)(2,1)S(1)}, bf16[16,1792]{1,0:T(8,128)(2,1)S(1)}, u32[]{:S(2)}, u32[]{:S(2)}) collective-permute-start(bf16[16,1792]{1,0:T(8,128)(2,1)S(1)} %slice.95), channel_id=1, source_target_pairs={{0,2},{1,17},{2,0},{3,19},{4,6},{5,21},{6,4},{7,23},{8,10},{9,25},... | collective-permute-start | bytes 172040 | tf_op jit(solution)/shard_map/ppermute | solution.py:111
  44.6 1.4 %collective-permute-done.13 = bf16[16,1792]{1,0:T(8,128)(2,1)S(1)} collective-permute-done((bf16[16,1792]{1,0:T(8,128)(2,1)S(1)}, bf16[16,1792]{1,0:T(8,128)(2,1)S(1)}, u32[]{:S(2)}, u32[]{:S(2)}) %collective-permute-start.13) | collective-permute-done | bytes 57376 | tf_op jit(solution)/shard_map/ppermute | solution.py:111
  46.1 1.6 %collective-permute-done.16 = bf16[16,1792]{1,0:T(8,128)(2,1)S(1)} collective-permute-done((bf16[16,1792]{1,0:T(8,128)(2,1)S(1)}, bf16[16,1792]{1,0:T(8,128)(2,1)S(1)}, u32[]{:S(2)}, u32[]{:S(2)}) %collective-permute-start.16) | collective-permute-done | bytes 57376 | tf_op jit(solution)/shard_map/ppermute | solution.py:111
  47.8 2.7 %collective-permute-start.17 = (bf16[4,3584]{1,0:T(4,128)(2,1)S(1)}, bf16[4,3584]{1,0:T(4,128)(2,1)S(1)}, u32[]{:S(2)}, u32[]{:S(2)}) collective-permute-start(bf16[4,3584]{1,0:T(4,128)(2,1)S(1)} %get-tuple-element.30), channel_id=1, source_target_pairs={{0,12},{1,13},{2,14},{3,15},{4,8},{5,9},{6,10},{7,11},{8,4},{9,5},... | collective-permute-start | bytes 86024 | tf_op jit(solution)/shard_map/ppermute | solution.py:111
  50.4 1.8 %collective-permute-start.18 = (bf16[4,3584]{1,0:T(4,128)(2,1)S(1)}, bf16[4,3584]{1,0:T(4,128)(2,1)S(1)}, u32[]{:S(2)}, u32[]{:S(2)}) collective-permute-start(bf16[4,3584]{1,0:T(4,128)(2,1)S(1)} %get-tuple-element.32), channel_id=1, source_target_pairs={{0,4},{1,5},{2,6},{3,7},{4,0},{5,1},{6,2},{7,3},{8,12},{9,13},{10,... | collective-permute-start | bytes 86024 | tf_op jit(solution)/shard_map/ppermute | solution.py:111
  52.2 2.1 %outer.2.refs_0_ = f32[512,3584]{1,0:T(8,128)} custom-call(bf16[512,128]{1,0:T(8,128)(2,1)S(1)} %get-tuple-element.28.hidden_t, bf16[128,3584]{1,0:T(8,128)(2,1)S(1)} %get-tuple-element.29.scaled), custom_call_target="tpu_custom_call" | custom-call | flops 1000000 | tf_op jit(solution)/shard_map/outer/pallas_call | solution.py:310
  54.3 2.1 %outer.3 = f32[512,3584]{1,0:T(8,128)} custom-call(bf16[512,128]{1,0:T(8,128)(2,1)S(1)} %get-tuple-element.28.hidden_t, bf16[128,3584]{1,0:T(8,128)(2,1)S(1)} %get-tuple-element.29.scaled, f32[512,3584]{1,0:T(8,128)} %outer.2.refs_0_), custom_call_target="tpu_custom_call", output_to_operand_aliasing={{}: (2, {})} | custom-call | flops 1000000 | tf_op jit(solution)/shard_map/outer/pallas_call | solution.py:310
  (48 shorter events, 7.3 us)
Async XLA Ops:
  0.6 26.7 %copy-start.2 = (bf16[1,512,3584]{2,1,0:T(8,128)(2,1)S(1)}, bf16[1,512,3584]{2,1,0:T(8,128)(2,1)}, u32[]{:S(2)}) copy-start(bf16[1,512,3584]{2,1,0:T(8,128)(2,1)} %param.13) | copy-start | bytes 11010052
  1.7 7.5 %collective-permute-start.2 = (bf16[8,3712]{1,0:T(8,128)(2,1)S(1)}, bf16[8,3712]{1,0:T(8,128)(2,1)S(1)}, u32[]{:S(2)}, u32[]{:S(2)}) collective-permute-start(bf16[8,3712]{1,0:T(8,128)(2,1)S(1)} %pack.1.refs_0_), channel_id=1, source_target_pairs={{0,12},{1,13},{2,14},{3,15},{4,8},{5,9},{6,10},{7,11},{8,4},{9,5},... | collective-permute-start | bytes 178184 | tf_op jit(solution)/shard_map/ppermute | solution.py:111
  6.9 5.2 %collective-permute-start.1 = (bf16[8,3712]{1,0:T(8,128)(2,1)S(1)}, bf16[8,3712]{1,0:T(8,128)(2,1)S(1)}, u32[]{:S(2)}, u32[]{:S(2)}) collective-permute-start(bf16[8,3712]{1,0:T(8,128)(2,1)S(1)} %pack.1.refs_0_), channel_id=1, source_target_pairs={{0,8},{1,9},{2,10},{3,11},{4,12},{5,13},{6,14},{7,15},{8,0},{9,1},... | collective-permute-start | bytes 178184 | tf_op jit(solution)/shard_map/ppermute | solution.py:111
  6.9 5.2 %collective-permute-start = (bf16[8,3712]{1,0:T(8,128)(2,1)S(1)}, bf16[8,3712]{1,0:T(8,128)(2,1)S(1)}, u32[]{:S(2)}, u32[]{:S(2)}) collective-permute-start(bf16[8,3712]{1,0:T(8,128)(2,1)S(1)} %pack.1.refs_0_), channel_id=1, source_target_pairs={{0,4},{1,5},{2,6},{3,7},{4,0},{5,1},{6,2},{7,3},{8,12},{9,13},{10,... | collective-permute-start | bytes 178184 | tf_op jit(solution)/shard_map/ppermute | solution.py:111
  12.1 8.2 %collective-permute-start.7 = (bf16[16,3584]{1,0:T(8,128)(2,1)S(1)}, bf16[16,3584]{1,0:T(8,128)(2,1)S(1)}, u32[]{:S(2)}, u32[]{:S(2)}) collective-permute-start(bf16[16,3584]{1,0:T(8,128)(2,1)S(1)} %get-tuple-element.19), channel_id=1, source_target_pairs={{0,2},{1,17},{2,0},{3,19},{4,6},{5,21},{6,4},{7,23},{8,10},{9,25},... | collective-permute-start | bytes 344072 | tf_op jit(solution)/shard_map/ppermute | solution.py:111
  13.8 4.9 %collective-permute-start.3 = (bf16[16,3712]{1,0:T(8,128)(2,1)S(1)}, bf16[16,3712]{1,0:T(8,128)(2,1)S(1)}, u32[]{:S(2)}, u32[]{:S(2)}) collective-permute-start(bf16[16,3712]{1,0:T(8,128)(2,1)S(1)} %get-tuple-element.16), channel_id=1, source_target_pairs={{0,2},{1,17},{2,0},{3,19},{4,6},{5,21},{6,4},{7,23},{8,10},{9,25},... | collective-permute-start | bytes 356360 | tf_op jit(solution)/shard_map/ppermute | solution.py:111
  18.7 6.2 %collective-permute-start.4 = (bf16[32,3712]{1,0:T(8,128)(2,1)S(1)}, bf16[32,3712]{1,0:T(8,128)(2,1)S(1)}, u32[]{:S(2)}, u32[]{:S(2)}) collective-permute-start(bf16[32,3712]{1,0:T(8,128)(2,1)S(1)} %constant_dynamic-update-slice_fusion.refs_0_), channel_id=1, source_target_pairs={{0,16},{1,3},{2,18},{3,1},{4,20},{5,7},{6,22},{7,5},{8,24},{9,11},... | collective-permute-start | bytes 712712 | tf_op jit(solution)/shard_map/ppermute | solution.py:111
  20.3 7.1 %collective-permute-start.8 = (bf16[32,3584]{1,0:T(8,128)(2,1)S(1)}, bf16[32,3584]{1,0:T(8,128)(2,1)S(1)}, u32[]{:S(2)}, u32[]{:S(2)}) collective-permute-start(bf16[32,3584]{1,0:T(8,128)(2,1)S(1)} %constant_dynamic-update-slice_fusion.2.refs_0_), channel_id=1, source_target_pairs={{0,16},{1,3},{2,18},{3,1},{4,20},{5,7},{6,22},{7,5},{8,24},{9,11},... | collective-permute-start | bytes 688136 | tf_op jit(solution)/shard_map/ppermute | solution.py:111
  20.9 12.8 %collective-permute-start.5 = (bf16[32,3712]{1,0:T(8,128)(2,1)S(1)}, bf16[32,3712]{1,0:T(8,128)(2,1)S(1)}, u32[]{:S(2)}, u32[]{:S(2)}) collective-permute-start(bf16[32,3712]{1,0:T(8,128)(2,1)S(1)} %constant_dynamic-update-slice_fusion.refs_0_), channel_id=1, source_target_pairs={{0,1},{1,0},{2,3},{3,2},{4,5},{5,4},{6,7},{7,6},{8,9},{9,8},{10,11... | collective-permute-start | bytes 712712 | tf_op jit(solution)/shard_map/ppermute | solution.py:111
  24.9 8.8 %collective-permute-start.6 = (bf16[32,3712]{1,0:T(8,128)(2,1)S(1)}, bf16[32,3712]{1,0:T(8,128)(2,1)S(1)}, u32[]{:S(2)}, u32[]{:S(2)}) collective-permute-start(bf16[32,3712]{1,0:T(8,128)(2,1)S(1)} %collective-permute-done.4.refs_1_), channel_id=1, source_target_pairs={{0,1},{1,0},{2,3},{3,2},{4,5},{5,4},{6,7},{7,6},{8,9},{9,8},{10,11... | collective-permute-start | bytes 712712 | tf_op jit(solution)/shard_map/ppermute | solution.py:111
  24.9 7.6 %collective-permute-start.9 = (bf16[32,3584]{1,0:T(8,128)(2,1)S(1)}, bf16[32,3584]{1,0:T(8,128)(2,1)S(1)}, u32[]{:S(2)}, u32[]{:S(2)}) collective-permute-start(bf16[32,3584]{1,0:T(8,128)(2,1)S(1)} %constant_dynamic-update-slice_fusion.2.refs_0_), channel_id=1, source_target_pairs={{0,1},{1,0},{2,3},{3,2},{4,5},{5,4},{6,7},{7,6},{8,9},{9,8},{10,11... | collective-permute-start | bytes 688136 | tf_op jit(solution)/shard_map/ppermute | solution.py:111
  27.3 5.1 %collective-permute-start.10 = (bf16[32,3584]{1,0:T(8,128)(2,1)S(1)}, bf16[32,3584]{1,0:T(8,128)(2,1)S(1)}, u32[]{:S(2)}, u32[]{:S(2)}) collective-permute-start(bf16[32,3584]{1,0:T(8,128)(2,1)S(1)} %collective-permute-done.8.refs_1_), channel_id=1, source_target_pairs={{0,1},{1,0},{2,3},{3,2},{4,5},{5,4},{6,7},{7,6},{8,9},{9,8},{10,11... | collective-permute-start | bytes 688136 | tf_op jit(solution)/shard_map/ppermute | solution.py:111
  27.3 2.0 %copy-start = (bf16[1,3584,512]{2,1,0:T(8,128)(2,1)S(1)}, bf16[1,3584,512]{2,1,0:T(8,128)(2,1)}, u32[]{:S(2)}) copy-start(bf16[1,3584,512]{2,1,0:T(8,128)(2,1)} %param.11) | copy-start | bytes 11010052
  27.3 3.2 %copy-start.1 = (bf16[1,3584,512]{2,1,0:T(8,128)(2,1)S(1)}, bf16[1,3584,512]{2,1,0:T(8,128)(2,1)}, u32[]{:S(2)}) copy-start(bf16[1,3584,512]{2,1,0:T(8,128)(2,1)} %param.12) | copy-start | bytes 11010052
  35.1 1.7 %collective-permute-start.11 = (bf16[64,1792]{1,0:T(8,128)(2,1)S(1)}, bf16[64,1792]{1,0:T(8,128)(2,1)S(1)}, u32[]{:S(2)}, u32[]{:S(2)}) collective-permute-start(bf16[64,1792]{1,0:T(8,128)(2,1)S(1)} %get-tuple-element.23), channel_id=1, source_target_pairs={{0,1},{1,0},{2,3},{3,2},{4,5},{5,4},{6,7},{7,6},{8,9},{9,8},{10,11... | collective-permute-start | bytes 688136 | tf_op jit(solution)/shard_map/ppermute | solution.py:111
  36.4 2.1 %collective-permute-start.14 = (bf16[64,1792]{1,0:T(8,128)(2,1)S(1)}, bf16[64,1792]{1,0:T(8,128)(2,1)S(1)}, u32[]{:S(2)}, u32[]{:S(2)}) collective-permute-start(bf16[64,1792]{1,0:T(8,128)(2,1)S(1)} %get-tuple-element.27), channel_id=1, source_target_pairs={{0,1},{1,0},{2,3},{3,2},{4,5},{5,4},{6,7},{7,6},{8,9},{9,8},{10,11... | collective-permute-start | bytes 688136 | tf_op jit(solution)/shard_map/ppermute | solution.py:111
  36.9 4.9 %collective-permute-start.12 = (bf16[32,1792]{1,0:T(8,128)(2,1)S(1)}, bf16[32,1792]{1,0:T(8,128)(2,1)S(1)}, u32[]{:S(2)}, u32[]{:S(2)}) collective-permute-start(bf16[32,1792]{1,0:T(8,128)(2,1)S(1)} %slice.94), channel_id=1, source_target_pairs={{0,16},{1,3},{2,18},{3,1},{4,20},{5,7},{6,22},{7,5},{8,24},{9,11},... | collective-permute-start | bytes 344072 | tf_op jit(solution)/shard_map/ppermute | solution.py:111
  38.5 4.9 %collective-permute-start.15 = (bf16[32,1792]{1,0:T(8,128)(2,1)S(1)}, bf16[32,1792]{1,0:T(8,128)(2,1)S(1)}, u32[]{:S(2)}, u32[]{:S(2)}) collective-permute-start(bf16[32,1792]{1,0:T(8,128)(2,1)S(1)} %slice.93), channel_id=1, source_target_pairs={{0,16},{1,3},{2,18},{3,1},{4,20},{5,7},{6,22},{7,5},{8,24},{9,11},... | collective-permute-start | bytes 344072 | tf_op jit(solution)/shard_map/ppermute | solution.py:111
  41.8 4.2 %collective-permute-start.13 = (bf16[16,1792]{1,0:T(8,128)(2,1)S(1)}, bf16[16,1792]{1,0:T(8,128)(2,1)S(1)}, u32[]{:S(2)}, u32[]{:S(2)}) collective-permute-start(bf16[16,1792]{1,0:T(8,128)(2,1)S(1)} %slice.96), channel_id=1, source_target_pairs={{0,2},{1,17},{2,0},{3,19},{4,6},{5,21},{6,4},{7,23},{8,10},{9,25},... | collective-permute-start | bytes 172040 | tf_op jit(solution)/shard_map/ppermute | solution.py:111
  43.4 4.2 %collective-permute-start.16 = (bf16[16,1792]{1,0:T(8,128)(2,1)S(1)}, bf16[16,1792]{1,0:T(8,128)(2,1)S(1)}, u32[]{:S(2)}, u32[]{:S(2)}) collective-permute-start(bf16[16,1792]{1,0:T(8,128)(2,1)S(1)} %slice.95), channel_id=1, source_target_pairs={{0,2},{1,17},{2,0},{3,19},{4,6},{5,21},{6,4},{7,23},{8,10},{9,25},... | collective-permute-start | bytes 172040 | tf_op jit(solution)/shard_map/ppermute | solution.py:111
  47.8 8.7 %collective-permute-start.17 = (bf16[4,3584]{1,0:T(4,128)(2,1)S(1)}, bf16[4,3584]{1,0:T(4,128)(2,1)S(1)}, u32[]{:S(2)}, u32[]{:S(2)}) collective-permute-start(bf16[4,3584]{1,0:T(4,128)(2,1)S(1)} %get-tuple-element.30), channel_id=1, source_target_pairs={{0,12},{1,13},{2,14},{3,15},{4,8},{5,9},{6,10},{7,11},{8,4},{9,5},... | collective-permute-start | bytes 86024 | tf_op jit(solution)/shard_map/ppermute | solution.py:111
  50.4 6.1 %collective-permute-start.19 = (bf16[4,3584]{1,0:T(4,128)(2,1)S(1)}, bf16[4,3584]{1,0:T(4,128)(2,1)S(1)}, u32[]{:S(2)}, u32[]{:S(2)}) collective-permute-start(bf16[4,3584]{1,0:T(4,128)(2,1)S(1)} %get-tuple-element.31), channel_id=1, source_target_pairs={{0,8},{1,9},{2,10},{3,11},{4,12},{5,13},{6,14},{7,15},{8,0},{9,1},... | collective-permute-start | bytes 86024 | tf_op jit(solution)/shard_map/ppermute | solution.py:111
  50.4 6.1 %collective-permute-start.18 = (bf16[4,3584]{1,0:T(4,128)(2,1)S(1)}, bf16[4,3584]{1,0:T(4,128)(2,1)S(1)}, u32[]{:S(2)}, u32[]{:S(2)}) collective-permute-start(bf16[4,3584]{1,0:T(4,128)(2,1)S(1)} %get-tuple-element.32), channel_id=1, source_target_pairs={{0,4},{1,5},{2,6},{3,7},{4,0},{5,1},{6,2},{7,3},{8,12},{9,13},{10,... | collective-permute-start | bytes 86024 | tf_op jit(solution)/shard_map/ppermute | solution.py:111

commit v5 on v4

--- a/solution.py
+++ b/solution.py
@@ -159,30 +159,61 @@
     )(*(pltpu.with_memory_space_constraint(x, pltpu.HBM) for x in operands))
 
 
-def stack_kernel(*refs):
+def split_kernel(*refs):
     in_ref, grad_ref = refs[-2:]
-    rows, width = refs[0].shape[0] // 2, in_ref.shape[1]
+    _, rows, width = in_ref.shape
     for n, ref in enumerate(refs[:-2]):
-        block = slice(n * rows, (n + 1) * rows)
-        in_ref[block, :] = ref[:rows, :width]
-        grad_ref[block, :] = ref[rows:, :]
-
-
-def stack(blocks, width):
+        in_ref[n] = ref[:rows, :width]
+        grad_ref[n] = ref[rows:, :]
+
+
+def split(blocks, width):
     rows, wide = blocks[0].shape
-    rows = len(blocks) * rows // 2
-    return pl.pallas_call(
-        stack_kernel,
+    n, rows = len(blocks), rows // 2
+    return pl.pallas_call(
+        split_kernel,
         out_shape=(
-            jax.ShapeDtypeStruct((rows, width), BF16),
-            jax.ShapeDtypeStruct((rows, wide), BF16),
+            jax.ShapeDtypeStruct((n, rows, width), BF16),
+            jax.ShapeDtypeStruct((n, rows, wide), BF16),
         ),
-        in_specs=[WHOLE] * len(blocks),
+        in_specs=[WHOLE] * n,
         out_specs=(WHOLE,) * 2,
         compiler_params=room(2),
         cost_estimate=QUICK,
-        name="stack",
+        name="split",
     )(*blocks)
+
+
+def place(near, away, skip, rows):
+    tok_dev, width = away[0].shape[1], rows.shape[1]
+    start = 0
+    for block, others in zip(near, away):
+        pack_rows = block.shape[0] // 2
+        per = others.shape[0] // 2
+        for p in range(2):
+            first = p * pack_rows + skip
+            rows[start : start + tok_dev, :] = block[first : first + tok_dev, :width]
+            start += tok_dev
+            for n in range(per):
+                rows[start : start + tok_dev, :] = others[p * per + n]
+                start += tok_dev
+
+
+def lay_kernel(n, *refs):
+    place(refs[:n], refs[n : 2 * n], 0, refs[2 * n])
+
+
+def lay(near, away, rows):
+    n = len(near)
+    return pl.pallas_call(
+        functools.partial(lay_kernel, n),
+        out_shape=jax.ShapeDtypeStruct((rows, away[0].shape[2]), BF16),
+        in_specs=[WHOLE] * (2 * n),
+        out_specs=WHOLE,
+        compiler_params=room(4),
+        cost_estimate=QUICK,
+        name="lay",
+    )(*near, *away)
 
 
 def turn_kernel(n, *refs):
@@ -205,14 +236,12 @@
     )(*weights)
 
 
-def forward_kernel(n, *refs):
-    pieces, (gate_w, up_w, gate_by, up_by, hidden_t) = refs[:n], refs[n:]
-    rows = jnp.concatenate([piece[...] for piece in pieces], axis=0)
+def forward_kernel(rows, gate_w, up_w, gate_by, up_by, hidden_t):
     step = min(256, gate_w.shape[1])
     for c in range(0, gate_w.shape[1], step):
         cols = slice(c, c + step)
-        gate_pre = jnp.dot(rows, gate_w[:, cols], preferred_element_type=F32)
-        up_pre = jnp.dot(rows, up_w[:, cols], preferred_element_type=F32)
+        gate_pre = jnp.dot(rows[...], gate_w[:, cols], preferred_element_type=F32)
+        up_pre = jnp.dot(rows[...], up_w[:, cols], preferred_element_type=F32)
         squash = jax.nn.sigmoid(gate_pre)
         swish = gate_pre * squash
         gate_by[:, cols] = up_pre * squash * (1.0 + gate_pre * (1.0 - squash))
@@ -233,17 +262,14 @@
 
 
 def backward_kernel(n, width, *refs):
-    pieces, refs = refs[:n], refs[n:]
-    down_t, gate_t, up_t, gate_by, up_by, own, other, scaled, gate_grad, up_grad = refs
+    near, away, refs = refs[:n], refs[n : 2 * n], refs[2 * n :]
+    down_t, gate_t, up_t, gate_by, up_by, own, other, scaled, gate_grad, up_grad, placed = refs
+    place(near, away, away[0].shape[1], placed)
     expert = lax.axis_index("ep")
-    start = 0
-    for piece in pieces:
-        spread = piece[:, width:].astype(F32)
-        lane = lax.broadcasted_iota(jnp.int32, spread.shape, 1)
-        weight = jnp.sum(jnp.where(lane == expert, spread, 0.0), axis=1, keepdims=True)
-        rows = slice(start, start + piece.shape[0])
-        scaled[rows, :] = (weight * piece[:, :width].astype(F32)).astype(BF16)
-        start += piece.shape[0]
+    spread = placed[:, width:].astype(F32)
+    lane = lax.broadcasted_iota(jnp.int32, spread.shape, 1)
+    weight = jnp.sum(jnp.where(lane == expert, spread, 0.0), axis=1, keepdims=True)
+    scaled[...] = (weight * placed[:, :width].astype(F32)).astype(BF16)
     hidden_grad = jnp.dot(scaled[...], down_t[...], preferred_element_type=F32)
     gates = (hidden_grad * gate_by[...]).astype(BF16)
     ups = (hidden_grad * up_by[...]).astype(BF16)
@@ -252,8 +278,8 @@
     part_columns(gates, ups, gate_t, up_t, 0, own, other)
 
 
-def backward(pieces, down_t, gate_t, up_t, gate_by, up_by):
-    n = len(pieces)
+def backward(near, away, down_t, gate_t, up_t, gate_by, up_by):
+    n = len(near)
     rows, units = gate_by.shape
     width = down_t.shape[0]
     half = jax.ShapeDtypeStruct((rows // 2, width // 2), BF16)
@@ -266,12 +292,13 @@
             jax.ShapeDtypeStruct((rows, units), BF16),
             jax.ShapeDtypeStruct((rows, units), BF16),
         ),
-        in_specs=[WHOLE] * (n + 5),
+        in_specs=[WHOLE] * (2 * n + 5),
         out_specs=(WHOLE,) * 5,
+        scratch_shapes=[pltpu.VMEM((rows, away[0].shape[2]), BF16)],
         compiler_params=room(24),
         cost_estimate=QUICK,
         name="backward",
-    )(*pieces, down_t, gate_t, up_t, gate_by, up_by)
+    )(*near, *away, down_t, gate_t, up_t, gate_by, up_by)
 
 
 def right_kernel(gate_grad, up_grad, gate_t, up_t, own, other):
@@ -345,30 +372,31 @@
 
     mine = pack(activations, out_grad, route_weights, expert_ids, n_ep)
     blocks = {j: swap(mine, lambda i, j=j: i ^ j) for j in far}
-    column_in, column_grad = stack([mine] + [blocks[j] for j in sorted(far)], width)
-    rows_in = gather(column_in)
-    rows_grad = gather(column_grad)
+    near = gather(mine)
+    far_in, far_grad = split([blocks[j] for j in sorted(far)], width)
+    rows_in = gather(far_in)
+    rows_grad = gather(far_grad)
     gate_w, up_w = w_gate[0], w_up[0]
     gate_t, up_t = turn(gate_w, up_w)
     (down_t,) = turn(w_down[0])
-    rows = sum(piece.shape[0] for piece in rows_in)
-    n = len(rows_in)
+    rows = tok_dev * n_ep * n_sp
+    placed = lay(near, rows_in, rows)
 
     gate_by, up_by, hidden_t = pl.pallas_call(
-        functools.partial(forward_kernel, n),
+        forward_kernel,
         out_shape=(
             jax.ShapeDtypeStruct((rows, units), F32),
             jax.ShapeDtypeStruct((rows, units), F32),
             jax.ShapeDtypeStruct((units, rows), BF16),
         ),
-        in_specs=[WHOLE] * (n + 2),
+        in_specs=[WHOLE] * 3,
         out_specs=(WHOLE,) * 3,
         compiler_params=room(16),
         cost_estimate=QUICK,
         name="forward",
-    )(*rows_in, gate_w, up_w)
+    )(placed, gate_w, up_w)
     own_left, other_left, scaled, gate_grad, up_grad = backward(
-        rows_grad, down_t, gate_t, up_t, gate_by, up_by
+        near, rows_grad, down_t, gate_t, up_t, gate_by, up_by
     )
     own_right, other_right = right_half(gate_grad, up_grad, gate_t, up_t)
     owns = (own_left, own_right)

time: 57.3 us -> 56.3 us (0.983)
  waiting for transfers between devices: 20.9 us -> 16.2 us
  starting transfers between devices: 20.7 us -> 23.9 us
    ppermute x20 -> x24, waiting for transfers between devices: 20.9 us -> 16.2 us  [exchange(): return lax.ppermute(value, ('sp', 'ep'), pairs)]
    ppermute x20 -> x24, starting transfers between devices: 20.7 us -> 23.9 us  [exchange(): return lax.ppermute(value, ('sp', 'ep'), pairs)]
    pallas_call x2 -> x3, Pallas kernels: 1.26 us -> 1.45 us  [the longest x1 1.22 us: dense(): pl.pallas_call(forward_kernel, out_shape=(jax.ShapeDtypeStruct((rows, uni...]
  transfers between devices with their start and end apart: 20 -> 24, of which waited for: 10 -> 10; matrix products, arithmetic and copies ran while one was open for 0% -> 1% of each run, Pallas kernels for 16% -> 17%
where the time goes in v5:
time: 56.3 us; the launch traced here: 56.1 us
  starting transfers between devices  23.9 us (42%)
  waiting for transfers between devices  16.2 us (29%)
  Pallas kernels  11.9 us (21%)
  local copies, waits for them, and re-layouts  2.39 us (4%)
  between operations  0.89 us (2%)
  other arithmetic  0.84 us (1%)
    ppermute x24, starting transfers between devices, exchange(): return lax.ppermute(value, ('sp', 'ep'), pairs)  23.9 us
    ppermute x24, waiting for transfers between devices, exchange(): return lax.ppermute(value, ('sp', 'ep'), pairs)  16.2 us
    pallas_call x2, Pallas kernels, outer(): pl.pallas_call(functools.partial(outer_kernel, first), out_shape=pltpu.HB...  4.27 us
    pallas_call x2, Pallas kernels, turn(): pl.pallas_call(functools.partial(turn_kernel, n), out_shape=[jax.ShapeDty...  2.93 us
    unnamed x8, local copies, waits for them, and re-layouts  2.22 us
    pallas_call x1, Pallas kernels, backward(): pl.pallas_call(functools.partial(backward_kernel, n, width), out_shape=(h...  1.55 us
    pallas_call x1, Pallas kernels, dense(): pl.pallas_call(forward_kernel, out_shape=(jax.ShapeDtypeStruct((rows, uni...  1.22 us
  transfers between devices with their start and end apart: 24, of which 10 were waited for; matrix products, arithmetic and copies ran while one was open for 1% of the time, Pallas kernels for 17%

profile of v5, /device:TPU:0, one launch (start us, length us, event | category | flops | bytes accessed | tf_op | source)
XLA Modules:
  0.0 56.1 jit_solution(6546905913096414329)
XLA Ops:
  0.6 1.1 %pack.1 = bf16[8,3712]{1,0:T(8,128)(2,1)S(1)} custom-call(bf16[1,4,3584]{2,1,0:T(4,128)(2,1)} %in_ref.1, bf16[1,4,3584]{2,1,0:T(4,128)(2,1)} %grad_ref.1, bf16[1,4,8]{2,1,0:T(4,128)(2,1)} %weight_ref.1, s32[1,4,8]{2,1,0:T(4,128)} %ids_ref.1), custom_call_target="tpu_custom_call" | custom-call | flops 10000000000 | tf_op jit(solution)/shard_map/pack/pallas_call | solution.py:145
  1.7 5.1 %collective-permute-start.6 = (bf16[8,3712]{1,0:T(8,128)(2,1)S(1)}, bf16[8,3712]{1,0:T(8,128)(2,1)S(1)}, u32[]{:S(2)}, u32[]{:S(2)}) collective-permute-start(bf16[8,3712]{1,0:T(8,128)(2,1)S(1)} %pack.1), channel_id=1, source_target_pairs={{0,12},{1,13},{2,14},{3,15},{4,8},{5,9},{6,10},{7,11},{8,4},{9,5},... | collective-permute-start | bytes 178184 | tf_op jit(solution)/shard_map/ppermute | solution.py:111
  7.5 1.7 %collective-permute-start = (bf16[8,3712]{1,0:T(8,128)(2,1)S(1)}, bf16[8,3712]{1,0:T(8,128)(2,1)S(1)}, u32[]{:S(2)}, u32[]{:S(2)}) collective-permute-start(bf16[8,3712]{1,0:T(8,128)(2,1)S(1)} %pack.1), channel_id=1, source_target_pairs={{0,2},{1,17},{2,0},{3,19},{4,6},{5,21},{6,4},{7,23},{8,10},{9,25},... | collective-permute-start | bytes 178184 | tf_op jit(solution)/shard_map/ppermute | solution.py:111
  9.2 2.8 %collective-permute-done.5.refs_1_ = bf16[8,3712]{1,0:T(8,128)(2,1)S(1)} collective-permute-done((bf16[8,3712]{1,0:T(8,128)(2,1)S(1)}, bf16[8,3712]{1,0:T(8,128)(2,1)S(1)}, u32[]{:S(2)}, u32[]{:S(2)}) %collective-permute-start.5) | collective-permute-done | bytes 59424 | tf_op jit(solution)/shard_map/ppermute | solution.py:111
  12.1 1.7 %collective-permute-start.11 = (bf16[3,4,3584]{2,1,0:T(4,128)(2,1)S(1)}, bf16[3,4,3584]{2,1,0:T(4,128)(2,1)S(1)}, u32[]{:S(2)}, u32[]{:S(2)}) collective-permute-start(bf16[3,4,3584]{2,1,0:T(4,128)(2,1)S(1)} %get-tuple-element.19), channel_id=1, source_target_pairs={{0,2},{1,17},{2,0},{3,19},{4,6},{5,21},{6,4},{7,23},{8,10},{9,25},... | collective-permute-start | bytes 258056 | tf_op jit(solution)/shard_map/ppermute | solution.py:111
  14.3 2.3 %collective-permute-done.11 = bf16[3,4,3584]{2,1,0:T(4,128)(2,1)S(1)} collective-permute-done((bf16[3,4,3584]{2,1,0:T(4,128)(2,1)S(1)}, bf16[3,4,3584]{2,1,0:T(4,128)(2,1)S(1)}, u32[]{:S(2)}, u32[]{:S(2)}) %collective-permute-start.11) | collective-permute-done | bytes 86048 | tf_op jit(solution)/shard_map/ppermute | solution.py:111
  16.7 1.6 %collective-permute-start.12 = (bf16[6,4,3584]{2,1,0:T(4,128)(2,1)S(1)}, bf16[6,4,3584]{2,1,0:T(4,128)(2,1)S(1)}, u32[]{:S(2)}, u32[]{:S(2)}) collective-permute-start(bf16[6,4,3584]{2,1,0:T(4,128)(2,1)S(1)} %constant_dynamic-update-slice_fusion.2.refs_4_), channel_id=1, source_target_pairs={{0,16},{1,3},{2,18},{3,1},{4,20},{5,7},{6,22},{7,5},{8,24},{9,11},... | collective-permute-start | bytes 516104 | tf_op jit(solution)/shard_map/ppermute | solution.py:111
  19.1 1.6 %collective-permute-start.8 = (bf16[6,4,3712]{2,1,0:T(4,128)(2,1)S(1)}, bf16[6,4,3712]{2,1,0:T(4,128)(2,1)S(1)}, u32[]{:S(2)}, u32[]{:S(2)}) collective-permute-start(bf16[6,4,3712]{2,1,0:T(4,128)(2,1)S(1)} %constant_dynamic-update-slice_fusion.refs_4_), channel_id=1, source_target_pairs={{0,16},{1,3},{2,18},{3,1},{4,20},{5,7},{6,22},{7,5},{8,24},{9,11},... | collective-permute-start | bytes 534536 | tf_op jit(solution)/shard_map/ppermute | solution.py:111
  21.4 3.3 %collective-permute-done.8.refs_5_ = bf16[6,4,3712]{2,1,0:T(4,128)(2,1)S(1)} collective-permute-done((bf16[6,4,3712]{2,1,0:T(4,128)(2,1)S(1)}, bf16[6,4,3712]{2,1,0:T(4,128)(2,1)S(1)}, u32[]{:S(2)}, u32[]{:S(2)}) %collective-permute-start.8) | collective-permute-done | bytes 178208 | tf_op jit(solution)/shard_map/ppermute | solution.py:111
  27.0 1.0 %copy-done = bf16[1,3584,512]{2,1,0:T(8,128)(2,1)S(1)} copy-done((bf16[1,3584,512]{2,1,0:T(8,128)(2,1)S(1)}, bf16[1,3584,512]{2,1,0:T(8,128)(2,1)}, u32[]{:S(2)}) %copy-start) | copy-done | bytes 3670040
  28.0 1.1 %copy-done.1 = bf16[1,3584,512]{2,1,0:T(8,128)(2,1)S(1)} copy-done((bf16[1,3584,512]{2,1,0:T(8,128)(2,1)S(1)}, bf16[1,3584,512]{2,1,0:T(8,128)(2,1)}, u32[]{:S(2)}) %copy-start.1) | copy-done | bytes 3670040
  29.1 1.9 %turn.3 = (bf16[512,3584]{1,0:T(8,128)(2,1)S(1)}, bf16[512,3584]{1,0:T(8,128)(2,1)S(1)}) custom-call(bf16[3584,512]{1,0:T(8,128)(2,1)S(1)} %bitcast.6, bf16[3584,512]{1,0:T(8,128)(2,1)S(1)} %bitcast.8), custom_call_target="tpu_custom_call" | custom-call | flops 1000000 | tf_op jit(solution)/shard_map/turn/pallas_call | solution.py:228
  31.3 1.2 %forward.1 = (f32[128,512]{1,0:T(8,128)S(1)}, f32[128,512]{1,0:T(8,128)S(1)}, bf16[512,128]{1,0:T(8,128)(2,1)S(1)}) custom-call(bf16[128,3584]{1,0:T(8,128)(2,1)S(1)} %lay.1.rows, bf16[3584,512]{1,0:T(8,128)(2,1)S(1)} %bitcast.7, bf16[3584,512]{1,0:T(8,128)(2,1)S(1)} %bitcast.9), custom_call_target="tpu_custom_call" | custom-call | flops 1000000 | tf_op jit(solution)/shard_map/forward/pallas_call | solution.py:385
  32.5 1.6 %backward.1 = (bf16[64,1792]{1,0:T(8,128)(2,1)S(1)}, bf16[64,1792]{1,0:T(8,128)(2,1)S(1)}, bf16[128,3584]{1,0:T(8,128)(2,1)S(1)}, bf16[128,512]{1,0:T(8,128)(2,1)S(1)}, bf16[128,512]{1,0:T(8,128)(2,1)S(1)}) custom-call(bf16[16,3712]{1,0:T(8,128)(2,1)S(1)} %pad_maximum_fusion.1.refs_0_, bf16[16,3712]{1,0:T(8,128)(2,1)S(1)} %collective-permute-done.1.refs_1_, ...), custom_call_target="tpu_custom_call" | custom-call | flops 1000000 | tf_op jit(solution)/shard_map/backward/pallas_call | solution.py:286
  35.8 1.6 %collective-permute-start.16 = (bf16[32,1792]{1,0:T(8,128)(2,1)S(1)}, bf16[32,1792]{1,0:T(8,128)(2,1)S(1)}, u32[]{:S(2)}, u32[]{:S(2)}) collective-permute-start(bf16[32,1792]{1,0:T(8,128)(2,1)S(1)} %slice.94), channel_id=1, source_target_pairs={{0,16},{1,3},{2,18},{3,1},{4,20},{5,7},{6,22},{7,5},{8,24},{9,11},... | collective-permute-start | bytes 344072 | tf_op jit(solution)/shard_map/ppermute | solution.py:111
  38.5 2.2 %collective-permute-done.16 = bf16[32,1792]{1,0:T(8,128)(2,1)S(1)} collective-permute-done((bf16[32,1792]{1,0:T(8,128)(2,1)S(1)}, bf16[32,1792]{1,0:T(8,128)(2,1)S(1)}, u32[]{:S(2)}, u32[]{:S(2)}) %collective-permute-start.16) | collective-permute-done | bytes 114720 | tf_op jit(solution)/shard_map/ppermute | solution.py:111
  40.7 1.1 %collective-permute-start.17 = (bf16[16,1792]{1,0:T(8,128)(2,1)S(1)}, bf16[16,1792]{1,0:T(8,128)(2,1)S(1)}, u32[]{:S(2)}, u32[]{:S(2)}) collective-permute-start(bf16[16,1792]{1,0:T(8,128)(2,1)S(1)} %slice.96), channel_id=1, source_target_pairs={{0,2},{1,17},{2,0},{3,19},{4,6},{5,21},{6,4},{7,23},{8,10},{9,25},... | collective-permute-start | bytes 172040 | tf_op jit(solution)/shard_map/ppermute | solution.py:111
  42.4 1.1 %collective-permute-start.20 = (bf16[16,1792]{1,0:T(8,128)(2,1)S(1)}, bf16[16,1792]{1,0:T(8,128)(2,1)S(1)}, u32[]{:S(2)}, u32[]{:S(2)}) collective-permute-start(bf16[16,1792]{1,0:T(8,128)(2,1)S(1)} %slice.95), channel_id=1, source_target_pairs={{0,2},{1,17},{2,0},{3,19},{4,6},{5,21},{6,4},{7,23},{8,10},{9,25},... | collective-permute-start | bytes 172040 | tf_op jit(solution)/shard_map/ppermute | solution.py:111
  43.4 1.5 %collective-permute-done.17 = bf16[16,1792]{1,0:T(8,128)(2,1)S(1)} collective-permute-done((bf16[16,1792]{1,0:T(8,128)(2,1)S(1)}, bf16[16,1792]{1,0:T(8,128)(2,1)S(1)}, u32[]{:S(2)}, u32[]{:S(2)}) %collective-permute-start.17) | collective-permute-done | bytes 57376 | tf_op jit(solution)/shard_map/ppermute | solution.py:111
  45.0 1.6 %collective-permute-done.20 = bf16[16,1792]{1,0:T(8,128)(2,1)S(1)} collective-permute-done((bf16[16,1792]{1,0:T(8,128)(2,1)S(1)}, bf16[16,1792]{1,0:T(8,128)(2,1)S(1)}, u32[]{:S(2)}, u32[]{:S(2)}) %collective-permute-start.20) | collective-permute-done | bytes 57376 | tf_op jit(solution)/shard_map/ppermute | solution.py:111
  46.7 2.9 %collective-permute-start.21 = (bf16[4,3584]{1,0:T(4,128)(2,1)S(1)}, bf16[4,3584]{1,0:T(4,128)(2,1)S(1)}, u32[]{:S(2)}, u32[]{:S(2)}) collective-permute-start(bf16[4,3584]{1,0:T(4,128)(2,1)S(1)} %get-tuple-element.30), channel_id=1, source_target_pairs={{0,12},{1,13},{2,14},{3,15},{4,8},{5,9},{6,10},{7,11},{8,4},{9,5},... | collective-permute-start | bytes 86024 | tf_op jit(solution)/shard_map/ppermute | solution.py:111
  49.6 1.5 %collective-permute-start.22 = (bf16[4,3584]{1,0:T(4,128)(2,1)S(1)}, bf16[4,3584]{1,0:T(4,128)(2,1)S(1)}, u32[]{:S(2)}, u32[]{:S(2)}) collective-permute-start(bf16[4,3584]{1,0:T(4,128)(2,1)S(1)} %get-tuple-element.32), channel_id=1, source_target_pairs={{0,4},{1,5},{2,6},{3,7},{4,0},{5,1},{6,2},{7,3},{8,12},{9,13},{10,... | collective-permute-start | bytes 86024 | tf_op jit(solution)/shard_map/ppermute | solution.py:111
  51.1 2.1 %outer.2.refs_0_ = f32[512,3584]{1,0:T(8,128)} custom-call(bf16[512,128]{1,0:T(8,128)(2,1)S(1)} %get-tuple-element.28.hidden_t, bf16[128,3584]{1,0:T(8,128)(2,1)S(1)} %get-tuple-element.29.scaled), custom_call_target="tpu_custom_call" | custom-call | flops 1000000 | tf_op jit(solution)/shard_map/outer/pallas_call | solution.py:337
  53.3 2.1 %outer.3 = f32[512,3584]{1,0:T(8,128)} custom-call(bf16[512,128]{1,0:T(8,128)(2,1)S(1)} %get-tuple-element.28.hidden_t, bf16[128,3584]{1,0:T(8,128)(2,1)S(1)} %get-tuple-element.29.scaled, f32[512,3584]{1,0:T(8,128)} %outer.2.refs_0_), custom_call_target="tpu_custom_call", output_to_operand_aliasing={{}: (2, {})} | custom-call | flops 1000000 | tf_op jit(solution)/shard_map/outer/pallas_call | solution.py:337
  (58 shorter events, 9.4 us)
Async XLA Ops:
  1.7 7.5 %collective-permute-start.6 = (bf16[8,3712]{1,0:T(8,128)(2,1)S(1)}, bf16[8,3712]{1,0:T(8,128)(2,1)S(1)}, u32[]{:S(2)}, u32[]{:S(2)}) collective-permute-start(bf16[8,3712]{1,0:T(8,128)(2,1)S(1)} %pack.1), channel_id=1, source_target_pairs={{0,12},{1,13},{2,14},{3,15},{4,8},{5,9},{6,10},{7,11},{8,4},{9,5},... | collective-permute-start | bytes 178184 | tf_op jit(solution)/shard_map/ppermute | solution.py:111
  6.9 5.2 %collective-permute-start.5 = (bf16[8,3712]{1,0:T(8,128)(2,1)S(1)}, bf16[8,3712]{1,0:T(8,128)(2,1)S(1)}, u32[]{:S(2)}, u32[]{:S(2)}) collective-permute-start(bf16[8,3712]{1,0:T(8,128)(2,1)S(1)} %pack.1), channel_id=1, source_target_pairs={{0,8},{1,9},{2,10},{3,11},{4,12},{5,13},{6,14},{7,15},{8,0},{9,1},... | collective-permute-start | bytes 178184 | tf_op jit(solution)/shard_map/ppermute | solution.py:111
  6.9 5.2 %collective-permute-start.4 = (bf16[8,3712]{1,0:T(8,128)(2,1)S(1)}, bf16[8,3712]{1,0:T(8,128)(2,1)S(1)}, u32[]{:S(2)}, u32[]{:S(2)}) collective-permute-start(bf16[8,3712]{1,0:T(8,128)(2,1)S(1)} %pack.1), channel_id=1, source_target_pairs={{0,4},{1,5},{2,6},{3,7},{4,0},{5,1},{6,2},{7,3},{8,12},{9,13},{10,... | collective-permute-start | bytes 178184 | tf_op jit(solution)/shard_map/ppermute | solution.py:111
  7.5 13.2 %collective-permute-start = (bf16[8,3712]{1,0:T(8,128)(2,1)S(1)}, bf16[8,3712]{1,0:T(8,128)(2,1)S(1)}, u32[]{:S(2)}, u32[]{:S(2)}) collective-permute-start(bf16[8,3712]{1,0:T(8,128)(2,1)S(1)} %pack.1), channel_id=1, source_target_pairs={{0,2},{1,17},{2,0},{3,19},{4,6},{5,21},{6,4},{7,23},{8,10},{9,25},... | collective-permute-start | bytes 178184 | tf_op jit(solution)/shard_map/ppermute | solution.py:111
  12.1 4.6 %collective-permute-start.11 = (bf16[3,4,3584]{2,1,0:T(4,128)(2,1)S(1)}, bf16[3,4,3584]{2,1,0:T(4,128)(2,1)S(1)}, u32[]{:S(2)}, u32[]{:S(2)}) collective-permute-start(bf16[3,4,3584]{2,1,0:T(4,128)(2,1)S(1)} %get-tuple-element.19), channel_id=1, source_target_pairs={{0,2},{1,17},{2,0},{3,19},{4,6},{5,21},{6,4},{7,23},{8,10},{9,25},... | collective-permute-start | bytes 258056 | tf_op jit(solution)/shard_map/ppermute | solution.py:111
  13.8 5.3 %collective-permute-start.7 = (bf16[3,4,3712]{2,1,0:T(4,128)(2,1)S(1)}, bf16[3,4,3712]{2,1,0:T(4,128)(2,1)S(1)}, u32[]{:S(2)}, u32[]{:S(2)}) collective-permute-start(bf16[3,4,3712]{2,1,0:T(4,128)(2,1)S(1)} %get-tuple-element.16), channel_id=1, source_target_pairs={{0,2},{1,17},{2,0},{3,19},{4,6},{5,21},{6,4},{7,23},{8,10},{9,25},... | collective-permute-start | bytes 267272 | tf_op jit(solution)/shard_map/ppermute | solution.py:111
  16.7 8.5 %collective-permute-start.12 = (bf16[6,4,3584]{2,1,0:T(4,128)(2,1)S(1)}, bf16[6,4,3584]{2,1,0:T(4,128)(2,1)S(1)}, u32[]{:S(2)}, u32[]{:S(2)}) collective-permute-start(bf16[6,4,3584]{2,1,0:T(4,128)(2,1)S(1)} %constant_dynamic-update-slice_fusion.2.refs_4_), channel_id=1, source_target_pairs={{0,16},{1,3},{2,18},{3,1},{4,20},{5,7},{6,22},{7,5},{8,24},{9,11},... | collective-permute-start | bytes 516104 | tf_op jit(solution)/shard_map/ppermute | solution.py:111
  19.1 5.5 %collective-permute-start.8 = (bf16[6,4,3712]{2,1,0:T(4,128)(2,1)S(1)}, bf16[6,4,3712]{2,1,0:T(4,128)(2,1)S(1)}, u32[]{:S(2)}, u32[]{:S(2)}) collective-permute-start(bf16[6,4,3712]{2,1,0:T(4,128)(2,1)S(1)} %constant_dynamic-update-slice_fusion.refs_4_), channel_id=1, source_target_pairs={{0,16},{1,3},{2,18},{3,1},{4,20},{5,7},{6,22},{7,5},{8,24},{9,11},... | collective-permute-start | bytes 534536 | tf_op jit(solution)/shard_map/ppermute | solution.py:111
  20.7 4.0 %collective-permute-start.2 = (bf16[16,3712]{1,0:T(8,128)(2,1)S(1)}, bf16[16,3712]{1,0:T(8,128)(2,1)S(1)}, u32[]{:S(2)}, u32[]{:S(2)}) collective-permute-start(bf16[16,3712]{1,0:T(8,128)(2,1)S(1)} %pad_maximum_fusion.1.refs_0_), channel_id=1, source_target_pairs={{0,1},{1,0},{2,3},{3,2},{4,5},{5,4},{6,7},{7,6},{8,9},{9,8},{10,11... | collective-permute-start | bytes 356360 | tf_op jit(solution)/shard_map/ppermute | solution.py:111
  20.8 5.2 %collective-permute-start.1 = (bf16[16,3712]{1,0:T(8,128)(2,1)S(1)}, bf16[16,3712]{1,0:T(8,128)(2,1)S(1)}, u32[]{:S(2)}, u32[]{:S(2)}) collective-permute-start(bf16[16,3712]{1,0:T(8,128)(2,1)S(1)} %pad_maximum_fusion.1.refs_0_), channel_id=1, source_target_pairs={{0,16},{1,3},{2,18},{3,1},{4,20},{5,7},{6,22},{7,5},{8,24},{9,11},... | collective-permute-start | bytes 356360 | tf_op jit(solution)/shard_map/ppermute | solution.py:111
  21.4 11.1 %collective-permute-start.9 = (bf16[6,4,3712]{2,1,0:T(4,128)(2,1)S(1)}, bf16[6,4,3712]{2,1,0:T(4,128)(2,1)S(1)}, u32[]{:S(2)}, u32[]{:S(2)}) collective-permute-start(bf16[6,4,3712]{2,1,0:T(4,128)(2,1)S(1)} %constant_dynamic-update-slice_fusion.refs_4_), channel_id=1, source_target_pairs={{0,1},{1,0},{2,3},{3,2},{4,5},{5,4},{6,7},{7,6},{8,9},{9,8},{10,11... | collective-permute-start | bytes 534536 | tf_op jit(solution)/shard_map/ppermute | solution.py:111
  24.7 7.8 %collective-permute-start.10 = (bf16[6,4,3712]{2,1,0:T(4,128)(2,1)S(1)}, bf16[6,4,3712]{2,1,0:T(4,128)(2,1)S(1)}, u32[]{:S(2)}, u32[]{:S(2)}) collective-permute-start(bf16[6,4,3712]{2,1,0:T(4,128)(2,1)S(1)} %collective-permute-done.8.refs_5_), channel_id=1, source_target_pairs={{0,1},{1,0},{2,3},{3,2},{4,5},{5,4},{6,7},{7,6},{8,9},{9,8},{10,11... | collective-permute-start | bytes 534536 | tf_op jit(solution)/shard_map/ppermute | solution.py:111
  24.7 6.4 %collective-permute-start.13 = (bf16[6,4,3584]{2,1,0:T(4,128)(2,1)S(1)}, bf16[6,4,3584]{2,1,0:T(4,128)(2,1)S(1)}, u32[]{:S(2)}, u32[]{:S(2)}) collective-permute-start(bf16[6,4,3584]{2,1,0:T(4,128)(2,1)S(1)} %constant_dynamic-update-slice_fusion.2.refs_4_), channel_id=1, source_target_pairs={{0,1},{1,0},{2,3},{3,2},{4,5},{5,4},{6,7},{7,6},{8,9},{9,8},{10,11... | collective-permute-start | bytes 516104 | tf_op jit(solution)/shard_map/ppermute | solution.py:111
  25.2 5.9 %collective-permute-start.14 = (bf16[6,4,3584]{2,1,0:T(4,128)(2,1)S(1)}, bf16[6,4,3584]{2,1,0:T(4,128)(2,1)S(1)}, u32[]{:S(2)}, u32[]{:S(2)}) collective-permute-start(bf16[6,4,3584]{2,1,0:T(4,128)(2,1)S(1)} %collective-permute-done.12.refs_5_), channel_id=1, source_target_pairs={{0,1},{1,0},{2,3},{3,2},{4,5},{5,4},{6,7},{7,6},{8,9},{9,8},{10,11... | collective-permute-start | bytes 516104 | tf_op jit(solution)/shard_map/ppermute | solution.py:111
  25.9 5.1 %collective-permute-start.3 = (bf16[16,3712]{1,0:T(8,128)(2,1)S(1)}, bf16[16,3712]{1,0:T(8,128)(2,1)S(1)}, u32[]{:S(2)}, u32[]{:S(2)}) collective-permute-start(bf16[16,3712]{1,0:T(8,128)(2,1)S(1)} %collective-permute-done.1.refs_1_), channel_id=1, source_target_pairs={{0,1},{1,0},{2,3},{3,2},{4,5},{5,4},{6,7},{7,6},{8,9},{9,8},{10,11... | collective-permute-start | bytes 356360 | tf_op jit(solution)/shard_map/ppermute | solution.py:111
  34.1 1.7 %collective-permute-start.15 = (bf16[64,1792]{1,0:T(8,128)(2,1)S(1)}, bf16[64,1792]{1,0:T(8,128)(2,1)S(1)}, u32[]{:S(2)}, u32[]{:S(2)}) collective-permute-start(bf16[64,1792]{1,0:T(8,128)(2,1)S(1)} %get-tuple-element.23), channel_id=1, source_target_pairs={{0,1},{1,0},{2,3},{3,2},{4,5},{5,4},{6,7},{7,6},{8,9},{9,8},{10,11... | collective-permute-start | bytes 688136 | tf_op jit(solution)/shard_map/ppermute | solution.py:111
  35.3 2.1 %collective-permute-start.18 = (bf16[64,1792]{1,0:T(8,128)(2,1)S(1)}, bf16[64,1792]{1,0:T(8,128)(2,1)S(1)}, u32[]{:S(2)}, u32[]{:S(2)}) collective-permute-start(bf16[64,1792]{1,0:T(8,128)(2,1)S(1)} %get-tuple-element.27), channel_id=1, source_target_pairs={{0,1},{1,0},{2,3},{3,2},{4,5},{5,4},{6,7},{7,6},{8,9},{9,8},{10,11... | collective-permute-start | bytes 688136 | tf_op jit(solution)/shard_map/ppermute | solution.py:111
  35.8 4.9 %collective-permute-start.16 = (bf16[32,1792]{1,0:T(8,128)(2,1)S(1)}, bf16[32,1792]{1,0:T(8,128)(2,1)S(1)}, u32[]{:S(2)}, u32[]{:S(2)}) collective-permute-start(bf16[32,1792]{1,0:T(8,128)(2,1)S(1)} %slice.94), channel_id=1, source_target_pairs={{0,16},{1,3},{2,18},{3,1},{4,20},{5,7},{6,22},{7,5},{8,24},{9,11},... | collective-permute-start | bytes 344072 | tf_op jit(solution)/shard_map/ppermute | solution.py:111
  37.5 4.9 %collective-permute-start.19 = (bf16[32,1792]{1,0:T(8,128)(2,1)S(1)}, bf16[32,1792]{1,0:T(8,128)(2,1)S(1)}, u32[]{:S(2)}, u32[]{:S(2)}) collective-permute-start(bf16[32,1792]{1,0:T(8,128)(2,1)S(1)} %slice.93), channel_id=1, source_target_pairs={{0,16},{1,3},{2,18},{3,1},{4,20},{5,7},{6,22},{7,5},{8,24},{9,11},... | collective-permute-start | bytes 344072 | tf_op jit(solution)/shard_map/ppermute | solution.py:111
  40.7 4.2 %collective-permute-start.17 = (bf16[16,1792]{1,0:T(8,128)(2,1)S(1)}, bf16[16,1792]{1,0:T(8,128)(2,1)S(1)}, u32[]{:S(2)}, u32[]{:S(2)}) collective-permute-start(bf16[16,1792]{1,0:T(8,128)(2,1)S(1)} %slice.96), channel_id=1, source_target_pairs={{0,2},{1,17},{2,0},{3,19},{4,6},{5,21},{6,4},{7,23},{8,10},{9,25},... | collective-permute-start | bytes 172040 | tf_op jit(solution)/shard_map/ppermute | solution.py:111
  42.4 4.2 %collective-permute-start.20 = (bf16[16,1792]{1,0:T(8,128)(2,1)S(1)}, bf16[16,1792]{1,0:T(8,128)(2,1)S(1)}, u32[]{:S(2)}, u32[]{:S(2)}) collective-permute-start(bf16[16,1792]{1,0:T(8,128)(2,1)S(1)} %slice.95), channel_id=1, source_target_pairs={{0,2},{1,17},{2,0},{3,19},{4,6},{5,21},{6,4},{7,23},{8,10},{9,25},... | collective-permute-start | bytes 172040 | tf_op jit(solution)/shard_map/ppermute | solution.py:111
  46.7 8.7 %collective-permute-start.21 = (bf16[4,3584]{1,0:T(4,128)(2,1)S(1)}, bf16[4,3584]{1,0:T(4,128)(2,1)S(1)}, u32[]{:S(2)}, u32[]{:S(2)}) collective-permute-start(bf16[4,3584]{1,0:T(4,128)(2,1)S(1)} %get-tuple-element.30), channel_id=1, source_target_pairs={{0,12},{1,13},{2,14},{3,15},{4,8},{5,9},{6,10},{7,11},{8,4},{9,5},... | collective-permute-start | bytes 86024 | tf_op jit(solution)/shard_map/ppermute | solution.py:111
  49.6 5.8 %collective-permute-start.23 = (bf16[4,3584]{1,0:T(4,128)(2,1)S(1)}, bf16[4,3584]{1,0:T(4,128)(2,1)S(1)}, u32[]{:S(2)}, u32[]{:S(2)}) collective-permute-start(bf16[4,3584]{1,0:T(4,128)(2,1)S(1)} %get-tuple-element.31), channel_id=1, source_target_pairs={{0,8},{1,9},{2,10},{3,11},{4,12},{5,13},{6,14},{7,15},{8,0},{9,1},... | collective-permute-start | bytes 86024 | tf_op jit(solution)/shard_map/ppermute | solution.py:111
  49.6 5.8 %collective-permute-start.22 = (bf16[4,3584]{1,0:T(4,128)(2,1)S(1)}, bf16[4,3584]{1,0:T(4,128)(2,1)S(1)}, u32[]{:S(2)}, u32[]{:S(2)}) collective-permute-start(bf16[4,3584]{1,0:T(4,128)(2,1)S(1)} %get-tuple-element.32), channel_id=1, source_target_pairs={{0,4},{1,5},{2,6},{3,7},{4,0},{5,1},{6,2},{7,3},{8,12},{9,13},{10,... | collective-permute-start | bytes 86024 | tf_op jit(solution)/shard_map/ppermute | solution.py:111
  (3 other events, 30.5 us)

commit v6 on v5

--- a/solution.py
+++ b/solution.py
@@ -249,21 +249,9 @@
         hidden_t[cols, :] = (swish * up_pre).T.astype(BF16)
 
 
-def part_columns(gate_grad, up_grad, gate_t, up_t, offset, own, other):
-    rows, width = own.shape
-    step = 256 if width % 256 == 0 else width
-    for c in range(0, width, step):
-        cols = slice(offset + c, offset + c + step)
-        first = jnp.dot(gate_grad, gate_t[:, cols], preferred_element_type=F32)
-        second = jnp.dot(up_grad, up_t[:, cols], preferred_element_type=F32)
-        part = (first + second).astype(BF16)
-        own[:, c : c + step] = part[:rows]
-        other[:, c : c + step] = part[rows:]
-
-
 def backward_kernel(n, width, *refs):
     near, away, refs = refs[:n], refs[n : 2 * n], refs[2 * n :]
-    down_t, gate_t, up_t, gate_by, up_by, own, other, scaled, gate_grad, up_grad, placed = refs
+    down_t, gate_t, up_t, gate_by, up_by, scaled, own, *others, placed = refs
     place(near, away, away[0].shape[1], placed)
     expert = lax.axis_index("ep")
     spread = placed[:, width:].astype(F32)
@@ -271,29 +259,36 @@
     weight = jnp.sum(jnp.where(lane == expert, spread, 0.0), axis=1, keepdims=True)
     scaled[...] = (weight * placed[:, :width].astype(F32)).astype(BF16)
     hidden_grad = jnp.dot(scaled[...], down_t[...], preferred_element_type=F32)
-    gates = (hidden_grad * gate_by[...]).astype(BF16)
-    ups = (hidden_grad * up_by[...]).astype(BF16)
-    gate_grad[...] = gates
-    up_grad[...] = ups
-    part_columns(gates, ups, gate_t, up_t, 0, own, other)
+    gate_grad = (hidden_grad * gate_by[...]).astype(BF16)
+    up_grad = (hidden_grad * up_by[...]).astype(BF16)
+    kept = own.shape[0]
+    step = 256 if width % 256 == 0 else width
+    for c in range(0, width, step):
+        cols = slice(c, c + step)
+        first = jnp.dot(gate_grad, gate_t[:, cols], preferred_element_type=F32)
+        second = jnp.dot(up_grad, up_t[:, cols], preferred_element_type=F32)
+        part = (first + second).astype(BF16)
+        own[:, cols] = part[:kept]
+        start = kept
+        for other in others:
+            other[:, cols] = part[start : start + other.shape[0]]
+            start += other.shape[0]
 
 
 def backward(near, away, down_t, gate_t, up_t, gate_by, up_by):
     n = len(near)
-    rows, units = gate_by.shape
+    rows = gate_by.shape[0]
     width = down_t.shape[0]
-    half = jax.ShapeDtypeStruct((rows // 2, width // 2), BF16)
     return pl.pallas_call(
         functools.partial(backward_kernel, n, width),
         out_shape=(
-            half,
-            half,
             jax.ShapeDtypeStruct((rows, width), BF16),
-            jax.ShapeDtypeStruct((rows, units), BF16),
-            jax.ShapeDtypeStruct((rows, units), BF16),
+            jax.ShapeDtypeStruct((rows // 2, width), BF16),
+            jax.ShapeDtypeStruct((rows * 3 // 8, width), BF16),
+            jax.ShapeDtypeStruct((rows // 8, width), BF16),
         ),
         in_specs=[WHOLE] * (2 * n + 5),
-        out_specs=(WHOLE,) * 5,
+        out_specs=(WHOLE,) * 4,
         scratch_shapes=[pltpu.VMEM((rows, away[0].shape[2]), BF16)],
         compiler_params=room(24),
         cost_estimate=QUICK,
@@ -301,29 +296,12 @@
     )(*near, *away, down_t, gate_t, up_t, gate_by, up_by)
 
 
-def right_kernel(gate_grad, up_grad, gate_t, up_t, own, other):
-    part_columns(gate_grad[...], up_grad[...], gate_t, up_t, own.shape[1], own, other)
-
-
-def right_half(gate_grad, up_grad, gate_t, up_t):
-    half = jax.ShapeDtypeStruct((gate_grad.shape[0] // 2, gate_t.shape[1] // 2), BF16)
-    return pl.pallas_call(
-        right_kernel,
-        out_shape=(half, half),
-        in_specs=[WHOLE] * 4,
-        out_specs=(WHOLE,) * 2,
-        compiler_params=room(16),
-        cost_estimate=QUICK,
-        name="right",
-    )(gate_grad, up_grad, gate_t, up_t)
-
-
-def outer_kernel(first, hidden_t, scaled, *refs):
+def outer_kernel(start, hidden_t, scaled, *refs):
     out, buffer, sem = refs[-3:]
     chunks, size = buffer.shape[:2]
     copies = []
     for n in range(chunks):
-        rows = pl.ds((first * chunks + n) * size, size)
+        rows = pl.ds(start + n * size, size)
         buffer[n] = jnp.dot(hidden_t[rows, :], scaled[...], preferred_element_type=F32)
         copies.append(pltpu.make_async_copy(buffer.at[n], out.at[rows], sem.at[n]))
         copies[-1].start()
@@ -331,16 +309,15 @@
         copy.wait()
 
 
-def outer(first, hidden_t, scaled, *so_far):
+def outer(start, chunks, hidden_t, scaled, *so_far):
     units, width = hidden_t.shape[0], scaled.shape[1]
-    chunks = 4
-    return pl.pallas_call(
-        functools.partial(outer_kernel, first),
+    return pl.pallas_call(
+        functools.partial(outer_kernel, start * (units // 8)),
         out_shape=pltpu.HBM((units, width), F32),
         in_specs=[WHOLE] * 2 + [pl.BlockSpec(memory_space=pltpu.HBM)] * len(so_far),
         out_specs=pl.BlockSpec(memory_space=pltpu.HBM),
         scratch_shapes=[
-            pltpu.VMEM((chunks, units // 2 // chunks, width), F32),
+            pltpu.VMEM((chunks, units // 8, width), F32),
             pltpu.SemaphoreType.DMA((chunks,)),
         ],
         input_output_aliases={2: 0} if so_far else {},
@@ -348,6 +325,25 @@
         cost_estimate=QUICK,
         name="outer",
     )(hidden_t, scaled, *so_far)
+
+
+def add_kernel(starts, *refs):
+    out = refs[-1]
+    rows = out.shape[0]
+    total = sum(ref[n : n + rows, :].astype(F32) for n, ref in zip(starts, refs))
+    out[...] = total.astype(BF16)
+
+
+def add_rows(rows, *terms):
+    return pl.pallas_call(
+        functools.partial(add_kernel, [start for _, start in terms]),
+        out_shape=jax.ShapeDtypeStruct((rows, terms[0][0].shape[1]), BF16),
+        in_specs=[WHOLE] * len(terms),
+        out_specs=WHOLE,
+        compiler_params=room(4),
+        cost_estimate=QUICK,
+        name="add",
+    )(*(array for array, _ in terms))
 
 
 def dense(activations, out_grad, route_weights, expert_ids, w_gate, w_up, w_down):
@@ -395,21 +391,25 @@
         cost_estimate=QUICK,
         name="forward",
     )(placed, gate_w, up_w)
-    own_left, other_left, scaled, gate_grad, up_grad = backward(
+    scaled, kept, other, other_corner = backward(
         near, rows_grad, down_t, gate_t, up_t, gate_by, up_by
     )
-    own_right, other_right = right_half(gate_grad, up_grad, gate_t, up_t)
-    owns = (own_left, own_right)
-    got = [swap(x, core) for x in (other_left, other_right)]
-    weight_grad = outer(0, hidden_t, scaled)
-    weight_grad = outer(1, hidden_t, scaled, weight_grad)
-
-    totals = [a.astype(F32) + b.astype(F32) for a, b in zip(owns, got)]
-    for partner in (two, one):
-        half = totals[0].shape[0] // 2
-        got = [swap(x[half:].astype(BF16), partner) for x in totals]
-        totals = [x[:half].astype(F32) + y.astype(F32) for x, y in zip(totals, got)]
-    total = jnp.concatenate(totals, axis=1)
+    weight_grad = ()
+    for start, chunks in ((0, 2), (2, 2), (4, 4)):
+        weight_grad = (outer(start, chunks, hidden_t, scaled, *weight_grad),)
+    weight_grad = weight_grad[0]
+
+    size = kept.shape[0] // 4
+    got = swap(other_corner, core)
+    corner = add_rows(size, (kept, 3 * size), (got, 0))
+    passed = swap(corner, two)
+    got = swap(other, core)
+    second = add_rows(size, (kept, 2 * size), (got, 2 * size))
+    second = swap(second, two)
+    first = add_rows(size, (kept, size), (got, size), (passed, 0))
+    first = swap(first, one)
+    total = kept[:size].astype(F32) + got[:size].astype(F32)
+    total = total + second.astype(F32) + first.astype(F32)
     sent = total.astype(BF16)
     own = total[:tok_dev]
     for j in back_order(far):

time: 56.3 us -> 56.8 us (level)
  starting transfers between devices: 23.9 us -> 22.4 us
  waiting for transfers between devices: 16.2 us -> 17.7 us
  Pallas kernels: 11.9 us -> 12.7 us
    ppermute x24 -> x23, waiting for transfers between devices: 16.2 us -> 17.7 us  [exchange(): return lax.ppermute(value, ('sp', 'ep'), pairs)]
    ppermute x24 -> x23, starting transfers between devices: 23.9 us -> 22.4 us  [exchange(): return lax.ppermute(value, ('sp', 'ep'), pairs)]
    pallas_call x4 -> x7, Pallas kernels: 6.48 us -> 7.19 us  [the longest x3 5.17 us: outer(): pl.pallas_call(functools.partial(outer_kernel, start * (units // 8)), out...]
  transfers between devices with their start and end apart: 24 -> 23, of which waited for: 10 -> 9; matrix products, arithmetic and copies ran while one was open for 1% -> 0% of each run, Pallas kernels for 17% -> 17%
where the time goes in v6:
time: 56.8 us; the launch traced here: 56.7 us
  starting transfers between devices  22.4 us (39%)
  waiting for transfers between devices  17.7 us (31%)
  Pallas kernels  12.7 us (22%)
  local copies, waits for them, and re-layouts  2.34 us (4%)
  between operations  0.84 us (1%)
  other arithmetic  0.71 us (1%)
    ppermute x23, starting transfers between devices, exchange(): return lax.ppermute(value, ('sp', 'ep'), pairs)  22.4 us
    ppermute x23, waiting for transfers between devices, exchange(): return lax.ppermute(value, ('sp', 'ep'), pairs)  17.7 us
    pallas_call x3, Pallas kernels, outer(): pl.pallas_call(functools.partial(outer_kernel, start * (units // 8)), out...  5.17 us
    pallas_call x2, Pallas kernels, turn(): pl.pallas_call(functools.partial(turn_kernel, n), out_shape=[jax.ShapeDty...  2.93 us
    unnamed x8, local copies, waits for them, and re-layouts  2.22 us
    pallas_call x1, Pallas kernels, backward(): pl.pallas_call(functools.partial(backward_kernel, n, width), out_shape=(j...  1.92 us
    pallas_call x1, Pallas kernels, dense(): pl.pallas_call(forward_kernel, out_shape=(jax.ShapeDtypeStruct((rows, uni...  1.22 us
  transfers between devices with their start and end apart: 23, of which 9 were waited for; matrix products, arithmetic and copies ran while one was open for 0% of the time, Pallas kernels for 17%

profile of v6, /device:TPU:0, one launch (start us, length us, event | category | flops | bytes accessed | tf_op | source)
XLA Modules:
  0.0 56.7 jit_solution(14386309849622813246)
XLA Ops:
  0.6 1.1 %pack.1 = bf16[8,3712]{1,0:T(8,128)(2,1)S(1)} custom-call(bf16[1,4,3584]{2,1,0:T(4,128)(2,1)} %in_ref.1, bf16[1,4,3584]{2,1,0:T(4,128)(2,1)} %grad_ref.1, bf16[1,4,8]{2,1,0:T(4,128)(2,1)} %weight_ref.1, s32[1,4,8]{2,1,0:T(4,128)} %ids_ref.1), custom_call_target="tpu_custom_call" | custom-call | flops 10000000000 | tf_op jit(solution)/shard_map/pack/pallas_call | solution.py:145
  1.7 5.1 %collective-permute-start.6 = (bf16[8,3712]{1,0:T(8,128)(2,1)S(1)}, bf16[8,3712]{1,0:T(8,128)(2,1)S(1)}, u32[]{:S(2)}, u32[]{:S(2)}) collective-permute-start(bf16[8,3712]{1,0:T(8,128)(2,1)S(1)} %pack.1), channel_id=1, source_target_pairs={{0,12},{1,13},{2,14},{3,15},{4,8},{5,9},{6,10},{7,11},{8,4},{9,5},... | collective-permute-start | bytes 178184 | tf_op jit(solution)/shard_map/ppermute | solution.py:111
  7.5 1.7 %collective-permute-start = (bf16[8,3712]{1,0:T(8,128)(2,1)S(1)}, bf16[8,3712]{1,0:T(8,128)(2,1)S(1)}, u32[]{:S(2)}, u32[]{:S(2)}) collective-permute-start(bf16[8,3712]{1,0:T(8,128)(2,1)S(1)} %pack.1), channel_id=1, source_target_pairs={{0,2},{1,17},{2,0},{3,19},{4,6},{5,21},{6,4},{7,23},{8,10},{9,25},... | collective-permute-start | bytes 178184 | tf_op jit(solution)/shard_map/ppermute | solution.py:111
  9.2 2.8 %collective-permute-done.5.refs_1_ = bf16[8,3712]{1,0:T(8,128)(2,1)S(1)} collective-permute-done((bf16[8,3712]{1,0:T(8,128)(2,1)S(1)}, bf16[8,3712]{1,0:T(8,128)(2,1)S(1)}, u32[]{:S(2)}, u32[]{:S(2)}) %collective-permute-start.5) | collective-permute-done | bytes 59424 | tf_op jit(solution)/shard_map/ppermute | solution.py:111
  12.1 1.7 %collective-permute-start.11 = (bf16[3,4,3584]{2,1,0:T(4,128)(2,1)S(1)}, bf16[3,4,3584]{2,1,0:T(4,128)(2,1)S(1)}, u32[]{:S(2)}, u32[]{:S(2)}) collective-permute-start(bf16[3,4,3584]{2,1,0:T(4,128)(2,1)S(1)} %get-tuple-element.16), channel_id=1, source_target_pairs={{0,2},{1,17},{2,0},{3,19},{4,6},{5,21},{6,4},{7,23},{8,10},{9,25},... | collective-permute-start | bytes 258056 | tf_op jit(solution)/shard_map/ppermute | solution.py:111
  14.3 2.3 %collective-permute-done.11 = bf16[3,4,3584]{2,1,0:T(4,128)(2,1)S(1)} collective-permute-done((bf16[3,4,3584]{2,1,0:T(4,128)(2,1)S(1)}, bf16[3,4,3584]{2,1,0:T(4,128)(2,1)S(1)}, u32[]{:S(2)}, u32[]{:S(2)}) %collective-permute-start.11) | collective-permute-done | bytes 86048 | tf_op jit(solution)/shard_map/ppermute | solution.py:111
  16.7 1.6 %collective-permute-start.12 = (bf16[6,4,3584]{2,1,0:T(4,128)(2,1)S(1)}, bf16[6,4,3584]{2,1,0:T(4,128)(2,1)S(1)}, u32[]{:S(2)}, u32[]{:S(2)}) collective-permute-start(bf16[6,4,3584]{2,1,0:T(4,128)(2,1)S(1)} %constant_dynamic-update-slice_fusion.2.refs_4_), channel_id=1, source_target_pairs={{0,16},{1,3},{2,18},{3,1},{4,20},{5,7},{6,22},{7,5},{8,24},{9,11},... | collective-permute-start | bytes 516104 | tf_op jit(solution)/shard_map/ppermute | solution.py:111
  19.1 1.6 %collective-permute-start.8 = (bf16[6,4,3712]{2,1,0:T(4,128)(2,1)S(1)}, bf16[6,4,3712]{2,1,0:T(4,128)(2,1)S(1)}, u32[]{:S(2)}, u32[]{:S(2)}) collective-permute-start(bf16[6,4,3712]{2,1,0:T(4,128)(2,1)S(1)} %constant_dynamic-update-slice_fusion.refs_4_), channel_id=1, source_target_pairs={{0,16},{1,3},{2,18},{3,1},{4,20},{5,7},{6,22},{7,5},{8,24},{9,11},... | collective-permute-start | bytes 534536 | tf_op jit(solution)/shard_map/ppermute | solution.py:111
  21.4 3.3 %collective-permute-done.8.refs_5_ = bf16[6,4,3712]{2,1,0:T(4,128)(2,1)S(1)} collective-permute-done((bf16[6,4,3712]{2,1,0:T(4,128)(2,1)S(1)}, bf16[6,4,3712]{2,1,0:T(4,128)(2,1)S(1)}, u32[]{:S(2)}, u32[]{:S(2)}) %collective-permute-start.8) | collective-permute-done | bytes 178208 | tf_op jit(solution)/shard_map/ppermute | solution.py:111
  27.0 1.0 %copy-done = bf16[1,3584,512]{2,1,0:T(8,128)(2,1)S(1)} copy-done((bf16[1,3584,512]{2,1,0:T(8,128)(2,1)S(1)}, bf16[1,3584,512]{2,1,0:T(8,128)(2,1)}, u32[]{:S(2)}) %copy-start) | copy-done | bytes 3670040
  28.0 1.1 %copy-done.1 = bf16[1,3584,512]{2,1,0:T(8,128)(2,1)S(1)} copy-done((bf16[1,3584,512]{2,1,0:T(8,128)(2,1)S(1)}, bf16[1,3584,512]{2,1,0:T(8,128)(2,1)}, u32[]{:S(2)}) %copy-start.1) | copy-done | bytes 3670040
  29.1 1.9 %turn.3 = (bf16[512,3584]{1,0:T(8,128)(2,1)S(1)}, bf16[512,3584]{1,0:T(8,128)(2,1)S(1)}) custom-call(bf16[3584,512]{1,0:T(8,128)(2,1)S(1)} %bitcast.6, bf16[3584,512]{1,0:T(8,128)(2,1)S(1)} %bitcast.8), custom_call_target="tpu_custom_call" | custom-call | flops 1000000 | tf_op jit(solution)/shard_map/turn/pallas_call | solution.py:228
  31.3 1.2 %forward.1 = (f32[128,512]{1,0:T(8,128)S(1)}, f32[128,512]{1,0:T(8,128)S(1)}, bf16[512,128]{1,0:T(8,128)(2,1)S(1)}) custom-call(bf16[128,3584]{1,0:T(8,128)(2,1)S(1)} %lay.1.rows, bf16[3584,512]{1,0:T(8,128)(2,1)S(1)} %bitcast.7, bf16[3584,512]{1,0:T(8,128)(2,1)S(1)} %bitcast.9), custom_call_target="tpu_custom_call" | custom-call | flops 1000000 | tf_op jit(solution)/shard_map/forward/pallas_call | solution.py:381
  32.5 1.9 %backward.1 = (bf16[128,3584]{1,0:T(8,128)(2,1)S(1)}, bf16[64,3584]{1,0:T(8,128)(2,1)S(1)}, bf16[48,3584]{1,0:T(8,128)(2,1)S(1)}, bf16[16,3584]{1,0:T(8,128)(2,1)S(1)}) custom-call(bf16[16,3712]{1,0:T(8,128)(2,1)S(1)} %pad_maximum_fusion.refs_0_, bf16[16,3712]{1,0:T(8,128)(2,1)S(1)} %collective-permute-done.1.refs_1_, ...), custom_call_target="tpu_custom_call" | custom-call | flops 1000000 | tf_op jit(solution)/shard_map/backward/pallas_call | solution.py:282
  35.1 1.4 %collective-permute-done.17.refs_1_ = bf16[16,3584]{1,0:T(8,128)(2,1)S(1)} collective-permute-done((bf16[16,3584]{1,0:T(8,128)(2,1)S(1)}, bf16[16,3584]{1,0:T(8,128)(2,1)S(1)}, u32[]{:S(2)}, u32[]{:S(2)}) %collective-permute-start.17) | collective-permute-done | bytes 114720 | tf_op jit(solution)/shard_map/ppermute | solution.py:111
  36.5 1.6 %collective-permute-start.18 = (bf16[16,3584]{1,0:T(8,128)(2,1)S(1)}, bf16[16,3584]{1,0:T(8,128)(2,1)S(1)}, u32[]{:S(2)}, u32[]{:S(2)}) collective-permute-start(bf16[16,3584]{1,0:T(8,128)(2,1)S(1)} %add.55), channel_id=1, source_target_pairs={{0,16},{1,3},{2,18},{3,1},{4,20},{5,7},{6,22},{7,5},{8,24},{9,11},... | collective-permute-start | bytes 344072 | tf_op jit(solution)/shard_map/ppermute | solution.py:111
  38.7 2.7 %collective-permute-done.18.refs_2_ = bf16[16,3584]{1,0:T(8,128)(2,1)S(1)} collective-permute-done((bf16[16,3584]{1,0:T(8,128)(2,1)S(1)}, bf16[16,3584]{1,0:T(8,128)(2,1)S(1)}, u32[]{:S(2)}, u32[]{:S(2)}) %collective-permute-start.18) | collective-permute-done | bytes 114720 | tf_op jit(solution)/shard_map/ppermute | solution.py:111
  41.4 1.1 %collective-permute-start.19 = (bf16[16,3584]{1,0:T(8,128)(2,1)S(1)}, bf16[16,3584]{1,0:T(8,128)(2,1)S(1)}, u32[]{:S(2)}, u32[]{:S(2)}) collective-permute-start(bf16[16,3584]{1,0:T(8,128)(2,1)S(1)} %add.56), channel_id=1, source_target_pairs={{0,2},{1,17},{2,0},{3,19},{4,6},{5,21},{6,4},{7,23},{8,10},{9,25},... | collective-permute-start | bytes 344072 | tf_op jit(solution)/shard_map/ppermute | solution.py:111
  42.9 3.3 %collective-permute-done.19 = bf16[16,3584]{1,0:T(8,128)(2,1)S(1)} collective-permute-done((bf16[16,3584]{1,0:T(8,128)(2,1)S(1)}, bf16[16,3584]{1,0:T(8,128)(2,1)S(1)}, u32[]{:S(2)}, u32[]{:S(2)}) %collective-permute-start.19) | collective-permute-done | bytes 114720 | tf_op jit(solution)/shard_map/ppermute | solution.py:111
  46.3 2.9 %collective-permute-start.20 = (bf16[4,3584]{1,0:T(4,128)(2,1)S(1)}, bf16[4,3584]{1,0:T(4,128)(2,1)S(1)}, u32[]{:S(2)}, u32[]{:S(2)}) collective-permute-start(bf16[4,3584]{1,0:T(4,128)(2,1)S(1)} %get-tuple-element.26), channel_id=1, source_target_pairs={{0,12},{1,13},{2,14},{3,15},{4,8},{5,9},{6,10},{7,11},{8,4},{9,5},... | collective-permute-start | bytes 86024 | tf_op jit(solution)/shard_map/ppermute | solution.py:111
  49.3 1.5 %collective-permute-start.21 = (bf16[4,3584]{1,0:T(4,128)(2,1)S(1)}, bf16[4,3584]{1,0:T(4,128)(2,1)S(1)}, u32[]{:S(2)}, u32[]{:S(2)}) collective-permute-start(bf16[4,3584]{1,0:T(4,128)(2,1)S(1)} %get-tuple-element.28), channel_id=1, source_target_pairs={{0,4},{1,5},{2,6},{3,7},{4,0},{5,1},{6,2},{7,3},{8,12},{9,13},{10,... | collective-permute-start | bytes 86024 | tf_op jit(solution)/shard_map/ppermute | solution.py:111
  50.8 1.5 %outer.3.refs_0_ = f32[512,3584]{1,0:T(8,128)} custom-call(bf16[512,128]{1,0:T(8,128)(2,1)S(1)} %get-tuple-element.22.hidden_t, bf16[128,3584]{1,0:T(8,128)(2,1)S(1)} %get-tuple-element.23.scaled), custom_call_target="tpu_custom_call" | custom-call | flops 1000000 | tf_op jit(solution)/shard_map/outer/pallas_call | solution.py:314
  52.3 1.5 %outer.4.refs_0_ = f32[512,3584]{1,0:T(8,128)} custom-call(bf16[512,128]{1,0:T(8,128)(2,1)S(1)} %get-tuple-element.22.hidden_t, bf16[128,3584]{1,0:T(8,128)(2,1)S(1)} %get-tuple-element.23.scaled, f32[512,3584]{1,0:T(8,128)} %outer.3.refs_0_), custom_call_target="tpu_custom_call", output_to_operand_aliasing={{}: (2, {})} | custom-call | flops 1000000 | tf_op jit(solution)/shard_map/outer/pallas_call | solution.py:314
  53.8 2.1 %outer.5 = f32[512,3584]{1,0:T(8,128)} custom-call(bf16[512,128]{1,0:T(8,128)(2,1)S(1)} %get-tuple-element.22.hidden_t, bf16[128,3584]{1,0:T(8,128)(2,1)S(1)} %get-tuple-element.23.scaled, f32[512,3584]{1,0:T(8,128)} %outer.4.refs_0_), custom_call_target="tpu_custom_call", output_to_operand_aliasing={{}: (2, {})} | custom-call | flops 1000000 | tf_op jit(solution)/shard_map/outer/pallas_call | solution.py:314
  (49 shorter events, 7.8 us)
Async XLA Ops:
  0.6 25.3 %copy-start.2 = (bf16[1,512,3584]{2,1,0:T(8,128)(2,1)S(1)}, bf16[1,512,3584]{2,1,0:T(8,128)(2,1)}, u32[]{:S(2)}) copy-start(bf16[1,512,3584]{2,1,0:T(8,128)(2,1)} %param.13) | copy-start | bytes 11010052
  1.7 7.5 %collective-permute-start.6 = (bf16[8,3712]{1,0:T(8,128)(2,1)S(1)}, bf16[8,3712]{1,0:T(8,128)(2,1)S(1)}, u32[]{:S(2)}, u32[]{:S(2)}) collective-permute-start(bf16[8,3712]{1,0:T(8,128)(2,1)S(1)} %pack.1), channel_id=1, source_target_pairs={{0,12},{1,13},{2,14},{3,15},{4,8},{5,9},{6,10},{7,11},{8,4},{9,5},... | collective-permute-start | bytes 178184 | tf_op jit(solution)/shard_map/ppermute | solution.py:111
  6.9 5.2 %collective-permute-start.5 = (bf16[8,3712]{1,0:T(8,128)(2,1)S(1)}, bf16[8,3712]{1,0:T(8,128)(2,1)S(1)}, u32[]{:S(2)}, u32[]{:S(2)}) collective-permute-start(bf16[8,3712]{1,0:T(8,128)(2,1)S(1)} %pack.1), channel_id=1, source_target_pairs={{0,8},{1,9},{2,10},{3,11},{4,12},{5,13},{6,14},{7,15},{8,0},{9,1},... | collective-permute-start | bytes 178184 | tf_op jit(solution)/shard_map/ppermute | solution.py:111
  6.9 5.2 %collective-permute-start.4 = (bf16[8,3712]{1,0:T(8,128)(2,1)S(1)}, bf16[8,3712]{1,0:T(8,128)(2,1)S(1)}, u32[]{:S(2)}, u32[]{:S(2)}) collective-permute-start(bf16[8,3712]{1,0:T(8,128)(2,1)S(1)} %pack.1), channel_id=1, source_target_pairs={{0,4},{1,5},{2,6},{3,7},{4,0},{5,1},{6,2},{7,3},{8,12},{9,13},{10,... | collective-permute-start | bytes 178184 | tf_op jit(solution)/shard_map/ppermute | solution.py:111
  7.5 13.2 %collective-permute-start = (bf16[8,3712]{1,0:T(8,128)(2,1)S(1)}, bf16[8,3712]{1,0:T(8,128)(2,1)S(1)}, u32[]{:S(2)}, u32[]{:S(2)}) collective-permute-start(bf16[8,3712]{1,0:T(8,128)(2,1)S(1)} %pack.1), channel_id=1, source_target_pairs={{0,2},{1,17},{2,0},{3,19},{4,6},{5,21},{6,4},{7,23},{8,10},{9,25},... | collective-permute-start | bytes 178184 | tf_op jit(solution)/shard_map/ppermute | solution.py:111
  12.1 4.6 %collective-permute-start.11 = (bf16[3,4,3584]{2,1,0:T(4,128)(2,1)S(1)}, bf16[3,4,3584]{2,1,0:T(4,128)(2,1)S(1)}, u32[]{:S(2)}, u32[]{:S(2)}) collective-permute-start(bf16[3,4,3584]{2,1,0:T(4,128)(2,1)S(1)} %get-tuple-element.16), channel_id=1, source_target_pairs={{0,2},{1,17},{2,0},{3,19},{4,6},{5,21},{6,4},{7,23},{8,10},{9,25},... | collective-permute-start | bytes 258056 | tf_op jit(solution)/shard_map/ppermute | solution.py:111
  13.8 5.3 %collective-permute-start.7 = (bf16[3,4,3712]{2,1,0:T(4,128)(2,1)S(1)}, bf16[3,4,3712]{2,1,0:T(4,128)(2,1)S(1)}, u32[]{:S(2)}, u32[]{:S(2)}) collective-permute-start(bf16[3,4,3712]{2,1,0:T(4,128)(2,1)S(1)} %get-tuple-element.13), channel_id=1, source_target_pairs={{0,2},{1,17},{2,0},{3,19},{4,6},{5,21},{6,4},{7,23},{8,10},{9,25},... | collective-permute-start | bytes 267272 | tf_op jit(solution)/shard_map/ppermute | solution.py:111
  16.7 8.5 %collective-permute-start.12 = (bf16[6,4,3584]{2,1,0:T(4,128)(2,1)S(1)}, bf16[6,4,3584]{2,1,0:T(4,128)(2,1)S(1)}, u32[]{:S(2)}, u32[]{:S(2)}) collective-permute-start(bf16[6,4,3584]{2,1,0:T(4,128)(2,1)S(1)} %constant_dynamic-update-slice_fusion.2.refs_4_), channel_id=1, source_target_pairs={{0,16},{1,3},{2,18},{3,1},{4,20},{5,7},{6,22},{7,5},{8,24},{9,11},... | collective-permute-start | bytes 516104 | tf_op jit(solution)/shard_map/ppermute | solution.py:111
  19.1 5.5 %collective-permute-start.8 = (bf16[6,4,3712]{2,1,0:T(4,128)(2,1)S(1)}, bf16[6,4,3712]{2,1,0:T(4,128)(2,1)S(1)}, u32[]{:S(2)}, u32[]{:S(2)}) collective-permute-start(bf16[6,4,3712]{2,1,0:T(4,128)(2,1)S(1)} %constant_dynamic-update-slice_fusion.refs_4_), channel_id=1, source_target_pairs={{0,16},{1,3},{2,18},{3,1},{4,20},{5,7},{6,22},{7,5},{8,24},{9,11},... | collective-permute-start | bytes 534536 | tf_op jit(solution)/shard_map/ppermute | solution.py:111
  20.7 4.0 %collective-permute-start.2 = (bf16[16,3712]{1,0:T(8,128)(2,1)S(1)}, bf16[16,3712]{1,0:T(8,128)(2,1)S(1)}, u32[]{:S(2)}, u32[]{:S(2)}) collective-permute-start(bf16[16,3712]{1,0:T(8,128)(2,1)S(1)} %pad_maximum_fusion.refs_0_), channel_id=1, source_target_pairs={{0,1},{1,0},{2,3},{3,2},{4,5},{5,4},{6,7},{7,6},{8,9},{9,8},{10,11... | collective-permute-start | bytes 356360 | tf_op jit(solution)/shard_map/ppermute | solution.py:111
  20.8 5.2 %collective-permute-start.1 = (bf16[16,3712]{1,0:T(8,128)(2,1)S(1)}, bf16[16,3712]{1,0:T(8,128)(2,1)S(1)}, u32[]{:S(2)}, u32[]{:S(2)}) collective-permute-start(bf16[16,3712]{1,0:T(8,128)(2,1)S(1)} %pad_maximum_fusion.refs_0_), channel_id=1, source_target_pairs={{0,16},{1,3},{2,18},{3,1},{4,20},{5,7},{6,22},{7,5},{8,24},{9,11},... | collective-permute-start | bytes 356360 | tf_op jit(solution)/shard_map/ppermute | solution.py:111
  21.4 11.1 %collective-permute-start.9 = (bf16[6,4,3712]{2,1,0:T(4,128)(2,1)S(1)}, bf16[6,4,3712]{2,1,0:T(4,128)(2,1)S(1)}, u32[]{:S(2)}, u32[]{:S(2)}) collective-permute-start(bf16[6,4,3712]{2,1,0:T(4,128)(2,1)S(1)} %constant_dynamic-update-slice_fusion.refs_4_), channel_id=1, source_target_pairs={{0,1},{1,0},{2,3},{3,2},{4,5},{5,4},{6,7},{7,6},{8,9},{9,8},{10,11... | collective-permute-start | bytes 534536 | tf_op jit(solution)/shard_map/ppermute | solution.py:111
  24.7 7.8 %collective-permute-start.10 = (bf16[6,4,3712]{2,1,0:T(4,128)(2,1)S(1)}, bf16[6,4,3712]{2,1,0:T(4,128)(2,1)S(1)}, u32[]{:S(2)}, u32[]{:S(2)}) collective-permute-start(bf16[6,4,3712]{2,1,0:T(4,128)(2,1)S(1)} %collective-permute-done.8.refs_5_), channel_id=1, source_target_pairs={{0,1},{1,0},{2,3},{3,2},{4,5},{5,4},{6,7},{7,6},{8,9},{9,8},{10,11... | collective-permute-start | bytes 534536 | tf_op jit(solution)/shard_map/ppermute | solution.py:111
  24.7 6.4 %collective-permute-start.13 = (bf16[6,4,3584]{2,1,0:T(4,128)(2,1)S(1)}, bf16[6,4,3584]{2,1,0:T(4,128)(2,1)S(1)}, u32[]{:S(2)}, u32[]{:S(2)}) collective-permute-start(bf16[6,4,3584]{2,1,0:T(4,128)(2,1)S(1)} %constant_dynamic-update-slice_fusion.2.refs_4_), channel_id=1, source_target_pairs={{0,1},{1,0},{2,3},{3,2},{4,5},{5,4},{6,7},{7,6},{8,9},{9,8},{10,11... | collective-permute-start | bytes 516104 | tf_op jit(solution)/shard_map/ppermute | solution.py:111
  25.2 5.9 %collective-permute-start.14 = (bf16[6,4,3584]{2,1,0:T(4,128)(2,1)S(1)}, bf16[6,4,3584]{2,1,0:T(4,128)(2,1)S(1)}, u32[]{:S(2)}, u32[]{:S(2)}) collective-permute-start(bf16[6,4,3584]{2,1,0:T(4,128)(2,1)S(1)} %collective-permute-done.12.refs_5_), channel_id=1, source_target_pairs={{0,1},{1,0},{2,3},{3,2},{4,5},{5,4},{6,7},{7,6},{8,9},{9,8},{10,11... | collective-permute-start | bytes 516104 | tf_op jit(solution)/shard_map/ppermute | solution.py:111
  25.9 5.1 %collective-permute-start.3 = (bf16[16,3712]{1,0:T(8,128)(2,1)S(1)}, bf16[16,3712]{1,0:T(8,128)(2,1)S(1)}, u32[]{:S(2)}, u32[]{:S(2)}) collective-permute-start(bf16[16,3712]{1,0:T(8,128)(2,1)S(1)} %collective-permute-done.1.refs_1_), channel_id=1, source_target_pairs={{0,1},{1,0},{2,3},{3,2},{4,5},{5,4},{6,7},{7,6},{8,9},{9,8},{10,11... | collective-permute-start | bytes 356360 | tf_op jit(solution)/shard_map/ppermute | solution.py:111
  34.4 3.6 %collective-permute-start.15 = (bf16[48,3584]{1,0:T(8,128)(2,1)S(1)}, bf16[48,3584]{1,0:T(8,128)(2,1)S(1)}, u32[]{:S(2)}, u32[]{:S(2)}) collective-permute-start(bf16[48,3584]{1,0:T(8,128)(2,1)S(1)} %get-tuple-element.20), channel_id=1, source_target_pairs={{0,1},{1,0},{2,3},{3,2},{4,5},{5,4},{6,7},{7,6},{8,9},{9,8},{10,11... | collective-permute-start | bytes 1032200 | tf_op jit(solution)/shard_map/ppermute | solution.py:111
  35.0 1.4 %collective-permute-start.17 = (bf16[16,3584]{1,0:T(8,128)(2,1)S(1)}, bf16[16,3584]{1,0:T(8,128)(2,1)S(1)}, u32[]{:S(2)}, u32[]{:S(2)}) collective-permute-start(bf16[16,3584]{1,0:T(8,128)(2,1)S(1)} %get-tuple-element.21), channel_id=1, source_target_pairs={{0,1},{1,0},{2,3},{3,2},{4,5},{5,4},{6,7},{7,6},{8,9},{9,8},{10,11... | collective-permute-start | bytes 344072 | tf_op jit(solution)/shard_map/ppermute | solution.py:111
  36.5 4.9 %collective-permute-start.18 = (bf16[16,3584]{1,0:T(8,128)(2,1)S(1)}, bf16[16,3584]{1,0:T(8,128)(2,1)S(1)}, u32[]{:S(2)}, u32[]{:S(2)}) collective-permute-start(bf16[16,3584]{1,0:T(8,128)(2,1)S(1)} %add.55), channel_id=1, source_target_pairs={{0,16},{1,3},{2,18},{3,1},{4,20},{5,7},{6,22},{7,5},{8,24},{9,11},... | collective-permute-start | bytes 344072 | tf_op jit(solution)/shard_map/ppermute | solution.py:111
  38.1 4.9 %collective-permute-start.16 = (bf16[16,3584]{1,0:T(8,128)(2,1)S(1)}, bf16[16,3584]{1,0:T(8,128)(2,1)S(1)}, u32[]{:S(2)}, u32[]{:S(2)}) collective-permute-start(bf16[16,3584]{1,0:T(8,128)(2,1)S(1)} %add.54), channel_id=1, source_target_pairs={{0,16},{1,3},{2,18},{3,1},{4,20},{5,7},{6,22},{7,5},{8,24},{9,11},... | collective-permute-start | bytes 344072 | tf_op jit(solution)/shard_map/ppermute | solution.py:111
  41.4 4.9 %collective-permute-start.19 = (bf16[16,3584]{1,0:T(8,128)(2,1)S(1)}, bf16[16,3584]{1,0:T(8,128)(2,1)S(1)}, u32[]{:S(2)}, u32[]{:S(2)}) collective-permute-start(bf16[16,3584]{1,0:T(8,128)(2,1)S(1)} %add.56), channel_id=1, source_target_pairs={{0,2},{1,17},{2,0},{3,19},{4,6},{5,21},{6,4},{7,23},{8,10},{9,25},... | collective-permute-start | bytes 344072 | tf_op jit(solution)/shard_map/ppermute | solution.py:111
  46.3 9.7 %collective-permute-start.20 = (bf16[4,3584]{1,0:T(4,128)(2,1)S(1)}, bf16[4,3584]{1,0:T(4,128)(2,1)S(1)}, u32[]{:S(2)}, u32[]{:S(2)}) collective-permute-start(bf16[4,3584]{1,0:T(4,128)(2,1)S(1)} %get-tuple-element.26), channel_id=1, source_target_pairs={{0,12},{1,13},{2,14},{3,15},{4,8},{5,9},{6,10},{7,11},{8,4},{9,5},... | collective-permute-start | bytes 86024 | tf_op jit(solution)/shard_map/ppermute | solution.py:111
  49.3 6.7 %collective-permute-start.22 = (bf16[4,3584]{1,0:T(4,128)(2,1)S(1)}, bf16[4,3584]{1,0:T(4,128)(2,1)S(1)}, u32[]{:S(2)}, u32[]{:S(2)}) collective-permute-start(bf16[4,3584]{1,0:T(4,128)(2,1)S(1)} %get-tuple-element.27), channel_id=1, source_target_pairs={{0,8},{1,9},{2,10},{3,11},{4,12},{5,13},{6,14},{7,15},{8,0},{9,1},... | collective-permute-start | bytes 86024 | tf_op jit(solution)/shard_map/ppermute | solution.py:111
  49.3 6.7 %collective-permute-start.21 = (bf16[4,3584]{1,0:T(4,128)(2,1)S(1)}, bf16[4,3584]{1,0:T(4,128)(2,1)S(1)}, u32[]{:S(2)}, u32[]{:S(2)}) collective-permute-start(bf16[4,3584]{1,0:T(4,128)(2,1)S(1)} %get-tuple-element.28), channel_id=1, source_target_pairs={{0,4},{1,5},{2,6},{3,7},{4,0},{5,1},{6,2},{7,3},{8,12},{9,13},{10,... | collective-permute-start | bytes 86024 | tf_op jit(solution)/shard_map/ppermute | solution.py:111
  (2 other events, 5.2 us)

commit v7 on v6

--- a/solution.py
+++ b/solution.py
@@ -160,60 +160,74 @@
 
 
 def split_kernel(*refs):
-    in_ref, grad_ref = refs[-2:]
+    all_ref, in_ref, grad_ref = refs[-3:]
     _, rows, width = in_ref.shape
-    for n, ref in enumerate(refs[:-2]):
+    for n, ref in enumerate(refs[:-3]):
+        all_ref[2 * n * rows : 2 * (n + 1) * rows, :] = ref[...]
         in_ref[n] = ref[:rows, :width]
         grad_ref[n] = ref[rows:, :]
 
 
 def split(blocks, width):
     rows, wide = blocks[0].shape
-    n, rows = len(blocks), rows // 2
+    n, half = len(blocks), rows // 2
     return pl.pallas_call(
         split_kernel,
         out_shape=(
-            jax.ShapeDtypeStruct((n, rows, width), BF16),
-            jax.ShapeDtypeStruct((n, rows, wide), BF16),
+            jax.ShapeDtypeStruct((n * rows, wide), BF16),
+            jax.ShapeDtypeStruct((n, half, width), BF16),
+            jax.ShapeDtypeStruct((n, half, wide), BF16),
         ),
         in_specs=[WHOLE] * n,
-        out_specs=(WHOLE,) * 2,
+        out_specs=(WHOLE,) * 3,
         compiler_params=room(2),
         cost_estimate=QUICK,
         name="split",
     )(*blocks)
 
 
-def place(near, away, skip, rows):
-    tok_dev, width = away[0].shape[1], rows.shape[1]
+def place(pieces, skip, rows):
+    tok_dev, width = pieces[2].shape[1], rows.shape[1]
     start = 0
-    for block, others in zip(near, away):
-        pack_rows = block.shape[0] // 2
-        per = others.shape[0] // 2
+
+    def put(block):
+        nonlocal start
+        rows[start : start + tok_dev, :] = block
+        start += tok_dev
+
+    def packed(ref, n):
+        first = n * 2 * tok_dev + skip
+        return ref[first : first + tok_dev, :width]
+
+    for k in range(0, len(pieces), 5):
+        near, near_two, both, second, corner = pieces[k : k + 5]
+        per = corner.shape[0]
         for p in range(2):
-            first = p * pack_rows + skip
-            rows[start : start + tok_dev, :] = block[first : first + tok_dev, :width]
-            start += tok_dev
+            put(packed(near, p))
             for n in range(per):
-                rows[start : start + tok_dev, :] = others[p * per + n]
-                start += tok_dev
-
-
-def lay_kernel(n, *refs):
-    place(refs[:n], refs[n : 2 * n], 0, refs[2 * n])
-
-
-def lay(near, away, rows):
-    n = len(near)
-    return pl.pallas_call(
-        functools.partial(lay_kernel, n),
-        out_shape=jax.ShapeDtypeStruct((rows, away[0].shape[2]), BF16),
-        in_specs=[WHOLE] * (2 * n),
+                put(both[p * per + n])
+        put(packed(near_two, 0))
+        for n in range(per):
+            put(packed(second, n))
+        put(packed(near_two, 1))
+        for n in range(per):
+            put(corner[n])
+
+
+def lay_kernel(*refs):
+    place(refs[:-1], 0, refs[-1])
+
+
+def lay(pieces, rows):
+    return pl.pallas_call(
+        lay_kernel,
+        out_shape=jax.ShapeDtypeStruct((rows, pieces[2].shape[2]), BF16),
+        in_specs=[WHOLE] * len(pieces),
         out_specs=WHOLE,
         compiler_params=room(4),
         cost_estimate=QUICK,
         name="lay",
-    )(*near, *away)
+    )(*pieces)
 
 
 def turn_kernel(n, *refs):
@@ -250,9 +264,9 @@
 
 
 def backward_kernel(n, width, *refs):
-    near, away, refs = refs[:n], refs[n : 2 * n], refs[2 * n :]
+    pieces, refs = refs[:n], refs[n:]
     down_t, gate_t, up_t, gate_by, up_by, scaled, own, *others, placed = refs
-    place(near, away, away[0].shape[1], placed)
+    place(pieces, pieces[2].shape[1], placed)
     expert = lax.axis_index("ep")
     spread = placed[:, width:].astype(F32)
     lane = lax.broadcasted_iota(jnp.int32, spread.shape, 1)
@@ -275,8 +289,8 @@
             start += other.shape[0]
 
 
-def backward(near, away, down_t, gate_t, up_t, gate_by, up_by):
-    n = len(near)
+def backward(pieces, down_t, gate_t, up_t, gate_by, up_by):
+    n = len(pieces)
     rows = gate_by.shape[0]
     width = down_t.shape[0]
     return pl.pallas_call(
@@ -287,13 +301,13 @@
             jax.ShapeDtypeStruct((rows * 3 // 8, width), BF16),
             jax.ShapeDtypeStruct((rows // 8, width), BF16),
         ),
-        in_specs=[WHOLE] * (2 * n + 5),
+        in_specs=[WHOLE] * (n + 5),
         out_specs=(WHOLE,) * 4,
-        scratch_shapes=[pltpu.VMEM((rows, away[0].shape[2]), BF16)],
+        scratch_shapes=[pltpu.VMEM((rows, pieces[2].shape[2]), BF16)],
         compiler_params=room(24),
         cost_estimate=QUICK,
         name="backward",
-    )(*near, *away, down_t, gate_t, up_t, gate_by, up_by)
+    )(*pieces, down_t, gate_t, up_t, gate_by, up_by)
 
 
 def outer_kernel(start, hidden_t, scaled, *refs):
@@ -360,23 +374,31 @@
     two = lambda i: i ^ 2 if i & 1 else i ^ n_ep
     core = lambda i: i ^ 1
 
-    def gather(column):
-        half = jnp.concatenate([column, swap(column, one)], axis=0)
-        other = swap(half, core)
-        rest = swap(half, two)
-        return [half, rest, other, swap(rest, core)]
-
     mine = pack(activations, out_grad, route_weights, expert_ids, n_ep)
     blocks = {j: swap(mine, lambda i, j=j: i ^ j) for j in far}
-    near = gather(mine)
-    far_in, far_grad = split([blocks[j] for j in sorted(far)], width)
+    near = jnp.concatenate([mine, swap(mine, one)], axis=0)
+    near_two = swap(near, two)
+    near = (near, swap(near, core))
+    near_two = (near_two, swap(near_two, core))
+    all_far, far_in, far_grad = split([blocks[j] for j in sorted(far)], width)
+    second = swap(all_far, two)
+    second = (second, swap(second, core))
+
+    def gather(column):
+        first = swap(column, one)
+        both = jnp.concatenate([column, first], axis=0)
+        both = (both, swap(both, core))
+        corner = swap(first, two)
+        corner = (corner, swap(corner, core))
+        return [x[k] for k in range(2) for x in (near, near_two, both, second, corner)]
+
     rows_in = gather(far_in)
     rows_grad = gather(far_grad)
     gate_w, up_w = w_gate[0], w_up[0]
     gate_t, up_t = turn(gate_w, up_w)
     (down_t,) = turn(w_down[0])
     rows = tok_dev * n_ep * n_sp
-    placed = lay(near, rows_in, rows)
+    placed = lay(rows_in, rows)
 
     gate_by, up_by, hidden_t = pl.pallas_call(
         forward_kernel,
@@ -392,7 +414,7 @@
         name="forward",
     )(placed, gate_w, up_w)
     scaled, kept, other, other_corner = backward(
-        near, rows_grad, down_t, gate_t, up_t, gate_by, up_by
+        rows_grad, down_t, gate_t, up_t, gate_by, up_by
     )
     weight_grad = ()
     for start, chunks in ((0, 2), (2, 2), (4, 4)):

time: 56.8 us -> 56.9 us (level)
  starting transfers between devices: 22.4 us -> 24.4 us
  waiting for transfers between devices: 17.7 us -> 15.8 us
    ppermute x23 -> x25, starting transfers between devices: 22.4 us -> 24.4 us  [exchange(): return lax.ppermute(value, ('sp', 'ep'), pairs)]
    ppermute x23 -> x25, waiting for transfers between devices: 17.7 us -> 15.8 us  [exchange(): return lax.ppermute(value, ('sp', 'ep'), pairs)]
  transfers between devices with their start and end apart: 23 -> 25, of which waited for: 9 -> 10; matrix products, arithmetic and copies ran while one was open for 0% -> 0% of each run, Pallas kernels for 17% -> 17%
where the time goes in v7:
time: 56.9 us; the launch traced here: 56.8 us
  starting transfers between devices  24.4 us (43%)
  waiting for transfers between devices  15.8 us (28%)
  Pallas kernels  12.7 us (22%)
  local copies, waits for them, and re-layouts  2.35 us (4%)
  between operations  0.85 us (1%)
  other arithmetic  0.71 us (1%)
    ppermute x25, starting transfers between devices, exchange(): return lax.ppermute(value, ('sp', 'ep'), pairs)  24.4 us
    ppermute x25, waiting for transfers between devices, exchange(): return lax.ppermute(value, ('sp', 'ep'), pairs)  15.8 us
    pallas_call x3, Pallas kernels, outer(): pl.pallas_call(functools.partial(outer_kernel, start * (units // 8)), out...  5.17 us
    pallas_call x2, Pallas kernels, turn(): pl.pallas_call(functools.partial(turn_kernel, n), out_shape=[jax.ShapeDty...  2.93 us
    unnamed x8, local copies, waits for them, and re-layouts  2.23 us
    pallas_call x1, Pallas kernels, backward(): pl.pallas_call(functools.partial(backward_kernel, n, width), out_shape=(j...  1.92 us
    pallas_call x1, Pallas kernels, dense(): pl.pallas_call(forward_kernel, out_shape=(jax.ShapeDtypeStruct((rows, uni...  1.22 us
  transfers between devices with their start and end apart: 25, of which 10 were waited for; matrix products, arithmetic and copies ran while one was open for 0% of the time, Pallas kernels for 17%

profile of v7, /device:TPU:0, one launch (start us, length us, event | category | flops | bytes accessed | tf_op | source)
XLA Modules:
  0.0 56.8 jit_solution(7319522804755365485)
XLA Ops:
  0.6 1.1 %pack.1 = bf16[8,3712]{1,0:T(8,128)(2,1)S(1)} custom-call(bf16[1,4,3584]{2,1,0:T(4,128)(2,1)} %in_ref.1, bf16[1,4,3584]{2,1,0:T(4,128)(2,1)} %grad_ref.1, bf16[1,4,8]{2,1,0:T(4,128)(2,1)} %weight_ref.1, s32[1,4,8]{2,1,0:T(4,128)} %ids_ref.1), custom_call_target="tpu_custom_call" | custom-call | flops 10000000000 | tf_op jit(solution)/shard_map/pack/pallas_call | solution.py:145
  1.7 3.1 %collective-permute-start = (bf16[8,3712]{1,0:T(8,128)(2,1)S(1)}, bf16[8,3712]{1,0:T(8,128)(2,1)S(1)}, u32[]{:S(2)}, u32[]{:S(2)}) collective-permute-start(bf16[8,3712]{1,0:T(8,128)(2,1)S(1)} %pack.1), channel_id=1, source_target_pairs={{0,2},{1,17},{2,0},{3,19},{4,6},{5,21},{6,4},{7,23},{8,10},{9,25},... | collective-permute-start | bytes 178184 | tf_op jit(solution)/shard_map/ppermute | solution.py:111
  4.8 3.6 %collective-permute-start.4 = (bf16[8,3712]{1,0:T(8,128)(2,1)S(1)}, bf16[8,3712]{1,0:T(8,128)(2,1)S(1)}, u32[]{:S(2)}, u32[]{:S(2)}) collective-permute-start(bf16[8,3712]{1,0:T(8,128)(2,1)S(1)} %pack.1), channel_id=1, source_target_pairs={{0,12},{1,13},{2,14},{3,15},{4,8},{5,9},{6,10},{7,11},{8,4},{9,5},... | collective-permute-start | bytes 178184 | tf_op jit(solution)/shard_map/ppermute | solution.py:111
  9.3 1.6 %collective-permute-start.1 = (bf16[16,3712]{1,0:T(8,128)(2,1)S(1)}, bf16[16,3712]{1,0:T(8,128)(2,1)S(1)}, u32[]{:S(2)}, u32[]{:S(2)}) collective-permute-start(bf16[16,3712]{1,0:T(8,128)(2,1)S(1)} %pad_maximum_fusion.refs_0_), channel_id=1, source_target_pairs={{0,16},{1,3},{2,18},{3,1},{4,20},{5,7},{6,22},{7,5},{8,24},{9,11},... | collective-permute-start | bytes 356360 | tf_op jit(solution)/shard_map/ppermute | solution.py:111
  11.4 2.1 %collective-permute-done.3.refs_1_ = bf16[8,3712]{1,0:T(8,128)(2,1)S(1)} collective-permute-done((bf16[8,3712]{1,0:T(8,128)(2,1)S(1)}, bf16[8,3712]{1,0:T(8,128)(2,1)S(1)}, u32[]{:S(2)}, u32[]{:S(2)}) %collective-permute-start.3) | collective-permute-done | bytes 59424 | tf_op jit(solution)/shard_map/ppermute | solution.py:111
  13.6 1.1 %collective-permute-start.13 = (bf16[3,4,3584]{2,1,0:T(4,128)(2,1)S(1)}, bf16[3,4,3584]{2,1,0:T(4,128)(2,1)S(1)}, u32[]{:S(2)}, u32[]{:S(2)}) collective-permute-start(bf16[3,4,3584]{2,1,0:T(4,128)(2,1)S(1)} %get-tuple-element.18), channel_id=1, source_target_pairs={{0,2},{1,17},{2,0},{3,19},{4,6},{5,21},{6,4},{7,23},{8,10},{9,25},... | collective-permute-start | bytes 258056 | tf_op jit(solution)/shard_map/ppermute | solution.py:111
  15.8 1.6 %collective-permute-start.6 = (bf16[24,3712]{1,0:T(8,128)(2,1)S(1)}, bf16[24,3712]{1,0:T(8,128)(2,1)S(1)}, u32[]{:S(2)}, u32[]{:S(2)}) collective-permute-start(bf16[24,3712]{1,0:T(8,128)(2,1)S(1)} %get-tuple-element.15), channel_id=1, source_target_pairs={{0,16},{1,3},{2,18},{3,1},{4,20},{5,7},{6,22},{7,5},{8,24},{9,11},... | collective-permute-start | bytes 534536 | tf_op jit(solution)/shard_map/ppermute | solution.py:111
  17.3 1.7 %collective-permute-done.13 = bf16[3,4,3584]{2,1,0:T(4,128)(2,1)S(1)} collective-permute-done((bf16[3,4,3584]{2,1,0:T(4,128)(2,1)S(1)}, bf16[3,4,3584]{2,1,0:T(4,128)(2,1)S(1)}, u32[]{:S(2)}, u32[]{:S(2)}) %collective-permute-start.13) | collective-permute-done | bytes 86048 | tf_op jit(solution)/shard_map/ppermute | solution.py:111
  19.0 1.5 %collective-permute-start.14 = (bf16[3,4,3584]{2,1,0:T(4,128)(2,1)S(1)}, bf16[3,4,3584]{2,1,0:T(4,128)(2,1)S(1)}, u32[]{:S(2)}, u32[]{:S(2)}) collective-permute-start(bf16[3,4,3584]{2,1,0:T(4,128)(2,1)S(1)} %collective-permute-done.13), channel_id=1, source_target_pairs={{0,16},{1,3},{2,18},{3,1},{4,20},{5,7},{6,22},{7,5},{8,24},{9,11},... | collective-permute-start | bytes 258056 | tf_op jit(solution)/shard_map/ppermute | solution.py:111
  21.1 1.3 %collective-permute-start.7 = (bf16[3,4,3712]{2,1,0:T(4,128)(2,1)S(1)}, bf16[3,4,3712]{2,1,0:T(4,128)(2,1)S(1)}, u32[]{:S(2)}, u32[]{:S(2)}) collective-permute-start(bf16[3,4,3712]{2,1,0:T(4,128)(2,1)S(1)} %collective-permute-done.5), channel_id=1, source_target_pairs={{0,16},{1,3},{2,18},{3,1},{4,20},{5,7},{6,22},{7,5},{8,24},{9,11},... | collective-permute-start | bytes 267272 | tf_op jit(solution)/shard_map/ppermute | solution.py:111
  23.5 2.1 %collective-permute-done.7.refs_4_ = bf16[3,4,3712]{2,1,0:T(4,128)(2,1)S(1)} collective-permute-done((bf16[3,4,3712]{2,1,0:T(4,128)(2,1)S(1)}, bf16[3,4,3712]{2,1,0:T(4,128)(2,1)S(1)}, u32[]{:S(2)}, u32[]{:S(2)}) %collective-permute-start.7) | collective-permute-done | bytes 89120 | tf_op jit(solution)/shard_map/ppermute | solution.py:111
  28.2 1.1 %copy-done.1 = bf16[1,3584,512]{2,1,0:T(8,128)(2,1)S(1)} copy-done((bf16[1,3584,512]{2,1,0:T(8,128)(2,1)S(1)}, bf16[1,3584,512]{2,1,0:T(8,128)(2,1)}, u32[]{:S(2)}) %copy-start.1) | copy-done | bytes 3670040
  29.3 1.9 %turn.3 = (bf16[512,3584]{1,0:T(8,128)(2,1)S(1)}, bf16[512,3584]{1,0:T(8,128)(2,1)S(1)}) custom-call(bf16[3584,512]{1,0:T(8,128)(2,1)S(1)} %bitcast.6, bf16[3584,512]{1,0:T(8,128)(2,1)S(1)} %bitcast.8), custom_call_target="tpu_custom_call" | custom-call | flops 1000000 | tf_op jit(solution)/shard_map/turn/pallas_call | solution.py:242
  31.5 1.2 %forward.1 = (f32[128,512]{1,0:T(8,128)S(1)}, f32[128,512]{1,0:T(8,128)S(1)}, bf16[512,128]{1,0:T(8,128)(2,1)S(1)}) custom-call(bf16[128,3584]{1,0:T(8,128)(2,1)S(1)} %lay.1.rows, bf16[3584,512]{1,0:T(8,128)(2,1)S(1)} %bitcast.7, bf16[3584,512]{1,0:T(8,128)(2,1)S(1)} %bitcast.9), custom_call_target="tpu_custom_call" | custom-call | flops 1000000 | tf_op jit(solution)/shard_map/forward/pallas_call | solution.py:403
  32.7 1.9 %backward.1 = (bf16[128,3584]{1,0:T(8,128)(2,1)S(1)}, bf16[64,3584]{1,0:T(8,128)(2,1)S(1)}, bf16[48,3584]{1,0:T(8,128)(2,1)S(1)}, bf16[16,3584]{1,0:T(8,128)(2,1)S(1)}) custom-call(bf16[16,3712]{1,0:T(8,128)(2,1)S(1)} %pad_maximum_fusion.refs_0_, bf16[16,3712]{1,0:T(8,128)(2,1)S(1)} %collective-permute-done.1.refs_1_, ...), custom_call_target="tpu_custom_call" | custom-call | flops 1000000 | tf_op jit(solution)/shard_map/backward/pallas_call | solution.py:296
  35.2 1.3 %collective-permute-done.19.refs_1_ = bf16[16,3584]{1,0:T(8,128)(2,1)S(1)} collective-permute-done((bf16[16,3584]{1,0:T(8,128)(2,1)S(1)}, bf16[16,3584]{1,0:T(8,128)(2,1)S(1)}, u32[]{:S(2)}, u32[]{:S(2)}) %collective-permute-start.19) | collective-permute-done | bytes 114720 | tf_op jit(solution)/shard_map/ppermute | solution.py:111
  36.6 1.3 %collective-permute-start.20 = (bf16[16,3584]{1,0:T(8,128)(2,1)S(1)}, bf16[16,3584]{1,0:T(8,128)(2,1)S(1)}, u32[]{:S(2)}, u32[]{:S(2)}) collective-permute-start(bf16[16,3584]{1,0:T(8,128)(2,1)S(1)} %add.55), channel_id=1, source_target_pairs={{0,16},{1,3},{2,18},{3,1},{4,20},{5,7},{6,22},{7,5},{8,24},{9,11},... | collective-permute-start | bytes 344072 | tf_op jit(solution)/shard_map/ppermute | solution.py:111
  38.8 2.7 %collective-permute-done.20.refs_2_ = bf16[16,3584]{1,0:T(8,128)(2,1)S(1)} collective-permute-done((bf16[16,3584]{1,0:T(8,128)(2,1)S(1)}, bf16[16,3584]{1,0:T(8,128)(2,1)S(1)}, u32[]{:S(2)}, u32[]{:S(2)}) %collective-permute-start.20) | collective-permute-done | bytes 114720 | tf_op jit(solution)/shard_map/ppermute | solution.py:111
  42.7 3.6 %collective-permute-done.21 = bf16[16,3584]{1,0:T(8,128)(2,1)S(1)} collective-permute-done((bf16[16,3584]{1,0:T(8,128)(2,1)S(1)}, bf16[16,3584]{1,0:T(8,128)(2,1)S(1)}, u32[]{:S(2)}, u32[]{:S(2)}) %collective-permute-start.21) | collective-permute-done | bytes 114720 | tf_op jit(solution)/shard_map/ppermute | solution.py:111
  46.4 2.4 %collective-permute-start.22 = (bf16[4,3584]{1,0:T(4,128)(2,1)S(1)}, bf16[4,3584]{1,0:T(4,128)(2,1)S(1)}, u32[]{:S(2)}, u32[]{:S(2)}) collective-permute-start(bf16[4,3584]{1,0:T(4,128)(2,1)S(1)} %get-tuple-element.28), channel_id=1, source_target_pairs={{0,12},{1,13},{2,14},{3,15},{4,8},{5,9},{6,10},{7,11},{8,4},{9,5},... | collective-permute-start | bytes 86024 | tf_op jit(solution)/shard_map/ppermute | solution.py:111
  48.9 2.0 %collective-permute-start.23 = (bf16[4,3584]{1,0:T(4,128)(2,1)S(1)}, bf16[4,3584]{1,0:T(4,128)(2,1)S(1)}, u32[]{:S(2)}, u32[]{:S(2)}) collective-permute-start(bf16[4,3584]{1,0:T(4,128)(2,1)S(1)} %get-tuple-element.30), channel_id=1, source_target_pairs={{0,4},{1,5},{2,6},{3,7},{4,0},{5,1},{6,2},{7,3},{8,12},{9,13},{10,... | collective-permute-start | bytes 86024 | tf_op jit(solution)/shard_map/ppermute | solution.py:111
  50.9 1.5 %outer.3.refs_0_ = f32[512,3584]{1,0:T(8,128)} custom-call(bf16[512,128]{1,0:T(8,128)(2,1)S(1)} %get-tuple-element.24.hidden_t, bf16[128,3584]{1,0:T(8,128)(2,1)S(1)} %get-tuple-element.25.scaled), custom_call_target="tpu_custom_call" | custom-call | flops 1000000 | tf_op jit(solution)/shard_map/outer/pallas_call | solution.py:328
  52.4 1.5 %outer.4.refs_0_ = f32[512,3584]{1,0:T(8,128)} custom-call(bf16[512,128]{1,0:T(8,128)(2,1)S(1)} %get-tuple-element.24.hidden_t, bf16[128,3584]{1,0:T(8,128)(2,1)S(1)} %get-tuple-element.25.scaled, f32[512,3584]{1,0:T(8,128)} %outer.3.refs_0_), custom_call_target="tpu_custom_call", output_to_operand_aliasing={{}: (2, {})} | custom-call | flops 1000000 | tf_op jit(solution)/shard_map/outer/pallas_call | solution.py:328
  53.9 2.1 %outer.5 = f32[512,3584]{1,0:T(8,128)} custom-call(bf16[512,128]{1,0:T(8,128)(2,1)S(1)} %get-tuple-element.24.hidden_t, bf16[128,3584]{1,0:T(8,128)(2,1)S(1)} %get-tuple-element.25.scaled, f32[512,3584]{1,0:T(8,128)} %outer.4.refs_0_), custom_call_target="tpu_custom_call", output_to_operand_aliasing={{}: (2, {})} | custom-call | flops 1000000 | tf_op jit(solution)/shard_map/outer/pallas_call | solution.py:328
  (53 shorter events, 10.7 us)
Async XLA Ops:
  1.7 7.5 %collective-permute-start = (bf16[8,3712]{1,0:T(8,128)(2,1)S(1)}, bf16[8,3712]{1,0:T(8,128)(2,1)S(1)}, u32[]{:S(2)}, u32[]{:S(2)}) collective-permute-start(bf16[8,3712]{1,0:T(8,128)(2,1)S(1)} %pack.1), channel_id=1, source_target_pairs={{0,2},{1,17},{2,0},{3,19},{4,6},{5,21},{6,4},{7,23},{8,10},{9,25},... | collective-permute-start | bytes 178184 | tf_op jit(solution)/shard_map/ppermute | solution.py:111
  4.8 6.6 %collective-permute-start.4 = (bf16[8,3712]{1,0:T(8,128)(2,1)S(1)}, bf16[8,3712]{1,0:T(8,128)(2,1)S(1)}, u32[]{:S(2)}, u32[]{:S(2)}) collective-permute-start(bf16[8,3712]{1,0:T(8,128)(2,1)S(1)} %pack.1), channel_id=1, source_target_pairs={{0,12},{1,13},{2,14},{3,15},{4,8},{5,9},{6,10},{7,11},{8,4},{9,5},... | collective-permute-start | bytes 178184 | tf_op jit(solution)/shard_map/ppermute | solution.py:111
  8.4 5.1 %collective-permute-start.3 = (bf16[8,3712]{1,0:T(8,128)(2,1)S(1)}, bf16[8,3712]{1,0:T(8,128)(2,1)S(1)}, u32[]{:S(2)}, u32[]{:S(2)}) collective-permute-start(bf16[8,3712]{1,0:T(8,128)(2,1)S(1)} %pack.1), channel_id=1, source_target_pairs={{0,8},{1,9},{2,10},{3,11},{4,12},{5,13},{6,14},{7,15},{8,0},{9,1},... | collective-permute-start | bytes 178184 | tf_op jit(solution)/shard_map/ppermute | solution.py:111
  8.4 5.1 %collective-permute-start.2 = (bf16[8,3712]{1,0:T(8,128)(2,1)S(1)}, bf16[8,3712]{1,0:T(8,128)(2,1)S(1)}, u32[]{:S(2)}, u32[]{:S(2)}) collective-permute-start(bf16[8,3712]{1,0:T(8,128)(2,1)S(1)} %pack.1), channel_id=1, source_target_pairs={{0,4},{1,5},{2,6},{3,7},{4,0},{5,1},{6,2},{7,3},{8,12},{9,13},{10,... | collective-permute-start | bytes 178184 | tf_op jit(solution)/shard_map/ppermute | solution.py:111
  9.2 11.9 %collective-permute-start.8 = (bf16[16,3712]{1,0:T(8,128)(2,1)S(1)}, bf16[16,3712]{1,0:T(8,128)(2,1)S(1)}, u32[]{:S(2)}, u32[]{:S(2)}) collective-permute-start(bf16[16,3712]{1,0:T(8,128)(2,1)S(1)} %pad_maximum_fusion.refs_0_), channel_id=1, source_target_pairs={{0,1},{1,0},{2,3},{3,2},{4,5},{5,4},{6,7},{7,6},{8,9},{9,8},{10,11... | collective-permute-start | bytes 356360 | tf_op jit(solution)/shard_map/ppermute | solution.py:111
  9.3 13.0 %collective-permute-start.1 = (bf16[16,3712]{1,0:T(8,128)(2,1)S(1)}, bf16[16,3712]{1,0:T(8,128)(2,1)S(1)}, u32[]{:S(2)}, u32[]{:S(2)}) collective-permute-start(bf16[16,3712]{1,0:T(8,128)(2,1)S(1)} %pad_maximum_fusion.refs_0_), channel_id=1, source_target_pairs={{0,16},{1,3},{2,18},{3,1},{4,20},{5,7},{6,22},{7,5},{8,24},{9,11},... | collective-permute-start | bytes 356360 | tf_op jit(solution)/shard_map/ppermute | solution.py:111
  13.6 5.5 %collective-permute-start.13 = (bf16[3,4,3584]{2,1,0:T(4,128)(2,1)S(1)}, bf16[3,4,3584]{2,1,0:T(4,128)(2,1)S(1)}, u32[]{:S(2)}, u32[]{:S(2)}) collective-permute-start(bf16[3,4,3584]{2,1,0:T(4,128)(2,1)S(1)} %get-tuple-element.18), channel_id=1, source_target_pairs={{0,2},{1,17},{2,0},{3,19},{4,6},{5,21},{6,4},{7,23},{8,10},{9,25},... | collective-permute-start | bytes 258056 | tf_op jit(solution)/shard_map/ppermute | solution.py:111
  14.7 6.2 %collective-permute-start.5 = (bf16[3,4,3712]{2,1,0:T(4,128)(2,1)S(1)}, bf16[3,4,3712]{2,1,0:T(4,128)(2,1)S(1)}, u32[]{:S(2)}, u32[]{:S(2)}) collective-permute-start(bf16[3,4,3712]{2,1,0:T(4,128)(2,1)S(1)} %get-tuple-element.14), channel_id=1, source_target_pairs={{0,2},{1,17},{2,0},{3,19},{4,6},{5,21},{6,4},{7,23},{8,10},{9,25},... | collective-permute-start | bytes 267272 | tf_op jit(solution)/shard_map/ppermute | solution.py:111
  15.8 6.5 %collective-permute-start.6 = (bf16[24,3712]{1,0:T(8,128)(2,1)S(1)}, bf16[24,3712]{1,0:T(8,128)(2,1)S(1)}, u32[]{:S(2)}, u32[]{:S(2)}) collective-permute-start(bf16[24,3712]{1,0:T(8,128)(2,1)S(1)} %get-tuple-element.15), channel_id=1, source_target_pairs={{0,16},{1,3},{2,18},{3,1},{4,20},{5,7},{6,22},{7,5},{8,24},{9,11},... | collective-permute-start | bytes 534536 | tf_op jit(solution)/shard_map/ppermute | solution.py:111
  19.0 4.5 %collective-permute-start.14 = (bf16[3,4,3584]{2,1,0:T(4,128)(2,1)S(1)}, bf16[3,4,3584]{2,1,0:T(4,128)(2,1)S(1)}, u32[]{:S(2)}, u32[]{:S(2)}) collective-permute-start(bf16[3,4,3584]{2,1,0:T(4,128)(2,1)S(1)} %collective-permute-done.13), channel_id=1, source_target_pairs={{0,16},{1,3},{2,18},{3,1},{4,20},{5,7},{6,22},{7,5},{8,24},{9,11},... | collective-permute-start | bytes 258056 | tf_op jit(solution)/shard_map/ppermute | solution.py:111
  21.0 11.7 %collective-permute-start.10 = (bf16[6,4,3712]{2,1,0:T(4,128)(2,1)S(1)}, bf16[6,4,3712]{2,1,0:T(4,128)(2,1)S(1)}, u32[]{:S(2)}, u32[]{:S(2)}) collective-permute-start(bf16[6,4,3712]{2,1,0:T(4,128)(2,1)S(1)} %constant_dynamic-update-slice_fusion.refs_2_), channel_id=1, source_target_pairs={{0,1},{1,0},{2,3},{3,2},{4,5},{5,4},{6,7},{7,6},{8,9},{9,8},{10,11... | collective-permute-start | bytes 534536 | tf_op jit(solution)/shard_map/ppermute | solution.py:111
  21.1 4.6 %collective-permute-start.7 = (bf16[3,4,3712]{2,1,0:T(4,128)(2,1)S(1)}, bf16[3,4,3712]{2,1,0:T(4,128)(2,1)S(1)}, u32[]{:S(2)}, u32[]{:S(2)}) collective-permute-start(bf16[3,4,3712]{2,1,0:T(4,128)(2,1)S(1)} %collective-permute-done.5), channel_id=1, source_target_pairs={{0,16},{1,3},{2,18},{3,1},{4,20},{5,7},{6,22},{7,5},{8,24},{9,11},... | collective-permute-start | bytes 267272 | tf_op jit(solution)/shard_map/ppermute | solution.py:111
  22.3 3.3 %collective-permute-start.9 = (bf16[16,3712]{1,0:T(8,128)(2,1)S(1)}, bf16[16,3712]{1,0:T(8,128)(2,1)S(1)}, u32[]{:S(2)}, u32[]{:S(2)}) collective-permute-start(bf16[16,3712]{1,0:T(8,128)(2,1)S(1)} %collective-permute-done.1.refs_1_), channel_id=1, source_target_pairs={{0,1},{1,0},{2,3},{3,2},{4,5},{5,4},{6,7},{7,6},{8,9},{9,8},{10,11... | collective-permute-start | bytes 356360 | tf_op jit(solution)/shard_map/ppermute | solution.py:111
  22.3 9.0 %collective-permute-start.11 = (bf16[24,3712]{1,0:T(8,128)(2,1)S(1)}, bf16[24,3712]{1,0:T(8,128)(2,1)S(1)}, u32[]{:S(2)}, u32[]{:S(2)}) collective-permute-start(bf16[24,3712]{1,0:T(8,128)(2,1)S(1)} %collective-permute-done.6.refs_3_), channel_id=1, source_target_pairs={{0,1},{1,0},{2,3},{3,2},{4,5},{5,4},{6,7},{7,6},{8,9},{9,8},{10,11... | collective-permute-start | bytes 534536 | tf_op jit(solution)/shard_map/ppermute | solution.py:111
  23.5 7.8 %collective-permute-start.15 = (bf16[6,4,3584]{2,1,0:T(4,128)(2,1)S(1)}, bf16[6,4,3584]{2,1,0:T(4,128)(2,1)S(1)}, u32[]{:S(2)}, u32[]{:S(2)}) collective-permute-start(bf16[6,4,3584]{2,1,0:T(4,128)(2,1)S(1)} %constant_dynamic-update-slice_fusion.2.refs_2_), channel_id=1, source_target_pairs={{0,1},{1,0},{2,3},{3,2},{4,5},{5,4},{6,7},{7,6},{8,9},{9,8},{10,11... | collective-permute-start | bytes 516104 | tf_op jit(solution)/shard_map/ppermute | solution.py:111
  25.6 7.1 %collective-permute-start.12 = (bf16[3,4,3712]{2,1,0:T(4,128)(2,1)S(1)}, bf16[3,4,3712]{2,1,0:T(4,128)(2,1)S(1)}, u32[]{:S(2)}, u32[]{:S(2)}) collective-permute-start(bf16[3,4,3712]{2,1,0:T(4,128)(2,1)S(1)} %collective-permute-done.7.refs_4_), channel_id=1, source_target_pairs={{0,1},{1,0},{2,3},{3,2},{4,5},{5,4},{6,7},{7,6},{8,9},{9,8},{10,11... | collective-permute-start | bytes 267272 | tf_op jit(solution)/shard_map/ppermute | solution.py:111
  25.7 5.6 %collective-permute-start.16 = (bf16[3,4,3584]{2,1,0:T(4,128)(2,1)S(1)}, bf16[3,4,3584]{2,1,0:T(4,128)(2,1)S(1)}, u32[]{:S(2)}, u32[]{:S(2)}) collective-permute-start(bf16[3,4,3584]{2,1,0:T(4,128)(2,1)S(1)} %collective-permute-done.14.refs_4_), channel_id=1, source_target_pairs={{0,1},{1,0},{2,3},{3,2},{4,5},{5,4},{6,7},{7,6},{8,9},{9,8},{10,11... | collective-permute-start | bytes 258056 | tf_op jit(solution)/shard_map/ppermute | solution.py:111
  34.7 3.2 %collective-permute-start.17 = (bf16[48,3584]{1,0:T(8,128)(2,1)S(1)}, bf16[48,3584]{1,0:T(8,128)(2,1)S(1)}, u32[]{:S(2)}, u32[]{:S(2)}) collective-permute-start(bf16[48,3584]{1,0:T(8,128)(2,1)S(1)} %get-tuple-element.22), channel_id=1, source_target_pairs={{0,1},{1,0},{2,3},{3,2},{4,5},{5,4},{6,7},{7,6},{8,9},{9,8},{10,11... | collective-permute-start | bytes 1032200 | tf_op jit(solution)/shard_map/ppermute | solution.py:111
  36.6 4.9 %collective-permute-start.20 = (bf16[16,3584]{1,0:T(8,128)(2,1)S(1)}, bf16[16,3584]{1,0:T(8,128)(2,1)S(1)}, u32[]{:S(2)}, u32[]{:S(2)}) collective-permute-start(bf16[16,3584]{1,0:T(8,128)(2,1)S(1)} %add.55), channel_id=1, source_target_pairs={{0,16},{1,3},{2,18},{3,1},{4,20},{5,7},{6,22},{7,5},{8,24},{9,11},... | collective-permute-start | bytes 344072 | tf_op jit(solution)/shard_map/ppermute | solution.py:111
  37.9 4.9 %collective-permute-start.18 = (bf16[16,3584]{1,0:T(8,128)(2,1)S(1)}, bf16[16,3584]{1,0:T(8,128)(2,1)S(1)}, u32[]{:S(2)}, u32[]{:S(2)}) collective-permute-start(bf16[16,3584]{1,0:T(8,128)(2,1)S(1)} %add.54), channel_id=1, source_target_pairs={{0,16},{1,3},{2,18},{3,1},{4,20},{5,7},{6,22},{7,5},{8,24},{9,11},... | collective-permute-start | bytes 344072 | tf_op jit(solution)/shard_map/ppermute | solution.py:111
  41.5 4.9 %collective-permute-start.21 = (bf16[16,3584]{1,0:T(8,128)(2,1)S(1)}, bf16[16,3584]{1,0:T(8,128)(2,1)S(1)}, u32[]{:S(2)}, u32[]{:S(2)}) collective-permute-start(bf16[16,3584]{1,0:T(8,128)(2,1)S(1)} %add.56), channel_id=1, source_target_pairs={{0,2},{1,17},{2,0},{3,19},{4,6},{5,21},{6,4},{7,23},{8,10},{9,25},... | collective-permute-start | bytes 344072 | tf_op jit(solution)/shard_map/ppermute | solution.py:111
  46.4 9.7 %collective-permute-start.22 = (bf16[4,3584]{1,0:T(4,128)(2,1)S(1)}, bf16[4,3584]{1,0:T(4,128)(2,1)S(1)}, u32[]{:S(2)}, u32[]{:S(2)}) collective-permute-start(bf16[4,3584]{1,0:T(4,128)(2,1)S(1)} %get-tuple-element.28), channel_id=1, source_target_pairs={{0,12},{1,13},{2,14},{3,15},{4,8},{5,9},{6,10},{7,11},{8,4},{9,5},... | collective-permute-start | bytes 86024 | tf_op jit(solution)/shard_map/ppermute | solution.py:111
  48.9 7.2 %collective-permute-start.24 = (bf16[4,3584]{1,0:T(4,128)(2,1)S(1)}, bf16[4,3584]{1,0:T(4,128)(2,1)S(1)}, u32[]{:S(2)}, u32[]{:S(2)}) collective-permute-start(bf16[4,3584]{1,0:T(4,128)(2,1)S(1)} %get-tuple-element.29), channel_id=1, source_target_pairs={{0,8},{1,9},{2,10},{3,11},{4,12},{5,13},{6,14},{7,15},{8,0},{9,1},... | collective-permute-start | bytes 86024 | tf_op jit(solution)/shard_map/ppermute | solution.py:111
  48.9 7.2 %collective-permute-start.23 = (bf16[4,3584]{1,0:T(4,128)(2,1)S(1)}, bf16[4,3584]{1,0:T(4,128)(2,1)S(1)}, u32[]{:S(2)}, u32[]{:S(2)}) collective-permute-start(bf16[4,3584]{1,0:T(4,128)(2,1)S(1)} %get-tuple-element.30), channel_id=1, source_target_pairs={{0,4},{1,5},{2,6},{3,7},{4,0},{5,1},{6,2},{7,3},{8,12},{9,13},{10,... | collective-permute-start | bytes 86024 | tf_op jit(solution)/shard_map/ppermute | solution.py:111
  (4 other events, 32.5 us)

commit v8 on v7

--- a/solution.py
+++ b/solution.py
@@ -186,42 +186,64 @@
     )(*blocks)
 
 
-def place(pieces, skip, rows):
-    tok_dev, width = pieces[2].shape[1], rows.shape[1]
+def place(blocks, rows):
     start = 0
-
-    def put(block):
-        nonlocal start
-        rows[start : start + tok_dev, :] = block
-        start += tok_dev
-
-    def packed(ref, n):
-        first = n * 2 * tok_dev + skip
-        return ref[first : first + tok_dev, :width]
-
-    for k in range(0, len(pieces), 5):
-        near, near_two, both, second, corner = pieces[k : k + 5]
-        per = corner.shape[0]
+    for block in blocks:
+        rows[start : start + block.shape[0], :] = block
+        start += block.shape[0]
+
+
+def packed(ref, n, like, skip):
+    tok_dev, width = like.shape[1:]
+    first = n * 2 * tok_dev + skip
+    return ref[first : first + tok_dev, :width]
+
+
+def first_columns(pieces, skip):
+    for k in range(0, len(pieces), 4):
+        near, near_two, both, second = pieces[k : k + 4]
+        per = both.shape[0] // 2
         for p in range(2):
-            put(packed(near, p))
+            yield packed(near, p, both, skip)
             for n in range(per):
-                put(both[p * per + n])
-        put(packed(near_two, 0))
+                yield both[p * per + n]
+        yield packed(near_two, 0, both, skip)
         for n in range(per):
-            put(packed(second, n))
-        put(packed(near_two, 1))
-        for n in range(per):
-            put(corner[n])
-
-
-def lay_kernel(*refs):
-    place(refs[:-1], 0, refs[-1])
-
-
-def lay(pieces, rows):
-    return pl.pallas_call(
-        lay_kernel,
-        out_shape=jax.ShapeDtypeStruct((rows, pieces[2].shape[2]), BF16),
+            yield packed(second, n, both, skip)
+
+
+def last_columns(pieces, skip):
+    for k in range(0, len(pieces), 2):
+        near_two, corner = pieces[k : k + 2]
+        yield packed(near_two, 1, corner, skip)
+        for n in range(corner.shape[0]):
+            yield corner[n]
+
+
+def merged(early, late):
+    n, m = early.shape[0] // 2, late.shape[0] // 2
+    return jnp.concatenate([early[:n], late[:m], early[n:], late[m:]], axis=0)
+
+
+def scaled_rows(placed, width):
+    spread = placed[:, width:].astype(F32)
+    lane = lax.broadcasted_iota(jnp.int32, spread.shape, 1)
+    weight = jnp.sum(jnp.where(lane == lax.axis_index("ep"), spread, 0.0), axis=1, keepdims=True)
+    return (weight * placed[:, :width].astype(F32)).astype(BF16)
+
+
+def lay_in_kernel(*refs):
+    *pieces, out = refs
+    own, corner, other = pieces[:4], pieces[4], pieces[5:]
+    blocks = list(first_columns(own, 0)) + list(last_columns((own[1], corner), 0))
+    place(blocks + list(first_columns(other, 0)), out)
+
+
+def lay(kernel, pieces, width, columns):
+    rows = (pieces[2].shape[0] // 2 + 1) * pieces[2].shape[1] * columns
+    return pl.pallas_call(
+        kernel,
+        out_shape=jax.ShapeDtypeStruct((rows, width), BF16),
         in_specs=[WHOLE] * len(pieces),
         out_specs=WHOLE,
         compiler_params=room(4),
@@ -250,12 +272,15 @@
     )(*weights)
 
 
-def forward_kernel(rows, gate_w, up_w, gate_by, up_by, hidden_t):
+def forward_kernel(n, early, *refs):
+    pieces, (gate_w, up_w, gate_by, up_by, hidden_t, late) = refs[:n], refs[n:]
+    place(last_columns(pieces, 0), late)
+    rows = jnp.concatenate([early[...], late[...]], axis=0)
     step = min(256, gate_w.shape[1])
     for c in range(0, gate_w.shape[1], step):
         cols = slice(c, c + step)
-        gate_pre = jnp.dot(rows[...], gate_w[:, cols], preferred_element_type=F32)
-        up_pre = jnp.dot(rows[...], up_w[:, cols], preferred_element_type=F32)
+        gate_pre = jnp.dot(rows, gate_w[:, cols], preferred_element_type=F32)
+        up_pre = jnp.dot(rows, up_w[:, cols], preferred_element_type=F32)
         squash = jax.nn.sigmoid(gate_pre)
         swish = gate_pre * squash
         gate_by[:, cols] = up_pre * squash * (1.0 + gate_pre * (1.0 - squash))
@@ -263,15 +288,13 @@
         hidden_t[cols, :] = (swish * up_pre).T.astype(BF16)
 
 
-def backward_kernel(n, width, *refs):
-    pieces, refs = refs[:n], refs[n:]
-    down_t, gate_t, up_t, gate_by, up_by, scaled, own, *others, placed = refs
-    place(pieces, pieces[2].shape[1], placed)
-    expert = lax.axis_index("ep")
-    spread = placed[:, width:].astype(F32)
-    lane = lax.broadcasted_iota(jnp.int32, spread.shape, 1)
-    weight = jnp.sum(jnp.where(lane == expert, spread, 0.0), axis=1, keepdims=True)
-    scaled[...] = (weight * placed[:, :width].astype(F32)).astype(BF16)
+def backward_kernel(n, m, width, *refs):
+    firsts, lasts, refs = refs[:n], refs[n : n + m], refs[n + m :]
+    down_t, gate_t, up_t, gate_by, up_by, scaled, own, *others, early, late = refs
+    skip = lasts[1].shape[1]
+    place(first_columns(firsts, skip), early)
+    place(last_columns(lasts, skip), late)
+    scaled[...] = merged(scaled_rows(early, width), scaled_rows(late, width))
     hidden_grad = jnp.dot(scaled[...], down_t[...], preferred_element_type=F32)
     gate_grad = (hidden_grad * gate_by[...]).astype(BF16)
     up_grad = (hidden_grad * up_by[...]).astype(BF16)
@@ -289,25 +312,28 @@
             start += other.shape[0]
 
 
-def backward(pieces, down_t, gate_t, up_t, gate_by, up_by):
-    n = len(pieces)
+def backward(early, pieces, down_t, gate_t, up_t, gate_by, up_by):
+    n, m = len(early), len(pieces)
     rows = gate_by.shape[0]
     width = down_t.shape[0]
     return pl.pallas_call(
-        functools.partial(backward_kernel, n, width),
+        functools.partial(backward_kernel, n, m, width),
         out_shape=(
             jax.ShapeDtypeStruct((rows, width), BF16),
             jax.ShapeDtypeStruct((rows // 2, width), BF16),
             jax.ShapeDtypeStruct((rows * 3 // 8, width), BF16),
             jax.ShapeDtypeStruct((rows // 8, width), BF16),
         ),
-        in_specs=[WHOLE] * (n + 5),
+        in_specs=[WHOLE] * (n + m + 5),
         out_specs=(WHOLE,) * 4,
-        scratch_shapes=[pltpu.VMEM((rows, pieces[2].shape[2]), BF16)],
+        scratch_shapes=[
+            pltpu.VMEM((rows * 3 // 4, pieces[1].shape[2]), BF16),
+            pltpu.VMEM((rows // 4, pieces[1].shape[2]), BF16),
+        ],
         compiler_params=room(24),
         cost_estimate=QUICK,
         name="backward",
-    )(*pieces, down_t, gate_t, up_t, gate_by, up_by)
+    )(*early, *pieces, down_t, gate_t, up_t, gate_by, up_by)
 
 
 def outer_kernel(start, hidden_t, scaled, *refs):
@@ -390,31 +416,36 @@
         both = (both, swap(both, core))
         corner = swap(first, two)
         corner = (corner, swap(corner, core))
-        return [x[k] for k in range(2) for x in (near, near_two, both, second, corner)]
-
-    rows_in = gather(far_in)
-    rows_grad = gather(far_grad)
+        early = [x[k] for k in range(2) for x in (near, near_two, both, second)]
+        return early, [x[k] for k in range(2) for x in (near_two, corner)]
+
+    early_in, late_in = gather(far_in)
+    early_grad, late_grad = gather(far_grad)
     gate_w, up_w = w_gate[0], w_up[0]
     gate_t, up_t = turn(gate_w, up_w)
     (down_t,) = turn(w_down[0])
     rows = tok_dev * n_ep * n_sp
-    placed = lay(rows_in, rows)
+    early_in = early_in[:4] + late_in[1:2] + early_in[4:]
+    early_in = lay(lay_in_kernel, early_in, width, 7)
+    late_in = late_in[2:]
+    n = len(late_in)
 
     gate_by, up_by, hidden_t = pl.pallas_call(
-        forward_kernel,
+        functools.partial(forward_kernel, n),
         out_shape=(
             jax.ShapeDtypeStruct((rows, units), F32),
             jax.ShapeDtypeStruct((rows, units), F32),
             jax.ShapeDtypeStruct((units, rows), BF16),
         ),
-        in_specs=[WHOLE] * 3,
+        in_specs=[WHOLE] * (n + 3),
         out_specs=(WHOLE,) * 3,
+        scratch_shapes=[pltpu.VMEM((rows // 8, width), BF16)],
         compiler_params=room(16),
         cost_estimate=QUICK,
         name="forward",
-    )(placed, gate_w, up_w)
+    )(early_in, *late_in, gate_w, up_w)
     scaled, kept, other, other_corner = backward(
-        rows_grad, down_t, gate_t, up_t, gate_by, up_by
+        early_grad, late_grad, down_t, gate_t, up_t, gate_by, up_by
     )
     weight_grad = ()
     for start, chunks in ((0, 2), (2, 2), (4, 4)):

time: 56.9 us -> 57 us (level)
  no operation moved by 1% of the time
where the time goes in v8:
time: 57 us; the launch traced here: 56.8 us
  starting transfers between devices  24.4 us (43%)
  waiting for transfers between devices  15.8 us (28%)
  Pallas kernels  12.7 us (22%)
  local copies, waits for them, and re-layouts  2.35 us (4%)
  between operations  0.85 us (1%)
  other arithmetic  0.72 us (1%)
    ppermute x25, starting transfers between devices, exchange(): return lax.ppermute(value, ('sp', 'ep'), pairs)  24.4 us
    ppermute x25, waiting for transfers between devices, exchange(): return lax.ppermute(value, ('sp', 'ep'), pairs)  15.8 us
    pallas_call x3, Pallas kernels, outer(): pl.pallas_call(functools.partial(outer_kernel, start * (units // 8)), out...  5.19 us
    pallas_call x2, Pallas kernels, turn(): pl.pallas_call(functools.partial(turn_kernel, n), out_shape=[jax.ShapeDty...  2.93 us
    unnamed x8, local copies, waits for them, and re-layouts  2.23 us
    pallas_call x1, Pallas kernels, backward(): pl.pallas_call(functools.partial(backward_kernel, n, m, width), out_shape...  1.92 us
    pallas_call x1, Pallas kernels, dense(): pl.pallas_call(functools.partial(forward_kernel, n), out_shape=(jax.Shape...  1.28 us
  transfers between devices with their start and end apart: 25, of which 10 were waited for; matrix products, arithmetic and copies ran while one was open for 0% of the time, Pallas kernels for 17%

profile of v8, /device:TPU:0, one launch (start us, length us, event | category | flops | bytes accessed | tf_op | source)
XLA Modules:
  0.0 56.8 jit_solution(11464497916828685877)
XLA Ops:
  0.6 1.1 %pack.1 = bf16[8,3712]{1,0:T(8,128)(2,1)S(1)} custom-call(bf16[1,4,3584]{2,1,0:T(4,128)(2,1)} %in_ref.1, bf16[1,4,3584]{2,1,0:T(4,128)(2,1)} %grad_ref.1, bf16[1,4,8]{2,1,0:T(4,128)(2,1)} %weight_ref.1, s32[1,4,8]{2,1,0:T(4,128)} %ids_ref.1), custom_call_target="tpu_custom_call" | custom-call | flops 10000000000 | tf_op jit(solution)/shard_map/pack/pallas_call | solution.py:145
  1.7 3.1 %collective-permute-start = (bf16[8,3712]{1,0:T(8,128)(2,1)S(1)}, bf16[8,3712]{1,0:T(8,128)(2,1)S(1)}, u32[]{:S(2)}, u32[]{:S(2)}) collective-permute-start(bf16[8,3712]{1,0:T(8,128)(2,1)S(1)} %pack.1), channel_id=1, source_target_pairs={{0,2},{1,17},{2,0},{3,19},{4,6},{5,21},{6,4},{7,23},{8,10},{9,25},... | collective-permute-start | bytes 178184 | tf_op jit(solution)/shard_map/ppermute | solution.py:111
  4.8 3.6 %collective-permute-start.4 = (bf16[8,3712]{1,0:T(8,128)(2,1)S(1)}, bf16[8,3712]{1,0:T(8,128)(2,1)S(1)}, u32[]{:S(2)}, u32[]{:S(2)}) collective-permute-start(bf16[8,3712]{1,0:T(8,128)(2,1)S(1)} %pack.1), channel_id=1, source_target_pairs={{0,12},{1,13},{2,14},{3,15},{4,8},{5,9},{6,10},{7,11},{8,4},{9,5},... | collective-permute-start | bytes 178184 | tf_op jit(solution)/shard_map/ppermute | solution.py:111
  9.3 1.6 %collective-permute-start.1 = (bf16[16,3712]{1,0:T(8,128)(2,1)S(1)}, bf16[16,3712]{1,0:T(8,128)(2,1)S(1)}, u32[]{:S(2)}, u32[]{:S(2)}) collective-permute-start(bf16[16,3712]{1,0:T(8,128)(2,1)S(1)} %pad_maximum_fusion.refs_0_), channel_id=1, source_target_pairs={{0,16},{1,3},{2,18},{3,1},{4,20},{5,7},{6,22},{7,5},{8,24},{9,11},... | collective-permute-start | bytes 356360 | tf_op jit(solution)/shard_map/ppermute | solution.py:111
  11.4 2.1 %collective-permute-done.3.refs_1_ = bf16[8,3712]{1,0:T(8,128)(2,1)S(1)} collective-permute-done((bf16[8,3712]{1,0:T(8,128)(2,1)S(1)}, bf16[8,3712]{1,0:T(8,128)(2,1)S(1)}, u32[]{:S(2)}, u32[]{:S(2)}) %collective-permute-start.3) | collective-permute-done | bytes 59424 | tf_op jit(solution)/shard_map/ppermute | solution.py:111
  13.6 1.1 %collective-permute-start.13 = (bf16[3,4,3584]{2,1,0:T(4,128)(2,1)S(1)}, bf16[3,4,3584]{2,1,0:T(4,128)(2,1)S(1)}, u32[]{:S(2)}, u32[]{:S(2)}) collective-permute-start(bf16[3,4,3584]{2,1,0:T(4,128)(2,1)S(1)} %get-tuple-element.18), channel_id=1, source_target_pairs={{0,2},{1,17},{2,0},{3,19},{4,6},{5,21},{6,4},{7,23},{8,10},{9,25},... | collective-permute-start | bytes 258056 | tf_op jit(solution)/shard_map/ppermute | solution.py:111
  15.8 1.6 %collective-permute-start.6 = (bf16[24,3712]{1,0:T(8,128)(2,1)S(1)}, bf16[24,3712]{1,0:T(8,128)(2,1)S(1)}, u32[]{:S(2)}, u32[]{:S(2)}) collective-permute-start(bf16[24,3712]{1,0:T(8,128)(2,1)S(1)} %get-tuple-element.15), channel_id=1, source_target_pairs={{0,16},{1,3},{2,18},{3,1},{4,20},{5,7},{6,22},{7,5},{8,24},{9,11},... | collective-permute-start | bytes 534536 | tf_op jit(solution)/shard_map/ppermute | solution.py:111
  17.3 1.7 %collective-permute-done.13 = bf16[3,4,3584]{2,1,0:T(4,128)(2,1)S(1)} collective-permute-done((bf16[3,4,3584]{2,1,0:T(4,128)(2,1)S(1)}, bf16[3,4,3584]{2,1,0:T(4,128)(2,1)S(1)}, u32[]{:S(2)}, u32[]{:S(2)}) %collective-permute-start.13) | collective-permute-done | bytes 86048 | tf_op jit(solution)/shard_map/ppermute | solution.py:111
  19.0 1.5 %collective-permute-start.14 = (bf16[3,4,3584]{2,1,0:T(4,128)(2,1)S(1)}, bf16[3,4,3584]{2,1,0:T(4,128)(2,1)S(1)}, u32[]{:S(2)}, u32[]{:S(2)}) collective-permute-start(bf16[3,4,3584]{2,1,0:T(4,128)(2,1)S(1)} %collective-permute-done.13), channel_id=1, source_target_pairs={{0,16},{1,3},{2,18},{3,1},{4,20},{5,7},{6,22},{7,5},{8,24},{9,11},... | collective-permute-start | bytes 258056 | tf_op jit(solution)/shard_map/ppermute | solution.py:111
  21.1 1.3 %collective-permute-start.11 = (bf16[3,4,3712]{2,1,0:T(4,128)(2,1)S(1)}, bf16[3,4,3712]{2,1,0:T(4,128)(2,1)S(1)}, u32[]{:S(2)}, u32[]{:S(2)}) collective-permute-start(bf16[3,4,3712]{2,1,0:T(4,128)(2,1)S(1)} %collective-permute-done.5), channel_id=1, source_target_pairs={{0,16},{1,3},{2,18},{3,1},{4,20},{5,7},{6,22},{7,5},{8,24},{9,11},... | collective-permute-start | bytes 267272 | tf_op jit(solution)/shard_map/ppermute | solution.py:111
  23.5 2.1 %collective-permute-done.11.refs_9_ = bf16[3,4,3712]{2,1,0:T(4,128)(2,1)S(1)} collective-permute-done((bf16[3,4,3712]{2,1,0:T(4,128)(2,1)S(1)}, bf16[3,4,3712]{2,1,0:T(4,128)(2,1)S(1)}, u32[]{:S(2)}, u32[]{:S(2)}) %collective-permute-start.11) | collective-permute-done | bytes 89120 | tf_op jit(solution)/shard_map/ppermute | solution.py:111
  28.2 1.1 %copy-done.1 = bf16[1,3584,512]{2,1,0:T(8,128)(2,1)S(1)} copy-done((bf16[1,3584,512]{2,1,0:T(8,128)(2,1)S(1)}, bf16[1,3584,512]{2,1,0:T(8,128)(2,1)}, u32[]{:S(2)}) %copy-start.1) | copy-done | bytes 3670040
  29.3 1.9 %turn.3 = (bf16[512,3584]{1,0:T(8,128)(2,1)S(1)}, bf16[512,3584]{1,0:T(8,128)(2,1)S(1)}) custom-call(bf16[3584,512]{1,0:T(8,128)(2,1)S(1)} %bitcast.6, bf16[3584,512]{1,0:T(8,128)(2,1)S(1)} %bitcast.8), custom_call_target="tpu_custom_call" | custom-call | flops 1000000 | tf_op jit(solution)/shard_map/turn/pallas_call | solution.py:264
  31.5 1.3 %forward.1 = (f32[128,512]{1,0:T(8,128)S(1)}, f32[128,512]{1,0:T(8,128)S(1)}, bf16[512,128]{1,0:T(8,128)(2,1)S(1)}) custom-call(bf16[112,3584]{1,0:T(8,128)(2,1)S(1)} %lay.1.early, bf16[16,3712]{1,0:T(8,128)(2,1)S(1)} %collective-permute-done.8.refs_6_.refs_0_.refs_5_.refs_10_, bf16[3,4,3584]{2,1,0:T(4,128)(2,1)S(1)} %collective-permute-done.16.refs_1_, ...), custom_call_target="tpu_custom_call" | custom-call | flops 1000000 | tf_op jit(solution)/shard_map/forward/pallas_call | solution.py:433
  32.8 1.9 %backward.1 = (bf16[128,3584]{1,0:T(8,128)(2,1)S(1)}, bf16[64,3584]{1,0:T(8,128)(2,1)S(1)}, bf16[48,3584]{1,0:T(8,128)(2,1)S(1)}, bf16[16,3584]{1,0:T(8,128)(2,1)S(1)}) custom-call(bf16[16,3712]{1,0:T(8,128)(2,1)S(1)} %pad_maximum_fusion.refs_0_, bf16[16,3712]{1,0:T(8,128)(2,1)S(1)} %collective-permute-done.1.refs_1_.refs_8_, ...), custom_call_target="tpu_custom_call" | custom-call | flops 1000000 | tf_op jit(solution)/shard_map/backward/pallas_call | solution.py:319
  35.3 1.3 %collective-permute-done.19.refs_1_ = bf16[16,3584]{1,0:T(8,128)(2,1)S(1)} collective-permute-done((bf16[16,3584]{1,0:T(8,128)(2,1)S(1)}, bf16[16,3584]{1,0:T(8,128)(2,1)S(1)}, u32[]{:S(2)}, u32[]{:S(2)}) %collective-permute-start.19) | collective-permute-done | bytes 114720 | tf_op jit(solution)/shard_map/ppermute | solution.py:111
  36.6 1.2 %collective-permute-start.20 = (bf16[16,3584]{1,0:T(8,128)(2,1)S(1)}, bf16[16,3584]{1,0:T(8,128)(2,1)S(1)}, u32[]{:S(2)}, u32[]{:S(2)}) collective-permute-start(bf16[16,3584]{1,0:T(8,128)(2,1)S(1)} %add.55), channel_id=1, source_target_pairs={{0,16},{1,3},{2,18},{3,1},{4,20},{5,7},{6,22},{7,5},{8,24},{9,11},... | collective-permute-start | bytes 344072 | tf_op jit(solution)/shard_map/ppermute | solution.py:111
  38.8 2.7 %collective-permute-done.20.refs_2_ = bf16[16,3584]{1,0:T(8,128)(2,1)S(1)} collective-permute-done((bf16[16,3584]{1,0:T(8,128)(2,1)S(1)}, bf16[16,3584]{1,0:T(8,128)(2,1)S(1)}, u32[]{:S(2)}, u32[]{:S(2)}) %collective-permute-start.20) | collective-permute-done | bytes 114720 | tf_op jit(solution)/shard_map/ppermute | solution.py:111
  42.7 3.6 %collective-permute-done.21 = bf16[16,3584]{1,0:T(8,128)(2,1)S(1)} collective-permute-done((bf16[16,3584]{1,0:T(8,128)(2,1)S(1)}, bf16[16,3584]{1,0:T(8,128)(2,1)S(1)}, u32[]{:S(2)}, u32[]{:S(2)}) %collective-permute-start.21) | collective-permute-done | bytes 114720 | tf_op jit(solution)/shard_map/ppermute | solution.py:111
  46.5 2.4 %collective-permute-start.22 = (bf16[4,3584]{1,0:T(4,128)(2,1)S(1)}, bf16[4,3584]{1,0:T(4,128)(2,1)S(1)}, u32[]{:S(2)}, u32[]{:S(2)}) collective-permute-start(bf16[4,3584]{1,0:T(4,128)(2,1)S(1)} %get-tuple-element.28), channel_id=1, source_target_pairs={{0,12},{1,13},{2,14},{3,15},{4,8},{5,9},{6,10},{7,11},{8,4},{9,5},... | collective-permute-start | bytes 86024 | tf_op jit(solution)/shard_map/ppermute | solution.py:111
  48.9 2.0 %collective-permute-start.23 = (bf16[4,3584]{1,0:T(4,128)(2,1)S(1)}, bf16[4,3584]{1,0:T(4,128)(2,1)S(1)}, u32[]{:S(2)}, u32[]{:S(2)}) collective-permute-start(bf16[4,3584]{1,0:T(4,128)(2,1)S(1)} %get-tuple-element.30), channel_id=1, source_target_pairs={{0,4},{1,5},{2,6},{3,7},{4,0},{5,1},{6,2},{7,3},{8,12},{9,13},{10,... | collective-permute-start | bytes 86024 | tf_op jit(solution)/shard_map/ppermute | solution.py:111
  50.9 1.5 %outer.3.refs_0_ = f32[512,3584]{1,0:T(8,128)} custom-call(bf16[512,128]{1,0:T(8,128)(2,1)S(1)} %get-tuple-element.24.hidden_t, bf16[128,3584]{1,0:T(8,128)(2,1)S(1)} %get-tuple-element.25.scaled), custom_call_target="tpu_custom_call" | custom-call | flops 1000000 | tf_op jit(solution)/shard_map/outer/pallas_call | solution.py:354
  52.5 1.5 %outer.4.refs_0_ = f32[512,3584]{1,0:T(8,128)} custom-call(bf16[512,128]{1,0:T(8,128)(2,1)S(1)} %get-tuple-element.24.hidden_t, bf16[128,3584]{1,0:T(8,128)(2,1)S(1)} %get-tuple-element.25.scaled, f32[512,3584]{1,0:T(8,128)} %outer.3.refs_0_), custom_call_target="tpu_custom_call", output_to_operand_aliasing={{}: (2, {})} | custom-call | flops 1000000 | tf_op jit(solution)/shard_map/outer/pallas_call | solution.py:354
  54.0 2.1 %outer.5 = f32[512,3584]{1,0:T(8,128)} custom-call(bf16[512,128]{1,0:T(8,128)(2,1)S(1)} %get-tuple-element.24.hidden_t, bf16[128,3584]{1,0:T(8,128)(2,1)S(1)} %get-tuple-element.25.scaled, f32[512,3584]{1,0:T(8,128)} %outer.4.refs_0_), custom_call_target="tpu_custom_call", output_to_operand_aliasing={{}: (2, {})} | custom-call | flops 1000000 | tf_op jit(solution)/shard_map/outer/pallas_call | solution.py:354
  (53 shorter events, 10.7 us)
Async XLA Ops:
  1.7 7.5 %collective-permute-start = (bf16[8,3712]{1,0:T(8,128)(2,1)S(1)}, bf16[8,3712]{1,0:T(8,128)(2,1)S(1)}, u32[]{:S(2)}, u32[]{:S(2)}) collective-permute-start(bf16[8,3712]{1,0:T(8,128)(2,1)S(1)} %pack.1), channel_id=1, source_target_pairs={{0,2},{1,17},{2,0},{3,19},{4,6},{5,21},{6,4},{7,23},{8,10},{9,25},... | collective-permute-start | bytes 178184 | tf_op jit(solution)/shard_map/ppermute | solution.py:111
  4.8 6.6 %collective-permute-start.4 = (bf16[8,3712]{1,0:T(8,128)(2,1)S(1)}, bf16[8,3712]{1,0:T(8,128)(2,1)S(1)}, u32[]{:S(2)}, u32[]{:S(2)}) collective-permute-start(bf16[8,3712]{1,0:T(8,128)(2,1)S(1)} %pack.1), channel_id=1, source_target_pairs={{0,12},{1,13},{2,14},{3,15},{4,8},{5,9},{6,10},{7,11},{8,4},{9,5},... | collective-permute-start | bytes 178184 | tf_op jit(solution)/shard_map/ppermute | solution.py:111
  8.4 5.1 %collective-permute-start.3 = (bf16[8,3712]{1,0:T(8,128)(2,1)S(1)}, bf16[8,3712]{1,0:T(8,128)(2,1)S(1)}, u32[]{:S(2)}, u32[]{:S(2)}) collective-permute-start(bf16[8,3712]{1,0:T(8,128)(2,1)S(1)} %pack.1), channel_id=1, source_target_pairs={{0,8},{1,9},{2,10},{3,11},{4,12},{5,13},{6,14},{7,15},{8,0},{9,1},... | collective-permute-start | bytes 178184 | tf_op jit(solution)/shard_map/ppermute | solution.py:111
  8.4 5.1 %collective-permute-start.2 = (bf16[8,3712]{1,0:T(8,128)(2,1)S(1)}, bf16[8,3712]{1,0:T(8,128)(2,1)S(1)}, u32[]{:S(2)}, u32[]{:S(2)}) collective-permute-start(bf16[8,3712]{1,0:T(8,128)(2,1)S(1)} %pack.1), channel_id=1, source_target_pairs={{0,4},{1,5},{2,6},{3,7},{4,0},{5,1},{6,2},{7,3},{8,12},{9,13},{10,... | collective-permute-start | bytes 178184 | tf_op jit(solution)/shard_map/ppermute | solution.py:111
  9.2 11.9 %collective-permute-start.7 = (bf16[16,3712]{1,0:T(8,128)(2,1)S(1)}, bf16[16,3712]{1,0:T(8,128)(2,1)S(1)}, u32[]{:S(2)}, u32[]{:S(2)}) collective-permute-start(bf16[16,3712]{1,0:T(8,128)(2,1)S(1)} %pad_maximum_fusion.refs_0_), channel_id=1, source_target_pairs={{0,1},{1,0},{2,3},{3,2},{4,5},{5,4},{6,7},{7,6},{8,9},{9,8},{10,11... | collective-permute-start | bytes 356360 | tf_op jit(solution)/shard_map/ppermute | solution.py:111
  9.3 13.0 %collective-permute-start.1 = (bf16[16,3712]{1,0:T(8,128)(2,1)S(1)}, bf16[16,3712]{1,0:T(8,128)(2,1)S(1)}, u32[]{:S(2)}, u32[]{:S(2)}) collective-permute-start(bf16[16,3712]{1,0:T(8,128)(2,1)S(1)} %pad_maximum_fusion.refs_0_), channel_id=1, source_target_pairs={{0,16},{1,3},{2,18},{3,1},{4,20},{5,7},{6,22},{7,5},{8,24},{9,11},... | collective-permute-start | bytes 356360 | tf_op jit(solution)/shard_map/ppermute | solution.py:111
  13.6 5.5 %collective-permute-start.13 = (bf16[3,4,3584]{2,1,0:T(4,128)(2,1)S(1)}, bf16[3,4,3584]{2,1,0:T(4,128)(2,1)S(1)}, u32[]{:S(2)}, u32[]{:S(2)}) collective-permute-start(bf16[3,4,3584]{2,1,0:T(4,128)(2,1)S(1)} %get-tuple-element.18), channel_id=1, source_target_pairs={{0,2},{1,17},{2,0},{3,19},{4,6},{5,21},{6,4},{7,23},{8,10},{9,25},... | collective-permute-start | bytes 258056 | tf_op jit(solution)/shard_map/ppermute | solution.py:111
  14.7 6.2 %collective-permute-start.5 = (bf16[3,4,3712]{2,1,0:T(4,128)(2,1)S(1)}, bf16[3,4,3712]{2,1,0:T(4,128)(2,1)S(1)}, u32[]{:S(2)}, u32[]{:S(2)}) collective-permute-start(bf16[3,4,3712]{2,1,0:T(4,128)(2,1)S(1)} %get-tuple-element.14), channel_id=1, source_target_pairs={{0,2},{1,17},{2,0},{3,19},{4,6},{5,21},{6,4},{7,23},{8,10},{9,25},... | collective-permute-start | bytes 267272 | tf_op jit(solution)/shard_map/ppermute | solution.py:111
  15.8 6.5 %collective-permute-start.6 = (bf16[24,3712]{1,0:T(8,128)(2,1)S(1)}, bf16[24,3712]{1,0:T(8,128)(2,1)S(1)}, u32[]{:S(2)}, u32[]{:S(2)}) collective-permute-start(bf16[24,3712]{1,0:T(8,128)(2,1)S(1)} %get-tuple-element.15), channel_id=1, source_target_pairs={{0,16},{1,3},{2,18},{3,1},{4,20},{5,7},{6,22},{7,5},{8,24},{9,11},... | collective-permute-start | bytes 534536 | tf_op jit(solution)/shard_map/ppermute | solution.py:111
  19.0 4.5 %collective-permute-start.14 = (bf16[3,4,3584]{2,1,0:T(4,128)(2,1)S(1)}, bf16[3,4,3584]{2,1,0:T(4,128)(2,1)S(1)}, u32[]{:S(2)}, u32[]{:S(2)}) collective-permute-start(bf16[3,4,3584]{2,1,0:T(4,128)(2,1)S(1)} %collective-permute-done.13), channel_id=1, source_target_pairs={{0,16},{1,3},{2,18},{3,1},{4,20},{5,7},{6,22},{7,5},{8,24},{9,11},... | collective-permute-start | bytes 258056 | tf_op jit(solution)/shard_map/ppermute | solution.py:111
  21.0 11.8 %collective-permute-start.9 = (bf16[6,4,3712]{2,1,0:T(4,128)(2,1)S(1)}, bf16[6,4,3712]{2,1,0:T(4,128)(2,1)S(1)}, u32[]{:S(2)}, u32[]{:S(2)}) collective-permute-start(bf16[6,4,3712]{2,1,0:T(4,128)(2,1)S(1)} %constant_dynamic-update-slice_fusion.refs_2_), channel_id=1, source_target_pairs={{0,1},{1,0},{2,3},{3,2},{4,5},{5,4},{6,7},{7,6},{8,9},{9,8},{10,11... | collective-permute-start | bytes 534536 | tf_op jit(solution)/shard_map/ppermute | solution.py:111
  21.1 4.6 %collective-permute-start.11 = (bf16[3,4,3712]{2,1,0:T(4,128)(2,1)S(1)}, bf16[3,4,3712]{2,1,0:T(4,128)(2,1)S(1)}, u32[]{:S(2)}, u32[]{:S(2)}) collective-permute-start(bf16[3,4,3712]{2,1,0:T(4,128)(2,1)S(1)} %collective-permute-done.5), channel_id=1, source_target_pairs={{0,16},{1,3},{2,18},{3,1},{4,20},{5,7},{6,22},{7,5},{8,24},{9,11},... | collective-permute-start | bytes 267272 | tf_op jit(solution)/shard_map/ppermute | solution.py:111
  22.3 3.3 %collective-permute-start.8 = (bf16[16,3712]{1,0:T(8,128)(2,1)S(1)}, bf16[16,3712]{1,0:T(8,128)(2,1)S(1)}, u32[]{:S(2)}, u32[]{:S(2)}) collective-permute-start(bf16[16,3712]{1,0:T(8,128)(2,1)S(1)} %collective-permute-done.1.refs_1_.refs_8_), channel_id=1, source_target_pairs={{0,1},{1,0},{2,3},{3,2},{4,5},{5,4},{6,7},{7,6},{8,9},{9,8},{10,11... | collective-permute-start | bytes 356360 | tf_op jit(solution)/shard_map/ppermute | solution.py:111
  22.3 8.9 %collective-permute-start.10 = (bf16[24,3712]{1,0:T(8,128)(2,1)S(1)}, bf16[24,3712]{1,0:T(8,128)(2,1)S(1)}, u32[]{:S(2)}, u32[]{:S(2)}) collective-permute-start(bf16[24,3712]{1,0:T(8,128)(2,1)S(1)} %collective-permute-done.6.refs_3_), channel_id=1, source_target_pairs={{0,1},{1,0},{2,3},{3,2},{4,5},{5,4},{6,7},{7,6},{8,9},{9,8},{10,11... | collective-permute-start | bytes 534536 | tf_op jit(solution)/shard_map/ppermute | solution.py:111
  23.5 7.8 %collective-permute-start.15 = (bf16[6,4,3584]{2,1,0:T(4,128)(2,1)S(1)}, bf16[6,4,3584]{2,1,0:T(4,128)(2,1)S(1)}, u32[]{:S(2)}, u32[]{:S(2)}) collective-permute-start(bf16[6,4,3584]{2,1,0:T(4,128)(2,1)S(1)} %constant_dynamic-update-slice_fusion.2.refs_2_), channel_id=1, source_target_pairs={{0,1},{1,0},{2,3},{3,2},{4,5},{5,4},{6,7},{7,6},{8,9},{9,8},{10,11... | collective-permute-start | bytes 516104 | tf_op jit(solution)/shard_map/ppermute | solution.py:111
  25.6 7.1 %collective-permute-start.12 = (bf16[3,4,3712]{2,1,0:T(4,128)(2,1)S(1)}, bf16[3,4,3712]{2,1,0:T(4,128)(2,1)S(1)}, u32[]{:S(2)}, u32[]{:S(2)}) collective-permute-start(bf16[3,4,3712]{2,1,0:T(4,128)(2,1)S(1)} %collective-permute-done.11.refs_9_), channel_id=1, source_target_pairs={{0,1},{1,0},{2,3},{3,2},{4,5},{5,4},{6,7},{7,6},{8,9},{9,8},{10,11... | collective-permute-start | bytes 267272 | tf_op jit(solution)/shard_map/ppermute | solution.py:111
  25.7 5.8 %collective-permute-start.16 = (bf16[3,4,3584]{2,1,0:T(4,128)(2,1)S(1)}, bf16[3,4,3584]{2,1,0:T(4,128)(2,1)S(1)}, u32[]{:S(2)}, u32[]{:S(2)}) collective-permute-start(bf16[3,4,3584]{2,1,0:T(4,128)(2,1)S(1)} %collective-permute-done.14.refs_4_), channel_id=1, source_target_pairs={{0,1},{1,0},{2,3},{3,2},{4,5},{5,4},{6,7},{7,6},{8,9},{9,8},{10,11... | collective-permute-start | bytes 258056 | tf_op jit(solution)/shard_map/ppermute | solution.py:111
  34.7 3.2 %collective-permute-start.17 = (bf16[48,3584]{1,0:T(8,128)(2,1)S(1)}, bf16[48,3584]{1,0:T(8,128)(2,1)S(1)}, u32[]{:S(2)}, u32[]{:S(2)}) collective-permute-start(bf16[48,3584]{1,0:T(8,128)(2,1)S(1)} %get-tuple-element.22), channel_id=1, source_target_pairs={{0,1},{1,0},{2,3},{3,2},{4,5},{5,4},{6,7},{7,6},{8,9},{9,8},{10,11... | collective-permute-start | bytes 1032200 | tf_op jit(solution)/shard_map/ppermute | solution.py:111
  36.6 4.9 %collective-permute-start.20 = (bf16[16,3584]{1,0:T(8,128)(2,1)S(1)}, bf16[16,3584]{1,0:T(8,128)(2,1)S(1)}, u32[]{:S(2)}, u32[]{:S(2)}) collective-permute-start(bf16[16,3584]{1,0:T(8,128)(2,1)S(1)} %add.55), channel_id=1, source_target_pairs={{0,16},{1,3},{2,18},{3,1},{4,20},{5,7},{6,22},{7,5},{8,24},{9,11},... | collective-permute-start | bytes 344072 | tf_op jit(solution)/shard_map/ppermute | solution.py:111
  37.9 4.9 %collective-permute-start.18 = (bf16[16,3584]{1,0:T(8,128)(2,1)S(1)}, bf16[16,3584]{1,0:T(8,128)(2,1)S(1)}, u32[]{:S(2)}, u32[]{:S(2)}) collective-permute-start(bf16[16,3584]{1,0:T(8,128)(2,1)S(1)} %add.54), channel_id=1, source_target_pairs={{0,16},{1,3},{2,18},{3,1},{4,20},{5,7},{6,22},{7,5},{8,24},{9,11},... | collective-permute-start | bytes 344072 | tf_op jit(solution)/shard_map/ppermute | solution.py:111
  41.5 4.9 %collective-permute-start.21 = (bf16[16,3584]{1,0:T(8,128)(2,1)S(1)}, bf16[16,3584]{1,0:T(8,128)(2,1)S(1)}, u32[]{:S(2)}, u32[]{:S(2)}) collective-permute-start(bf16[16,3584]{1,0:T(8,128)(2,1)S(1)} %add.56), channel_id=1, source_target_pairs={{0,2},{1,17},{2,0},{3,19},{4,6},{5,21},{6,4},{7,23},{8,10},{9,25},... | collective-permute-start | bytes 344072 | tf_op jit(solution)/shard_map/ppermute | solution.py:111
  46.5 9.7 %collective-permute-start.22 = (bf16[4,3584]{1,0:T(4,128)(2,1)S(1)}, bf16[4,3584]{1,0:T(4,128)(2,1)S(1)}, u32[]{:S(2)}, u32[]{:S(2)}) collective-permute-start(bf16[4,3584]{1,0:T(4,128)(2,1)S(1)} %get-tuple-element.28), channel_id=1, source_target_pairs={{0,12},{1,13},{2,14},{3,15},{4,8},{5,9},{6,10},{7,11},{8,4},{9,5},... | collective-permute-start | bytes 86024 | tf_op jit(solution)/shard_map/ppermute | solution.py:111
  48.9 7.2 %collective-permute-start.24 = (bf16[4,3584]{1,0:T(4,128)(2,1)S(1)}, bf16[4,3584]{1,0:T(4,128)(2,1)S(1)}, u32[]{:S(2)}, u32[]{:S(2)}) collective-permute-start(bf16[4,3584]{1,0:T(4,128)(2,1)S(1)} %get-tuple-element.29), channel_id=1, source_target_pairs={{0,8},{1,9},{2,10},{3,11},{4,12},{5,13},{6,14},{7,15},{8,0},{9,1},... | collective-permute-start | bytes 86024 | tf_op jit(solution)/shard_map/ppermute | solution.py:111
  48.9 7.2 %collective-permute-start.23 = (bf16[4,3584]{1,0:T(4,128)(2,1)S(1)}, bf16[4,3584]{1,0:T(4,128)(2,1)S(1)}, u32[]{:S(2)}, u32[]{:S(2)}) collective-permute-start(bf16[4,3584]{1,0:T(4,128)(2,1)S(1)} %get-tuple-element.30), channel_id=1, source_target_pairs={{0,4},{1,5},{2,6},{3,7},{4,0},{5,1},{6,2},{7,3},{8,12},{9,13},{10,... | collective-permute-start | bytes 86024 | tf_op jit(solution)/shard_map/ppermute | solution.py:111
  (4 other events, 32.5 us)
